TPU v7x, 32 devices: a whole 2x2x4 slice. The times are simulated.
32 devices in a mesh: fsdp: 4 (over z), ctx: 4 (over y, x), tp: 2 (over core).
Axes of the slice: x: 2, y: 2, z: 4, core: 2. Of those that a mesh axis runs over, the one named last changes fastest.
Arguments:
- tokens: bfloat16 [2, 4, 4, 256, 1024], P(None, None, 'ctx', 'fsdp'), may hold values from -6 to 6
- cotangent: bfloat16 [2, 4, 4, 256, 1024], P(None, None, 'ctx', 'fsdp'), may hold values from -6 to 6
- lengths: int32 [2, 4], replicated, may hold values from 256 to 1024, as said below
- owners: int32 [2, 4], replicated, may hold values from 0 to 3, each once within a row
- norm_attn: bfloat16 [1024], P(('fsdp', 'ctx')), may hold values from 0.099609375 to 1.8984375
- norm_mlp: bfloat16 [1024], P(('fsdp', 'ctx')), may hold values from 0.099609375 to 1.8984375
- w_qkv: bfloat16 [1024, 3, 1024], P(('fsdp', 'ctx'), None, 'tp'), may hold values from -0.1875 to 0.1875
- w_out: bfloat16 [1024, 1024], P('tp', ('fsdp', 'ctx')), may hold values from -3 to 3
- w_in: bfloat16 [1024, 2, 2624], P(('fsdp', 'ctx'), None, 'tp'), may hold values from -0.1875 to 0.1875
- w_down: bfloat16 [2624, 1024], P('tp', ('fsdp', 'ctx')), may hold values from -0.15625 to 0.15625
Outputs:
- output: bfloat16 [2, 4, 4, 256, 1024], P(None, None, 'ctx', 'fsdp')
- grad_tokens: bfloat16 [2, 4, 4, 256, 1024], P(None, None, 'ctx', 'fsdp')
- grad_norm_attn: float32 [1024], P(('fsdp', 'ctx'))
- grad_norm_mlp: float32 [1024], P(('fsdp', 'ctx'))
- grad_w_qkv: float32 [1024, 3, 1024], P(('fsdp', 'ctx'), None, 'tp')
- grad_w_out: float32 [1024, 1024], P('tp', ('fsdp', 'ctx'))
- grad_w_in: float32 [1024, 2, 2624], P(('fsdp', 'ctx'), None, 'tp')
- grad_w_down: float32 [2624, 1024], P('tp', ('fsdp', 'ctx'))
Inputs may be any that keep to these rules, and one draw needn't show every extreme that they name: Each row of owners names every owner slot once; sequence s of micro-batch m belongs to slot owners[m, s], and slot j is worked on by index j of fsdp. lengths[m, j] counts the live positions of the sequence in owner slot j; every micro-batch has one sequence of exactly 1024 and one of exactly 256 positions.
All inputs are finite; a program needn't handle non-finite values.
Results may differ from a plain program's by a relative error of at most 0.023.
Values may be sent and summed in bfloat16 or wider, within the bound.
A program may use at most 192 MiB of HBM per device.

v0:
```python
import jax
import jax.numpy as jnp
from jax import lax
from jax.sharding import PartitionSpec as P

D = 1024
HEAD_DIM = 64


norm_eps = 1e-05
rope_base = 160000.0
masked_score = -1e30


def layer_norm(values, norm_gain):
    center = values - jnp.mean(values, axis=-1, keepdims=True)
    spread = jnp.mean(center * center, axis=-1, keepdims=True)
    inverse_std = lax.rsqrt(spread + norm_eps)
    normed = center * inverse_std
    return (normed * norm_gain, normed, inverse_std)


def norm_backward(upstream, normed, inverse_std, norm_gain):
    scaled = upstream * norm_gain
    adjusted = (
        scaled
        - jnp.mean(scaled, axis=-1, keepdims=True)
        - normed * jnp.mean(scaled * normed, axis=-1, keepdims=True)
    )
    return (adjusted * inverse_std, jnp.sum(upstream * normed, axis=0))


def rope_tables(positions):
    inverse = rope_base ** (-jnp.arange(0, HEAD_DIM, 2).astype(jnp.float32) / HEAD_DIM)
    angles = positions.astype(jnp.float32)[:, None] * inverse[None, :]
    return (jnp.cos(angles)[:, None, :], jnp.sin(angles)[:, None, :])


def rotary(values, cosine_table, sine_table):
    half_dim = values.shape[-1] // 2
    first_half = values[..., :half_dim]
    second_half = values[..., half_dim:]
    return jnp.concatenate(
        [
            first_half * cosine_table - second_half * sine_table,
            second_half * cosine_table + first_half * sine_table,
        ],
        axis=-1,
    )


def block_size(row_count):
    block_rows = row_count
    while block_rows > 512 and block_rows % 2 == 0:
        block_rows = block_rows // 2
    return block_rows


def make_forward(queries, live_count):

    def fold_keys(running, shard_piece, first_row):
        key_piece, value_piece = shard_piece
        block_rows = block_size(key_piece.shape[0])

        def one_block(block_index, inner_state):
            row_max, row_total, weighted = inner_state
            offset = block_index * block_rows
            key_block = lax.dynamic_slice_in_dim(key_piece, offset, block_rows, 0).reshape(
                block_rows, -1, HEAD_DIM
            )
            value_block = lax.dynamic_slice_in_dim(value_piece, offset, block_rows, 0).reshape(
                block_rows, -1, HEAD_DIM
            )
            live_keys = (offset + jnp.arange(block_rows, dtype=jnp.int32) < live_count)[
                None, None, :
            ]
            scores = jnp.einsum(
                "qhd,khd->hqk", queries, key_block, preferred_element_type=jnp.float32
            ) * HEAD_DIM ** (-0.5)
            scores = jnp.where(live_keys, scores, masked_score)
            new_max = jnp.maximum(row_max, jnp.max(scores, axis=-1))
            rescale = jnp.exp(row_max - new_max)
            attn_probs = jnp.where(live_keys, jnp.exp(scores - new_max[..., None]), 0.0)
            row_total = row_total * rescale + jnp.sum(attn_probs, axis=-1)
            weighted = weighted * rescale[..., None] + jnp.einsum(
                "hqk,khd->hqd",
                attn_probs.astype(jnp.bfloat16),
                value_block,
                preferred_element_type=jnp.float32,
            )
            return (new_max, row_total, weighted)

        return lax.fori_loop(0, key_piece.shape[0] // block_rows, one_block, running)

    return fold_keys


def make_backward(queries, out_grad, log_total, row_delta, live_count):

    def fold_back(running, shard_piece, first_row):
        key_piece, value_piece = shard_piece
        block_rows = block_size(key_piece.shape[0])

        def one_block(block_index, inner_state):
            query_grad, key_grad, value_grad = inner_state
            offset = block_index * block_rows
            key_block = lax.dynamic_slice_in_dim(key_piece, offset, block_rows, 0).reshape(
                block_rows, -1, HEAD_DIM
            )
            value_block = lax.dynamic_slice_in_dim(value_piece, offset, block_rows, 0).reshape(
                block_rows, -1, HEAD_DIM
            )
            live_keys = (offset + jnp.arange(block_rows, dtype=jnp.int32) < live_count)[
                None, None, :
            ]
            scores = jnp.einsum(
                "qhd,khd->hqk", queries, key_block, preferred_element_type=jnp.float32
            ) * HEAD_DIM ** (-0.5)
            attn_probs = jnp.where(live_keys, jnp.exp(scores - log_total[..., None]), 0.0)
            prob_grad = jnp.einsum(
                "qhd,khd->hqk", out_grad, value_block, preferred_element_type=jnp.float32
            )
            score_grad = (attn_probs * (prob_grad - row_delta[..., None])).astype(jnp.bfloat16)
            query_grad = query_grad + jnp.einsum(
                "hqk,khd->qhd", score_grad, key_block, preferred_element_type=jnp.float32
            )
            key_part = jnp.einsum(
                "hqk,qhd->khd", score_grad, queries, preferred_element_type=jnp.float32
            ).reshape(block_rows, -1)
            value_part = jnp.einsum(
                "hqk,qhd->khd",
                attn_probs.astype(jnp.bfloat16),
                out_grad,
                preferred_element_type=jnp.float32,
            ).reshape(block_rows, -1)
            key_grad = lax.dynamic_update_slice_in_dim(
                key_grad,
                lax.dynamic_slice_in_dim(key_grad, offset, block_rows, 0) + key_part,
                offset,
                0,
            )
            value_grad = lax.dynamic_update_slice_in_dim(
                value_grad,
                lax.dynamic_slice_in_dim(value_grad, offset, block_rows, 0) + value_part,
                offset,
                0,
            )
            return (query_grad, key_grad, value_grad)

        return lax.fori_loop(0, key_piece.shape[0] // block_rows, one_block, running)

    return fold_back


def per_device(tokens, cotangent, lengths, owners, norm_attn, norm_mlp, w_qkv, w_out, w_in, w_down):
    gathered = (
        lax.all_gather(norm_attn, ("fsdp", "ctx"), axis=0, tiled=True),
        lax.all_gather(norm_mlp, ("fsdp", "ctx"), axis=0, tiled=True),
        lax.all_gather(w_qkv, ("fsdp", "ctx"), axis=0, tiled=True),
        lax.all_gather(w_out, ("fsdp", "ctx"), axis=1, tiled=True),
        lax.all_gather(w_in, ("fsdp", "ctx"), axis=0, tiled=True),
        lax.all_gather(w_down, ("fsdp", "ctx"), axis=1, tiled=True),
    )
    gain_attn = gathered[0].astype(jnp.float32)
    gain_mlp = gathered[1].astype(jnp.float32)
    qkv_weight = gathered[2].reshape(D, -1)
    local_width = qkv_weight.shape[1] // 3
    local_heads = local_width // HEAD_DIM
    out_weight = gathered[3]
    in_weight = gathered[4].reshape(D, -1)
    local_hidden = in_weight.shape[1] // 2
    down_weight = gathered[5]
    inverse_order = jnp.argsort(owners, axis=1)
    micro_index = jnp.arange(tokens.shape[0], dtype=jnp.int32)[:, None]
    sent_tokens = tokens[micro_index, inverse_order]
    sent_cot = cotangent[micro_index, inverse_order]
    own_tokens, own_cot = (
        lax.all_to_all(sent_tokens, "fsdp", split_axis=1, concat_axis=3, tiled=True),
        lax.all_to_all(sent_cot, "fsdp", split_axis=1, concat_axis=3, tiled=True),
    )
    own_slot = lax.axis_index("fsdp")
    piece_index = lax.axis_index("ctx")
    span_rows = own_tokens.shape[3]
    slot_rows = span_rows * lax.axis_size("ctx")
    live_counts = lax.dynamic_index_in_dim(lengths, own_slot, axis=1, keepdims=False)
    positions = piece_index * span_rows + jnp.arange(span_rows, dtype=jnp.int32)
    cosine_table, sine_table = rope_tables(positions)
    score_scale = HEAD_DIM ** (-0.5)
    grad_totals = None
    outputs = []
    input_grads = []
    for micro_step in range(own_tokens.shape[0]):
        token_rows = own_tokens[micro_step, 0, 0].astype(jnp.float32)
        upstream = own_cot[micro_step, 0, 0].astype(jnp.float32)
        live_count = live_counts[micro_step]
        first_normed, first_hat, first_std = layer_norm(token_rows, gain_attn)
        first_low = first_normed.astype(jnp.bfloat16)
        joined_proj = jnp.dot(first_low, qkv_weight, preferred_element_type=jnp.float32).reshape(
            span_rows, 3, local_heads, HEAD_DIM
        )
        queries = rotary(joined_proj[:, 0], cosine_table, sine_table).astype(jnp.bfloat16)
        key_rows = (
            rotary(joined_proj[:, 1], cosine_table, sine_table)
            .astype(jnp.bfloat16)
            .reshape(span_rows, local_width)
        )
        value_rows = joined_proj[:, 2].astype(jnp.bfloat16).reshape(span_rows, local_width)
        start_state = (
            jnp.full((local_heads, span_rows), masked_score, jnp.float32),
            jnp.zeros((local_heads, span_rows), jnp.float32),
            jnp.zeros((local_heads, span_rows, HEAD_DIM), jnp.float32),
        )
        fold_keys = make_forward(queries, live_count)
        row_max, row_total, weighted = fold_keys(
            start_state,
            (
                lax.all_gather(key_rows, "ctx", axis=0, tiled=True),
                lax.all_gather(value_rows, "ctx", axis=0, tiled=True),
            ),
            jnp.int32(0),
        )
        attn_out = weighted / row_total[..., None]
        log_total = row_max + jnp.log(row_total)
        mixed_low = attn_out.transpose(1, 0, 2).reshape(span_rows, local_width).astype(jnp.bfloat16)
        attn_part = jnp.dot(mixed_low, out_weight, preferred_element_type=jnp.float32)
        attended = lax.psum(attn_part.astype(jnp.bfloat16), "tp").astype(jnp.float32)
        hidden_in = token_rows + attended
        second_normed, second_hat, second_std = layer_norm(hidden_in, gain_mlp)
        second_low = second_normed.astype(jnp.bfloat16)
        gate_up = jnp.dot(second_low, in_weight, preferred_element_type=jnp.float32)
        gate_in = gate_up[:, :local_hidden]
        gate_mul = gate_up[:, local_hidden:]
        gelu_values, gelu_back = jax.vjp(
            lambda pre_act: jax.nn.gelu(pre_act, approximate=False), gate_in
        )
        activated = (gelu_values * gate_mul).astype(jnp.bfloat16)
        mlp_part = jnp.dot(activated, down_weight, preferred_element_type=jnp.float32)
        mlp_out = lax.psum(mlp_part.astype(jnp.bfloat16), "tp").astype(jnp.float32)
        outputs.append((hidden_in + mlp_out).astype(jnp.bfloat16))
        branch_low = upstream.astype(jnp.bfloat16)
        grad_down = jnp.einsum(
            "tf,td->fd", activated, branch_low, preferred_element_type=jnp.float32
        )
        act_grad = jnp.einsum(
            "td,fd->tf", branch_low, down_weight, preferred_element_type=jnp.float32
        )
        gate_in_grad = gelu_back(act_grad * gate_mul)[0]
        gate_mul_grad = act_grad * gelu_values
        gate_grad = jnp.concatenate([gate_in_grad, gate_mul_grad], axis=1).astype(jnp.bfloat16)
        grad_in = jnp.einsum("td,tf->df", second_low, gate_grad, preferred_element_type=jnp.float32)
        second_part = jnp.einsum(
            "tf,df->td", gate_grad, in_weight, preferred_element_type=jnp.float32
        )
        second_grad = lax.psum(second_part.astype(jnp.bfloat16), "tp").astype(jnp.float32)
        hidden_part, grad_gain_mlp = norm_backward(second_grad, second_hat, second_std, gain_mlp)
        hidden_grad = upstream + hidden_part
        attn_low = hidden_grad.astype(jnp.bfloat16)
        grad_out = jnp.einsum("tc,td->cd", mixed_low, attn_low, preferred_element_type=jnp.float32)
        mixed_grad = (
            jnp.einsum("td,cd->tc", attn_low, out_weight, preferred_element_type=jnp.float32)
            .astype(jnp.bfloat16)
            .reshape(span_rows, local_heads, HEAD_DIM)
        )
        row_delta = jnp.sum(mixed_grad.astype(jnp.float32).transpose(1, 0, 2) * attn_out, axis=-1)
        fold_back = make_backward(queries, mixed_grad, log_total, row_delta, live_count)
        back_state = (
            jnp.zeros((span_rows, local_heads, HEAD_DIM), jnp.float32),
            jnp.zeros((slot_rows, local_width), jnp.float32),
            jnp.zeros((slot_rows, local_width), jnp.float32),
        )
        query_grad, key_grad_all, value_grad_all = fold_back(
            back_state,
            (
                lax.all_gather(key_rows, "ctx", axis=0, tiled=True),
                lax.all_gather(value_rows, "ctx", axis=0, tiled=True),
            ),
            jnp.int32(0),
        )
        key_grad, value_grad = (
            lax.psum_scatter(
                key_grad_all.astype(jnp.bfloat16), "ctx", scatter_dimension=0, tiled=True
            ).astype(jnp.float32),
            lax.psum_scatter(
                value_grad_all.astype(jnp.bfloat16), "ctx", scatter_dimension=0, tiled=True
            ).astype(jnp.float32),
        )
        query_pre = rotary(query_grad * score_scale, cosine_table, -sine_table)
        key_pre = rotary(
            key_grad.reshape(span_rows, local_heads, HEAD_DIM) * score_scale,
            cosine_table,
            -sine_table,
        )
        joined_grad = (
            jnp.stack(
                [query_pre, key_pre, value_grad.reshape(span_rows, local_heads, HEAD_DIM)], axis=1
            )
            .reshape(span_rows, 3 * local_width)
            .astype(jnp.bfloat16)
        )
        grad_qkv = jnp.einsum(
            "td,tc->dc", first_low, joined_grad, preferred_element_type=jnp.float32
        )
        first_part = jnp.einsum(
            "tc,dc->td", joined_grad, qkv_weight, preferred_element_type=jnp.float32
        )
        first_grad = lax.psum(first_part.astype(jnp.bfloat16), "tp").astype(jnp.float32)
        token_part, grad_gain_attn = norm_backward(first_grad, first_hat, first_std, gain_attn)
        input_grads.append((hidden_grad + token_part).astype(jnp.bfloat16))
        step_grads = (
            grad_gain_attn,
            grad_gain_mlp,
            grad_qkv.reshape(D, 3, local_width),
            grad_out,
            grad_in.reshape(D, 2, local_hidden),
            grad_down,
        )
        grad_totals = (
            step_grads
            if grad_totals is None
            else tuple(
                (total_part + grad_part for total_part, grad_part in zip(grad_totals, step_grads))
            )
        )
    grad_shares = (
        lax.psum_scatter(grad_totals[0], ("fsdp", "ctx"), scatter_dimension=0, tiled=True),
        lax.psum_scatter(grad_totals[1], ("fsdp", "ctx"), scatter_dimension=0, tiled=True),
        lax.psum_scatter(grad_totals[2], ("fsdp", "ctx"), scatter_dimension=0, tiled=True),
        lax.psum_scatter(grad_totals[3], ("fsdp", "ctx"), scatter_dimension=1, tiled=True),
        lax.psum_scatter(grad_totals[4], ("fsdp", "ctx"), scatter_dimension=0, tiled=True),
        lax.psum_scatter(grad_totals[5], ("fsdp", "ctx"), scatter_dimension=1, tiled=True),
    )
    stacked = jnp.stack(outputs)[:, None, None]
    stacked_grads = jnp.stack(input_grads)[:, None, None]
    back_out, back_grad = (
        lax.all_to_all(stacked, "fsdp", split_axis=3, concat_axis=1, tiled=True),
        lax.all_to_all(stacked_grads, "fsdp", split_axis=3, concat_axis=1, tiled=True),
    )
    output_rows = back_out[micro_index, owners]
    grad_rows = back_grad[micro_index, owners]
    return (
        output_rows,
        grad_rows,
        grad_shares[0],
        grad_shares[1],
        grad_shares[2],
        grad_shares[3],
        grad_shares[4],
        grad_shares[5],
    )


def solution(mesh):
    placed = (
        P(None, None, "ctx", "fsdp", None),
        P(None, None, "ctx", "fsdp", None),
        P(),
        P(),
        P(("fsdp", "ctx")),
        P(("fsdp", "ctx")),
        P(("fsdp", "ctx"), None, "tp"),
        P("tp", ("fsdp", "ctx")),
        P(("fsdp", "ctx"), None, "tp"),
        P("tp", ("fsdp", "ctx")),
    )
    return jax.shard_map(
        per_device,
        mesh=mesh,
        in_specs=placed,
        out_specs=(
            P(None, None, "ctx", "fsdp", None),
            P(None, None, "ctx", "fsdp", None),
            P(("fsdp", "ctx")),
            P(("fsdp", "ctx")),
            P(("fsdp", "ctx"), None, "tp"),
            P("tp", ("fsdp", "ctx")),
            P(("fsdp", "ctx"), None, "tp"),
            P("tp", ("fsdp", "ctx")),
        ),
        check_vma=False,
    )
```

profile of v0, /device:TPU:0, one launch (start us, length us, event | category | flops | bytes accessed | tf_op | source)
XLA Modules:
  0.0 1445.1 jit_solution(17349704940463061459)
XLA Ops:
  11.2 6.4 all-to-all-start
  19.5 53.9 %all-reduce.6 = (bf16[1024]{0:T(1024)(128)(2,1)S(1)}, bf16[1024]{0:T(1024)(128)(2,1)S(1)}) all-reduce(bf16[1024]{0:T(1024)(128)(2,1)S(1)} %dynamic-update-slice, bf16[1024]{0:T(1024)(128)(2,1)S(1)} %dynamic-update-slice.1), channel_id=1, replica_groups=mesh['fsdp'=4,'ctx'=4,'tp'=2] {'fsdp','ctx'}, use_global_device_ids=true, to_apply=%add | all-reduce | flops 2048 | bytes 8192
  75.4 16.5 %all-gather.9.cloned.1.call-done = bf16[1024,3,512]{2,0,1:T(8,128)(2,1)} async-done(((bf16[64,3,512]{2,0,1:T(8,128)(2,1)}), bf16[1024,3,512]{2,0,1:T(8,128)(2,1)}) %all-gather.9.cloned.1.call-update) | async-done | bytes 3145744 | tf_op jit(solution)/shard_map/all_gather | solution.py:159
  91.9 4.7 copy.74
  107.0 20.1 %all-gather.21.cloned.1.call-done = bf16[1024,512]{0,1:T(8,128)(2,1)} async-done(((bf16[256,512]{0,1:T(8,128)(2,1)}), bf16[1024,512]{0,1:T(8,128)(2,1)}) %all-gather.21.cloned.1.call-update) | async-done | bytes 1048592 | tf_op jit(solution)/shard_map/all_gather | solution.py:217
  127.2 28.9 %all-gather.23.cloned.1.call-done = bf16[1024,512]{0,1:T(8,128)(2,1)} async-done(((bf16[256,512]{0,1:T(8,128)(2,1)}), bf16[1024,512]{0,1:T(8,128)(2,1)}) %all-gather.23.cloned.1.call-update) | async-done | bytes 1048592 | tf_op jit(solution)/shard_map/all_gather | solution.py:218
  156.1 21.8 %while.73 = (s32[]{:T(128)}, f32[8,256]{1,0:T(8,128)S(1)}, f32[8,256]{1,0:T(8,128)S(1)}, f32[8,256,64]{1,2,0:T(8,128)}, s32[]{:T(128)}, /*index=5*/bf16[1024,512...) while((s32[]{:T(128)}, f32[8,256]{1,0:T(8,128)S(1)}, ...), condition=%wide.region_16.17_spmd.clone, body=%wide.region_13.16_spmd.clone.sunk | while | flops 282471424 | bytes 33949916 | solution.py:93
  161.0 3.4 fusion.261
  171.4 3.4 fusion.261
  177.9 7.0 all-gather.11.cloned.1.call-done
  184.9 28.8 %all-gather.13.cloned.1.call-done = bf16[1024,512]{0,1:T(8,128)(2,1)} async-done(((bf16[256,512]{0,1:T(8,128)(2,1)}), bf16[1024,512]{0,1:T(8,128)(2,1)}) %all-gather.13.cloned.1.call-update) | async-done | bytes 1048592 | tf_op jit(solution)/shard_map/all_gather | solution.py:218
  213.7 19.2 %while.72 = (s32[]{:T(128)}, f32[8,256]{1,0:T(8,128)S(1)}, f32[8,256]{1,0:T(8,128)S(1)}, f32[8,256,64]{1,2,0:T(8,128)S(1)}, s32[]{:T(128)}, /*index=5*/bf16[1024...) while((s32[]{:T(128)}, f32[8,256]{1,0:T(8,128)S(1)}, ...), condition=%wide.region_6.7_spmd.clone, body=%wide.region_3.6_spmd.clone.sunk | while | flops 282471424 | bytes 33949916 | solution.py:93
  218.6 3.4 fusion.254
  228.2 3.4 fusion.254
  236.0 35.6 %all-gather.15.cloned.1.call-done = bf16[512,1024]{0,1:T(8,128)(2,1)} async-done(((bf16[512,64]{0,1:T(8,128)(2,1)}), bf16[512,1024]{0,1:T(8,128)(2,1)}) %all-gather.15.cloned.1.call-update) | async-done | bytes 1048592 | tf_op jit(solution)/shard_map/all_gather | solution.py:160
  279.9 3.5 all-to-all-start.2
  283.7 24.4 %all-to-all-done.2 = bf16[2,4,1,64,1024]{4,3,2,0,1:T(8,128)(2,1)S(1)} async-done(((bf16[2,4,1,64,1024]{4,3,2,0,1:T(8,128)(2,1)}), bf16[2,4,1,64,1024]{4,3,2,0,1:T(8,128)(2,1)S(1)}, u32[]{:S(2)}, u32[]{:S(2)}) %all-to-all-start.2) | async-done | bytes 1048608 | tf_op jit(solution)/shard_map/all_to_all | solution.py:179
  312.8 75.1 %all-gather.17.cloned.1.call-done = bf16[1024,2,1312]{2,1,0:T(2,128)(2,1)} async-done(((bf16[64,2,1312]{2,1,0:T(2,128)(2,1)}), bf16[1024,2,1312]{2,1,0:T(2,128)(2,1)}) %all-gather.17.cloned.1.call-update) | async-done | bytes 5373968 | tf_op jit(solution)/shard_map/all_gather | solution.py:161
  387.9 14.8 %copy.75 = bf16[1024,2,1312]{0,2,1:T(8,128)(2,1)} copy(bf16[1024,2,1312]{2,1,0:T(2,128)(2,1)} %all-gather.17.cloned.1.call-done) | data formatting | bytes 10747904 | tf_op jit(solution)/shard_map/all_gather | solution.py:161
  402.7 5.8 fusion.125
  411.7 43.7 %all-gather.19.cloned.1.call-done = bf16[1312,1024]{0,1:T(8,128)(2,1)} async-done(((bf16[1312,64]{0,1:T(8,128)(2,1)}), bf16[1312,1024]{0,1:T(8,128)(2,1)}) %all-gather.19.cloned.1.call-update) | async-done | bytes 2686992 | tf_op jit(solution)/shard_map/all_gather | solution.py:162
  455.3 7.8 add_convert_fusion
  464.4 5.3 convolution_convert_fusion.5
  469.7 4.1 add_convert_fusion.1
  478.6 18.8 %all-reduce.19.cloned.1.call-done = (bf16[256,1024]{1,0:T(8,128)(2,1)}, bf16[256,1024]{1,0:T(8,128)(2,1)}) async-done(((bf16[256,1024]{1,0:T(8,128)(2,1)}, bf16[256,1024]{1,0:T(8,128)(2,1)}), (bf16[256,1024]{1,0:T(8,128)(2,1)}, bf16[256,1024]{1,0:T(8,128)(2,1)})) %all-reduce.19.cloned.1.call-update) | async-done | bytes 1048592 | tf_op jit(solution)/shard_map/psum | solution.py:254
  512.8 32.6 %while.74 = (s32[]{:T(128)}, f32[256,8,64]{0,2,1:T(8,128)}, f32[1024,512]{0,1:T(8,128)}, f32[1024,512]{0,1:T(8,128)}, bf16[1024,512]{0,1:T(8,128)(2,1)}, /*index...) while((s32[]{:T(128)}, f32[256,8,64]{0,2,1:T(8,128)}, ...), condition=%wide.region_26.27_spmd.clone, body=%wide.region_25.26_spmd.clone.sunk | while | flops 682361856 | bytes 85485480 | solution.py:150
  520.9 3.2 fusion.276
  551.5 29.9 %while.75 = (s32[]{:T(128)}, f32[256,8,64]{0,2,1:T(8,128)}, f32[1024,512]{0,1:T(8,128)}, f32[1024,512]{0,1:T(8,128)}, bf16[1024,512]{0,1:T(8,128)(2,1)}, /*index...) while((s32[]{:T(128)}, f32[256,8,64]{0,2,1:T(8,128)}, ...), condition=%wide.region_37.38_spmd.clone, body=%wide.region_36.37_spmd.clone.sunk | while | flops 682361856 | bytes 85485480 | solution.py:150
  558.4 3.3 fusion.290
  573.9 3.2 fusion.290
  585.6 4.0 convolution_convert_fusion.2
  596.2 17.3 %reduce-scatter.12.cloned.1.call-done = bf16[256,512]{0,1:T(8,128)(2,1)} async-done(((bf16[1024,512]{0,1:T(8,128)(2,1)}), bf16[256,512]{0,1:T(8,128)(2,1)}) %reduce-scatter.12.cloned.1.call-update) | async-done | bytes 262160 | tf_op jit(solution)/shard_map/reduce_scatter | solution.py:280
  614.9 29.2 %reduce-scatter.14.cloned.1.call-done = bf16[256,512]{0,1:T(8,128)(2,1)} async-done(((bf16[1024,512]{0,1:T(8,128)(2,1)}), bf16[256,512]{0,1:T(8,128)(2,1)}) %reduce-scatter.14.cloned.1.call-update) | async-done | bytes 262160 | tf_op jit(solution)/shard_map/reduce_scatter | solution.py:283
  645.2 4.0 convolution_convert_fusion.4
  649.1 25.7 %reduce-scatter.10.cloned.1.call-done = bf16[256,512]{0,1:T(8,128)(2,1)} async-done(((bf16[1024,512]{0,1:T(8,128)(2,1)}), bf16[256,512]{0,1:T(8,128)(2,1)}) %reduce-scatter.10.cloned.1.call-update) | async-done | bytes 262160 | tf_op jit(solution)/shard_map/reduce_scatter | solution.py:283
  676.8 3.7 convolution_convert_fusion.6
  684.7 5.7 convolution_add_fusion
  690.3 17.8 %copy.90 = f32[1024,2,1312]{2,1,0:T(2,128)} copy(f32[1024,2,1312]{0,2,1:T(8,128)} %bitcast.400) | data formatting | bytes 21495808 | tf_op jit(solution)/shard_map/add | solution.py:321
  715.0 3.5 convolution_add_fusion.1
  721.3 3.8 convolution_add_fusion.2
  733.4 5.1 all-to-all-start.1
  740.7 50.2 %all-to-all-done.1 = bf16[2,1,1,256,1024]{4,0,2,1,3:T(2,128)(2,1)S(1)} async-done(((bf16[2,1,1,256,1024]{4,0,2,1,3:T(2,128)(2,1)}), bf16[2,1,1,256,1024]{4,0,2,1,3:T(2,128)(2,1)S(1)}, u32[]{:S(2)}, u32[]{:S(2)}) %all-to-all-start.1) | async-done | bytes 1048608 | tf_op jit(solution)/shard_map/all_to_all | solution.py:335
  790.9 3.5 all-to-all-start.3
  795.4 69.0 %all-reduce.5 = (f32[1024]{0:T(1024)S(1)}, f32[1024]{0:T(1024)S(1)}) all-reduce(f32[1024]{0:T(1024)S(1)} %add.438, f32[1024]{0:T(1024)S(1)} %add.439), channel_id=6, replica_groups=mesh['fsdp'=4,'ctx'=4,'tp'=2] {'fsdp','ctx'}, use_global_device_ids=true, to_apply=%region_45.46.clone | all-reduce | flops 2048 | bytes 16384
  869.4 220.8 %all-reduce.15.cloned.1.call-done = f32[1024,2,1312]{2,1,0:T(2,128)} async-done(((f32[1024,2,1312]{2,1,0:T(2,128)}), f32[1024,2,1312]{2,1,0:T(2,128)}) %all-reduce.15.cloned.1.call-update) | async-done | bytes 10747920
  1092.3 80.6 %reduce-scatter.18.cloned.1.call-done = f32[512,64]{0,1:T(8,128)} async-done(((f32[512,1024]{0,1:T(8,128)}), f32[512,64]{0,1:T(8,128)}) %reduce-scatter.18.cloned.1.call-update) | async-done | bytes 131088 | tf_op jit(solution)/shard_map/reduce_scatter | solution.py:328
  1172.8 125.4 %reduce-scatter.20.cloned.1.call-done = f32[1312,64]{0,1:T(8,128)} async-done(((f32[1312,1024]{0,1:T(8,128)}), f32[1312,64]{0,1:T(8,128)}) %reduce-scatter.20.cloned.1.call-update) | async-done | bytes 335888 | tf_op jit(solution)/shard_map/reduce_scatter | solution.py:330
  1298.2 140.1 %reduce-scatter.16.cloned.1.call-done = f32[64,3,512]{2,0,1:T(8,128)} async-done(((f32[1024,3,512]{2,0,1:T(8,128)}), f32[64,3,512]{2,0,1:T(8,128)}) %reduce-scatter.16.cloned.1.call-update) | async-done | bytes 393232 | tf_op jit(solution)/shard_map/reduce_scatter | solution.py:327
  (468 shorter events, 189.4 us)
Async XLA Ops:
  7.2 84.7 %all-gather.9.cloned.1.call-start = ((), (), s32[]{:S(2)}) async-start(), calls=%async_computation.11 | async-start | bytes 3342336 | tf_op jit(solution)/shard_map/all_gather | solution.py:159
  11.2 6.5 copy-start.92
  11.2 7.8 copy-start.96
  11.2 8.0 copy-start.97
  11.2 63.0 %all-to-all-start = ((bf16[2,4,1,64,1024]{4,3,2,0,1:T(8,128)(2,1)}), bf16[2,4,1,64,1024]{4,3,2,0,1:T(8,128)(2,1)S(1)}, u32[]{:S(2)}, u32[]{:S(2)}) async-start(bf16[2,4,1,64,1024]{4,3,2,0,1:T(8,128)(2,1)} %copy.72), calls=%async_computation | async-start | bytes 2097152 | tf_op jit(solution)/shard_map/all_to_all | solution.py:178
  17.7 109.5 %all-gather.21.cloned.1.call-start = ((), (), s32[]{:S(2)}) async-start(), calls=%async_computation.17 | async-start | bytes 1310720 | tf_op jit(solution)/shard_map/all_gather | solution.py:217
  74.3 26.7 %copy-start.75 = (f32[256,32]{0,1:T(8,128)}, f32[256,32]{0,1:T(8,128)S(1)}, u32[]{:S(2)}) copy-start(f32[256,32]{0,1:T(8,128)S(1)} %get-tuple-element.1011) | copy-start | bytes 98308
  74.3 237.1 %copy-start.6 = (bf16[2,4,1,64,1024]{4,3,2,0,1:T(8,128)(2,1)}, bf16[2,4,1,64,1024]{4,3,2,0,1:T(8,128)(2,1)S(1)}, u32[]{:S(2)}) copy-start(bf16[2,4,1,64,1024]{4,3,2,0,1:T(8,128)(2,1)S(1)} %all-to-all-done) | copy-start | bytes 3145732
  74.9 21.6 %copy-start.88 = (f32[4,64]{1,0:T(4,128)}, f32[4,64]{1,0:T(4,128)S(1)}, u32[]{:S(2)}) copy-start(f32[4,64]{1,0:T(4,128)S(1)} %add_rsqrt_fusion.1) | copy-start | bytes 3076
  75.0 21.6 %copy-start.86 = (f32[4,64]{1,0:T(4,128)}, f32[4,64]{1,0:T(4,128)S(1)}, u32[]{:S(2)}) copy-start(f32[4,64]{1,0:T(4,128)S(1)} %add_rsqrt_fusion) | copy-start | bytes 3076
  75.4 21.2 %copy-start.59 = (bf16[1,4,1,64,1024]{4,3,1,2,0:T(8,128)(2,1)}, bf16[1,4,1,64,1024]{4,3,1,2,0:T(8,128)(2,1)S(1)}, u32[]{:S(2)}) copy-start(bf16[1,4,1,64,1024]{4,3,1,2,0:T(8,128)(2,1)S(1)} %get-tuple-element.972) | copy-start | bytes 1572868
  75.4 24.4 %copy-start.57 = (bf16[1,4,1,64,1024]{4,3,1,2,0:T(8,128)(2,1)}, bf16[1,4,1,64,1024]{4,3,1,2,0:T(8,128)(2,1)S(1)}, u32[]{:S(2)}) copy-start(bf16[1,4,1,64,1024]{4,3,1,2,0:T(8,128)(2,1)S(1)} %get-tuple-element.973) | copy-start | bytes 1572868
  102.1 54.0 %all-gather.23.cloned.1.call-start = ((), (), s32[]{:S(2)}) async-start(), calls=%async_computation.18 | async-start | bytes 1310720 | tf_op jit(solution)/shard_map/all_gather | solution.py:218
  102.9 82.0 %all-gather.11.cloned.1.call-start = ((), (), s32[]{:S(2)}) async-start(), calls=%async_computation.12 | async-start | bytes 1310720 | tf_op jit(solution)/shard_map/all_gather | solution.py:217
  103.7 110.0 %all-gather.13.cloned.1.call-start = ((), (), s32[]{:S(2)}) async-start(), calls=%async_computation.13 | async-start | bytes 1310720 | tf_op jit(solution)/shard_map/all_gather | solution.py:218
  105.5 166.1 %all-gather.15.cloned.1.call-start = ((), (), s32[]{:S(2)}) async-start(), calls=%async_computation.14 | async-start | bytes 1114112 | tf_op jit(solution)/shard_map/all_gather | solution.py:160
  106.1 203.1 %all-reduce.21.cloned.1.call-start = ((), (), s32[]{:S(2)}) async-start(), calls=%async_computation.29 | async-start | bytes 2097152 | tf_op jit(solution)/shard_map/psum | solution.py:226
  234.8 40.7 %copy-start.53 = (bf16[8,256,64]{1,2,0:T(8,128)(2,1)}, bf16[8,256,64]{1,2,0:T(8,128)(2,1)S(1)}, u32[]{:S(2)}) copy-start(bf16[8,256,64]{1,2,0:T(8,128)(2,1)S(1)} %fusion.123) | copy-start | bytes 786436
  236.0 39.5 %copy-start.51 = (bf16[8,256,64]{1,2,0:T(8,128)(2,1)}, bf16[8,256,64]{1,2,0:T(8,128)(2,1)S(1)}, u32[]{:S(2)}) copy-start(bf16[8,256,64]{1,2,0:T(8,128)(2,1)S(1)} %fusion.122) | copy-start | bytes 786436
  275.5 112.4 %all-gather.17.cloned.1.call-start = ((), (), s32[]{:S(2)}) async-start(), calls=%async_computation.15 | async-start | bytes 6127616 | tf_op jit(solution)/shard_map/all_gather | solution.py:161
  276.3 179.1 %all-gather.19.cloned.1.call-start = ((), (), s32[]{:S(2)}) async-start(), calls=%async_computation.16 | async-start | bytes 3063808 | tf_op jit(solution)/shard_map/all_gather | solution.py:162
  279.9 28.2 %all-to-all-start.2 = ((bf16[2,4,1,64,1024]{4,3,2,0,1:T(8,128)(2,1)}), bf16[2,4,1,64,1024]{4,3,2,0,1:T(8,128)(2,1)S(1)}, u32[]{:S(2)}, u32[]{:S(2)}) async-start(bf16[2,4,1,64,1024]{4,3,2,0,1:T(8,128)(2,1)} %copy.83), calls=%async_computation.2 | async-start | bytes 2097152 | tf_op jit(solution)/shard_map/all_to_all | solution.py:179
  283.5 213.9 %all-reduce.19.cloned.1.call-start = ((), (), s32[]{:S(2)}) async-start(), calls=%async_computation.28 | async-start | bytes 2097152 | tf_op jit(solution)/shard_map/psum | solution.py:254
  312.7 186.8 %copy-start.21 = (f32[256,1024]{1,0:T(8,128)}, f32[256,1024]{1,0:T(8,128)S(1)}, u32[]{:S(2)}) copy-start(f32[256,1024]{1,0:T(8,128)S(1)} %get-tuple-element.978) | copy-start | bytes 3145732
  312.7 90.0 %copy-start.23 = (f32[256,1024]{1,0:T(8,128)S(1)}, f32[256,1024]{1,0:T(8,128)}, u32[]{:S(2)}) copy-start(f32[256,1024]{1,0:T(8,128)} %get-tuple-element.979) | copy-start | bytes 3145732
  402.7 5.8 copy-start.10
  408.5 46.8 %copy-start.36 = (bf16[1,4,1,64,1024]{4,3,2,0,1:T(8,128)(2,1)S(1)}, bf16[1,4,1,64,1024]{4,3,2,0,1:T(8,128)(2,1)}, u32[]{:S(2)}) copy-start(bf16[1,4,1,64,1024]{4,3,2,0,1:T(8,128)(2,1)} %get-tuple-element.977) | copy-start | bytes 1572868
  455.3 7.8 copy-start.32
  464.4 5.3 copy-start.46
  464.4 11.6 slice-start
  469.7 6.3 slice-start.1
  478.5 116.7 %reduce-scatter.8.cloned.1.call-start = ((), (), s32[]{:S(2)}) async-start(), calls=%async_computation.19 | async-start | bytes 1310720 | tf_op jit(solution)/shard_map/reduce_scatter | solution.py:280
  548.3 65.2 %reduce-scatter.12.cloned.1.call-start = ((), (), s32[]{:S(2)}) async-start(), calls=%async_computation.21 | async-start | bytes 1310720 | tf_op jit(solution)/shard_map/reduce_scatter | solution.py:280
  584.3 59.8 %reduce-scatter.14.cloned.1.call-start = ((), (), s32[]{:S(2)}) async-start(), calls=%async_computation.22 | async-start | bytes 1310720 | tf_op jit(solution)/shard_map/reduce_scatter | solution.py:283
  585.5 89.3 %reduce-scatter.10.cloned.1.call-start = ((), (), s32[]{:S(2)}) async-start(), calls=%async_computation.20 | async-start | bytes 1310720 | tf_op jit(solution)/shard_map/reduce_scatter | solution.py:283
  592.7 133.5 %all-reduce.17.cloned.1.call-start = ((), (), s32[]{:S(2)}) async-start(), calls=%async_computation.27 | async-start | bytes 4194304 | tf_op jit(solution)/shard_map/psum | solution.py:238
  594.0 20.4 %copy-start.76 = (f32[256,32]{0,1:T(8,128)S(1)}, f32[256,32]{0,1:T(8,128)}, u32[]{:S(2)}) copy-start(f32[256,32]{0,1:T(8,128)} %copy-done.75) | copy-start | bytes 98308
  594.0 20.4 %copy-start.77 = (f32[256,32]{0,1:T(8,128)S(1)}, f32[256,32]{0,1:T(8,128)}, u32[]{:S(2)}) copy-start(f32[256,32]{0,1:T(8,128)} %get-tuple-element.1009) | copy-start | bytes 98308
  680.5 409.7 %all-reduce.15.cloned.1.call-start = ((), (), s32[]{:S(2)}) async-start(), calls=%async_computation.26 | async-start | bytes 23068672
  708.2 464.7 %reduce-scatter.18.cloned.1.call-start = ((), (), s32[]{:S(2)}) async-start(), calls=%async_computation.24 | async-start | bytes 2228224 | tf_op jit(solution)/shard_map/reduce_scatter | solution.py:328
  711.8 586.4 %reduce-scatter.20.cloned.1.call-start = ((), (), s32[]{:S(2)}) async-start(), calls=%async_computation.25 | async-start | bytes 6127616 | tf_op jit(solution)/shard_map/reduce_scatter | solution.py:330
  718.6 719.7 %reduce-scatter.16.cloned.1.call-start = ((), (), s32[]{:S(2)}) async-start(), calls=%async_computation.23 | async-start | bytes 6684672 | tf_op jit(solution)/shard_map/reduce_scatter | solution.py:327
  733.4 57.5 %all-to-all-start.1 = ((bf16[2,1,1,256,1024]{4,0,2,1,3:T(2,128)(2,1)}), bf16[2,1,1,256,1024]{4,0,2,1,3:T(2,128)(2,1)S(1)}, u32[]{:S(2)}, u32[]{:S(2)}) async-start(bf16[2,1,1,256,1024]{4,0,2,1,3:T(2,128)(2,1)} %copy.77), calls=%async_computation.1 | async-start | bytes 2097152 | tf_op jit(solution)/shard_map/all_to_all | solution.py:335
  740.7 53.8 %copy-start.85 = (s32[2,4]{0,1:T(4,128)S(1)}, s32[2,4]{0,1:T(4,128)}, u32[]{:S(2)}) copy-start(s32[2,4]{0,1:T(4,128)} %copy-done.84) | copy-start | bytes 100
  740.7 54.7 %copy-start.90 = (f32[1024]{0:T(1024)S(1)}, f32[1024]{0:T(1024)}, u32[]{:S(2)}) copy-start(f32[1024]{0:T(1024)} %get-tuple-element.838) | copy-start | bytes 12292
  740.7 54.7 %copy-start.91 = (f32[1024]{0:T(1024)S(1)}, f32[1024]{0:T(1024)}, u32[]{:S(2)}) copy-start(f32[1024]{0:T(1024)} %get-tuple-element.836) | copy-start | bytes 12292
  790.9 76.6 %all-to-all-start.3 = ((bf16[2,1,1,256,1024]{4,0,2,1,3:T(2,128)(2,1)}), bf16[2,1,1,256,1024]{4,0,2,1,3:T(2,128)(2,1)S(1)}, u32[]{:S(2)}, u32[]{:S(2)}) async-start(bf16[2,1,1,256,1024]{4,0,2,1,3:T(2,128)(2,1)} %copy.86), calls=%async_computation.7 | async-start | bytes 2097152 | tf_op jit(solution)/shard_map/all_to_all | solution.py:336
  867.8 570.5 %copy-start.1 = (bf16[2,4,1,64,1024]{4,3,2,1,0:T(8,128)(2,1)S(1)}, bf16[2,4,1,64,1024]{4,3,2,1,0:T(8,128)(2,1)}, u32[]{:S(2)}) copy-start(bf16[2,4,1,64,1024]{4,3,2,1,0:T(8,128)(2,1)} %param.18) | copy-start | bytes 3145732
  (91 other events, 224.6 us)
Sparse Core Ops, SparseCore 0:
  10.8 81.0 all-gather.8
  102.2 24.9 all-gather.20
  129.6 26.4 all-gather.22
  158.3 26.4 all-gather.10
  187.1 26.4 all-gather.12
  216.3 55.2 all-gather.14
  275.6 18.4 all-reduce.20
  297.2 90.6 all-gather.16
  391.0 64.2 all-gather.18
  478.6 18.7 all-reduce.18
  548.4 28.8 reduce-scatter.7
  584.4 28.9 reduce-scatter.11
  616.3 27.7 reduce-scatter.13
  647.1 27.7 reduce-scatter.9
  680.6 21.3 all-reduce.16
  709.5 380.6 all-reduce.14
  1092.9 79.8 reduce-scatter.17
  1175.6 122.6 reduce-scatter.19
  1301.1 137.1 reduce-scatter.15
where the time goes:
time: 1450 us
  waiting for transfers between devices  991 us (68%)
  matrix products  131 us (9%)
  blocking collectives  123 us (8%)
  local copies, waits for them, and re-layouts  103 us (7%)
  other arithmetic  59.4 us (4%)
  starting transfers between devices  20.2 us (1%)
  between operations  16.8 us (1%)
    unnamed x20, waiting for transfers between devices  224 us
    reduce_scatter x1, waiting for transfers between devices, per_device(): lax.psum_scatter(grad_totals[2], ('fsdp', 'ctx'), scatter_dimension=0, ti...  140 us
    reduce_scatter x1, waiting for transfers between devices, per_device(): lax.psum_scatter(grad_totals[5], ('fsdp', 'ctx'), scatter_dimension=1, ti...  125 us
    unnamed x2, blocking collectives  123 us
    reduce_scatter x1, waiting for transfers between devices, per_device(): lax.psum_scatter(grad_totals[3], ('fsdp', 'ctx'), scatter_dimension=1, ti...  80.6 us
    all_gather x1, waiting for transfers between devices, per_device(): lax.all_gather(w_in, ('fsdp', 'ctx'), axis=0, tiled=True)  75.1 us
    all_gather x2, waiting for transfers between devices, per_device(): lax.all_gather(value_rows, 'ctx', axis=0, tiled=True)  57.7 us
    reduce_scatter x2, waiting for transfers between devices, per_device(): lax.psum_scatter(value_grad_all.astype(jnp.bfloat16), 'ctx', scatter_dime...  54.9 us
  transfers between devices with their start and end apart: 23, of which 18 were waited for; matrix products, arithmetic and copies ran while one was open for 13% of the time, Pallas kernels for 0%

commit v1 on v0

v1 whole, which is shorter than its diff:
```python
import functools

import jax
import jax.numpy as jnp
from jax import lax
from jax.experimental import pallas as pl
from jax.experimental.pallas import tpu as pltpu
from jax.sharding import PartitionSpec as P

D = 1024
HEAD_DIM = 64
norm_eps = 1e-05
rope_base = 160000.0
masked_score = -1e30
MESH = pl.DeviceIdType.MESH
BF = jnp.bfloat16
F32 = jnp.float32
VLIMIT = 56 << 20


def nn(a, b):
    return lax.dot_general(a, b, (((1,), (0,)), ((), ())), preferred_element_type=F32)


def nt(a, b):
    return lax.dot_general(a, b, (((1,), (1,)), ((), ())), preferred_element_type=F32)


def tn(a, b):
    return lax.dot_general(a, b, (((0,), (0,)), ((), ())), preferred_element_type=F32)


def norm_stats(values):
    center = values - jnp.mean(values, axis=-1, keepdims=True)
    spread = jnp.mean(center * center, axis=-1, keepdims=True)
    inverse_std = lax.rsqrt(spread + norm_eps)
    return center * inverse_std, inverse_std


def norm_back(upstream, normed, inverse_std, gain):
    scaled = upstream * gain
    adjusted = (
        scaled
        - jnp.mean(scaled, axis=-1, keepdims=True)
        - normed * jnp.mean(scaled * normed, axis=-1, keepdims=True)
    )
    return adjusted * inverse_std


def here():
    return lax.axis_index("fsdp"), lax.axis_index("ctx"), lax.axis_index("tp")


def remote(src, dst, sems, i, where):
    return pltpu.make_async_remote_copy(
        src_ref=src,
        dst_ref=dst,
        send_sem=sems.at[0, i],
        recv_sem=sems.at[1, i],
        device_id=where,
        device_id_type=MESH,
    )


def greet(peers):
    bar = pltpu.get_barrier_semaphore()
    for p in peers:
        pl.semaphore_signal(bar, inc=1, device_id=p, device_id_type=MESH)
    pl.semaphore_wait(bar, len(peers))


def plane_gather(full, sems, base=0):
    f, c, t = here()
    px, py, po = (f, c ^ 1, t), (f, c ^ 2, t), (f, c, 1 - t)
    cx, cy, cd = c ^ 1, c ^ 2, c ^ 3

    def cp(i, view, where):
        return remote(view, view, sems, base + i, where)

    sends = [
        cp(0, full.at[t, c], px),
        cp(1, full.at[t, c], py),
        cp(2, full.at[t, c], po),
    ]
    for s in sends:
        s.start()
    sends[0].wait_recv()
    more = [cp(3, full.at[t, cx, 1], py), cp(4, full.at[t, cx], po)]
    for s in more:
        s.start()
    sends[1].wait_recv()
    more += [cp(5, full.at[t, cy, 0], px), cp(6, full.at[t, cy], po)]
    for s in more[2:]:
        s.start()
    more[0].wait_recv()
    more[2].wait_recv()
    last = cp(7, full.at[t, cd], po)
    last.start()
    for s in (sends[2], more[1], more[3], last):
        s.wait_recv()
    for s in sends + more + [last]:
        s.wait_send()


GATHER_SEMS = 8
REDUCE_SEMS = 10


def plane_reduce(make, part, r0, rx, ry, sems, base=0):
    f, c, t = here()
    px, py, po = (f, c ^ 1, t), (f, c ^ 2, t), (f, c, 1 - t)
    cx, cy, cd = c ^ 1, c ^ 2, c ^ 3
    order = (cd, cx, cy, c)
    cross = []
    for i, span in enumerate(order):
        make(1 - t, span)
        s = remote(part.at[1 - t, span], r0.at[i], sems, base + i, po)
        s.start()
        cross.append(s)
    for span in order:
        make(t, span)

    def add(i, span):
        cross[i].wait_recv()
        part[t, span] = (part[t, span].astype(F32) + r0[i].astype(F32)).astype(BF)

    add(0, cd)
    a0 = remote(part.at[t, cd, 0], rx.at[0], sems, base + 4, px)
    b0 = remote(part.at[t, cd, 1], ry.at[0], sems, base + 5, py)
    a0.start()
    b0.start()
    add(1, cx)
    a1 = remote(part.at[t, cx, 0], rx.at[1], sems, base + 6, px)
    a1.start()
    add(2, cy)
    b1 = remote(part.at[t, cy, 1], ry.at[1], sems, base + 7, py)
    b1.start()
    a0.wait_recv()
    part[t, cy, 0] = (part[t, cy, 0].astype(F32) + rx[0].astype(F32)).astype(BF)
    b2 = remote(part.at[t, cy, 0], ry.at[2], sems, base + 8, py)
    b2.start()
    b0.wait_recv()
    part[t, cx, 1] = (part[t, cx, 1].astype(F32) + ry[0].astype(F32)).astype(BF)
    a2 = remote(part.at[t, cx, 1], rx.at[2], sems, base + 9, px)
    a2.start()
    cross[3].wait_recv()
    own = part[t, c].astype(F32) + r0[3].astype(F32)
    a1.wait_recv()
    b1.wait_recv()
    b2.wait_recv()
    top = own[0] + rx[1].astype(F32) + ry[2].astype(F32)
    a2.wait_recv()
    bottom = own[1] + ry[1].astype(F32) + rx[2].astype(F32)
    for s in cross + [a0, b0, a1, b1, a2, b2]:
        s.wait_send()
    return jnp.concatenate([top, bottom], axis=0)


def reduce_scratch(rows):
    return [
        pltpu.VMEM((2, 4, 2, rows, D), BF),
        pltpu.VMEM((4, 2, rows, D), BF),
        pltpu.VMEM((3, rows, D), BF),
        pltpu.VMEM((3, rows, D), BF),
    ]


def vm():
    return pl.BlockSpec(memory_space=pltpu.VMEM)


def shaped(shape, dtype):
    return jax.ShapeDtypeStruct(shape, dtype)


def comm_call(kernel, out_shape, scratch, n_sems, cid, n_in):
    return pl.pallas_call(
        kernel,
        out_shape=out_shape,
        in_specs=[vm()] * n_in,
        out_specs=jax.tree.map(lambda _: vm(), out_shape),
        scratch_shapes=scratch + [pltpu.SemaphoreType.DMA((2, n_sems))],
        compiler_params=pltpu.CompilerParams(
            collective_id=cid, has_side_effects=True, vmem_limit_bytes=VLIMIT
        ),
    )


def start_kernel(
    n_f, tok, cot, gains, w1, w2, w3, tok_o, cot_o, gains_o, w1_o, w2_o, w3_o, low_o, gz, gp, sems
):
    f, c, t = here()
    plane = [(f, c ^ 1, t), (f, c ^ 2, t), (f, c ^ 3, t)]
    zs = [(lax.rem(f + k, n_f), c, t) for k in range(1, n_f)]
    greet(plane + zs + [(f, c, 1 - t)])
    n_z = n_f - 1
    toks = [remote(tok.at[zs[k][0]], tok_o.at[f], sems, k, zs[k]) for k in range(n_z)]
    gs = [remote(gains, gz.at[f], sems, n_z + k, zs[k]) for k in range(n_z)]
    for k in range(n_z):
        gs[k].start()
        toks[k].start()
    base = 2 * n_z
    ws = []
    for k in range(3):
        for j, (src, dst) in enumerate(((w1, w1_o), (w2, w2_o), (w3, w3_o))):
            ws.append(remote(src.at[plane[k][1]], dst.at[c], sems, base + 3 * k + j, plane[k]))
            ws[-1].start()
    base += 9
    for src, dst in ((w1, w1_o), (w2, w2_o), (w3, w3_o)):
        dst[c] = src[c]
    tok_o[f] = tok[f]
    cot_o[f] = cot[f]
    gz[f] = gains[...]
    for g in gs:
        g.wait_recv()
    gp[c] = jnp.sum(gz[...], axis=0)
    gps = [remote(gp.at[c], gp.at[c], sems, base + k, plane[k]) for k in range(3)]
    for g in gps:
        g.start()
    base += 3
    for s in toks:
        s.wait_recv()
    cots = [remote(cot.at[zs[k][0]], cot_o.at[f], sems, base + k, zs[k]) for k in range(n_z)]
    for s in cots:
        s.start()
    base += n_z
    for g in gps:
        g.wait_recv()
    gains_o[...] = jnp.sum(gp[...], axis=0)
    rows = tok_o[...].reshape(-1, D).astype(F32)
    hat, _ = norm_stats(rows)
    low_o[t, c] = (hat * gains_o[0:1, :]).astype(BF).reshape(2, -1, D)
    plane_gather(low_o, sems, base)
    for s in ws + cots:
        s.wait_recv()
    for s in toks + gs + ws + gps + cots:
        s.wait_send()


def mid1_kernel(mixed, w_out, tok, gains, hidden_o, low_o, part, r0, rx, ry, sems):
    f, c, t = here()
    greet([(f, c ^ 1, t), (f, c ^ 2, t), (f, c, 1 - t)])
    half = part.shape[3]

    def make(m, span):
        part[m, span] = nt(mixed[m, span], w_out[...]).astype(BF).reshape(2, half, D)

    summed = plane_reduce(make, part, r0, rx, ry, sems)
    hidden = tok[...].reshape(-1, D).astype(F32) + summed
    hidden_o[...] = hidden
    hat, _ = norm_stats(hidden)
    low_o[t, c] = (hat * gains[1:2, :]).astype(BF).reshape(2, half, D)
    plane_gather(low_o, sems, REDUCE_SEMS)


def mlp_kernel(activated, w_down, hidden, out_o, part, r0, rx, ry, sems):
    f, c, t = here()
    greet([(f, c ^ 1, t), (f, c ^ 2, t), (f, c, 1 - t)])
    half = part.shape[3]

    def make(m, span):
        part[m, span] = nt(activated[m, span], w_down[...]).astype(BF).reshape(2, half, D)

    summed = plane_reduce(make, part, r0, rx, ry, sems)
    out_o[...] = (hidden[...] + summed).astype(BF).reshape(out_o.shape)


def mid2_kernel(
    gate_grad, w_in, hidden, cot, gains, hg_o, gain_o, low_o, part, r0, rx, ry, sems
):
    f, c, t = here()
    greet([(f, c ^ 1, t), (f, c ^ 2, t), (f, c, 1 - t)])
    half = part.shape[3]

    def make(m, span):
        part[m, span] = nt(gate_grad[m, span], w_in[...]).astype(BF).reshape(2, half, D)

    grad = plane_reduce(make, part, r0, rx, ry, sems)
    hat, inv = norm_stats(hidden[...])
    gain_o[...] = jnp.broadcast_to(jnp.sum(grad * hat, axis=0, keepdims=True), gain_o.shape)
    hg = cot[...].reshape(-1, D).astype(F32) + norm_back(grad, hat, inv, gains[1:2, :])
    hg_o[...] = hg
    low_o[t, c] = hg.astype(BF).reshape(2, half, D)
    plane_gather(low_o, sems, REDUCE_SEMS)


def end_kernel(
    n_f, joined, w_qkv, tok, hg, gains, gain2, out_rows,
    out_o, grad_o, gain_o, grad_rows, part, r0, rx, ry, gz, gp, gt, sems,
):
    f, c, t = here()
    plane = [(f, c ^ 1, t), (f, c ^ 2, t), (f, c ^ 3, t)]
    zs = [(lax.rem(f + k, n_f), c, t) for k in range(1, n_f)]
    po = (f, c, 1 - t)
    greet(plane + zs + [po])
    n_z = n_f - 1
    half = part.shape[3]
    outs = [remote(out_rows.at[zs[k][0]], out_o.at[f], sems, k, zs[k]) for k in range(n_z)]
    for s in outs:
        s.start()
    base = n_z
    out_o[f] = out_rows[f]

    def make(m, span):
        part[m, span] = nt(joined[m, span], w_qkv[...]).astype(BF).reshape(2, half, D)

    grad = plane_reduce(make, part, r0, rx, ry, sems, base)
    base += REDUCE_SEMS
    hat, inv = norm_stats(tok[...].reshape(-1, D).astype(F32))
    gain1 = jnp.sum(grad * hat, axis=0, keepdims=True)
    rows = hg[...] + norm_back(grad, hat, inv, gains[0:1, :])
    grad_rows[...] = rows.astype(BF).reshape(grad_rows.shape)
    grads = [remote(grad_rows.at[zs[k][0]], grad_o.at[f], sems, base + k, zs[k]) for k in range(n_z)]
    for s in grads:
        s.start()
    base += n_z
    grad_o[f] = grad_rows[f]
    row = lax.broadcasted_iota(jnp.int32, gain2.shape, 0)
    gt[0] = jnp.where(row == 0, gain1, jnp.where(row == 1, gain2[...], 0.0))
    s0 = remote(gt.at[0], gt.at[1], sems, base, po)
    s0.start()
    s0.wait_recv()
    gp[c] = gt[0] + gt[1]
    base += 1
    gps = [remote(gp.at[c], gp.at[c], sems, base + k, plane[k]) for k in range(3)]
    for s in gps:
        s.start()
    for s in gps:
        s.wait_recv()
    base += 3
    gz[f] = jnp.sum(gp[...], axis=0)
    gzs = [remote(gz.at[f], gz.at[f], sems, base + k, zs[k]) for k in range(n_z)]
    for s in gzs:
        s.start()
    for s in gzs:
        s.wait_recv()
    gain_o[...] = jnp.sum(gz[...], axis=0)
    for s in outs + grads:
        s.wait_recv()
    for s in outs + grads + [s0] + gps + gzs:
        s.wait_send()


def swap_kernel(src, dst, sems):
    f, c, t = here()
    plane = [(f, c ^ 1, t), (f, c ^ 2, t), (f, c ^ 3, t)]
    greet(plane)
    cps = [remote(src.at[p[1]], dst.at[c], sems, k, p) for k, p in enumerate(plane)]
    for s in cps:
        s.start()
    dst[c] = src[c]
    for s in cps:
        s.wait_recv()
    for s in cps:
        s.wait_send()


QB = 256


def rotate(u, cos, sin, lane, sign):
    partner = jnp.where(lane % HEAD_DIM < HEAD_DIM // 2, pltpu.roll(u, 96, 1), pltpu.roll(u, 32, 1))
    return u * cos + partner * (sin * sign)


def attend_kernel(live_ref, low, w, cos, sin, q_o, k_o, v_o, mixed_o, out_o, lse_o):
    live = live_ref[pl.program_id(0)]
    rows = low.shape[1]
    joined = nn(low[0], w[...])
    lane = lax.broadcasted_iota(jnp.int32, (rows, 128), 1)
    q_o[0] = (rotate(joined[:, 0:128], cos[...], sin[...], lane, 1.0).astype(BF) * BF(0.125))
    k_o[0] = rotate(joined[:, 128:256], cos[...], sin[...], lane, 1.0).astype(BF)
    v = joined[:, 256:384]
    v_o[0] = v.astype(BF)
    v_t = v.T.astype(BF)
    head_lane = lax.broadcasted_iota(jnp.int32, (QB, 128), 1) < HEAD_DIM
    alive = lax.broadcasted_iota(jnp.int32, (rows, QB), 0) < live

    def block(b, carry):
        at = pl.ds(pl.multiple_of(b * QB, QB), QB)
        qb = q_o[0, at, :]
        for h in range(2):
            qh = jnp.where(head_lane if h == 0 else ~head_lane, qb, BF(0.0))
            s = jnp.where(alive, nt(k_o[0], qh), masked_score)
            top = jnp.max(s, axis=0, keepdims=True)
            p = jnp.exp(s - top)
            total = jnp.sum(p, axis=0, keepdims=True)
            o = nn(v_t[h * HEAD_DIM : (h + 1) * HEAD_DIM], p.astype(BF)) / total
            out_o[0, h * HEAD_DIM : (h + 1) * HEAD_DIM, at] = o
            lse_o[0, h : h + 1, at] = top + jnp.log(total)
        return carry

    lax.fori_loop(0, rows // QB, block, 0)
    mixed_o[0] = out_o[0].T.astype(BF)


def attend(live, low, w, cos, sin):
    m, rows, _ = low.shape
    one = lambda *shape: pl.BlockSpec((1,) + shape, lambda i, live: (i, 0, 0))
    whole = lambda *shape: pl.BlockSpec(shape, lambda i, live: (0, 0))
    return pl.pallas_call(
        attend_kernel,
        out_shape=[shaped((m, rows, 128), BF)] * 4
        + [shaped((m, 128, rows), F32), shaped((m, 8, rows), F32)],
        grid_spec=pltpu.PrefetchScalarGridSpec(
            num_scalar_prefetch=1,
            grid=(m,),
            in_specs=[one(rows, D), whole(D, 384), whole(rows, 128), whole(rows, 128)],
            out_specs=[one(rows, 128)] * 4 + [one(128, rows), one(8, rows)],
        ),
        compiler_params=pltpu.CompilerParams(vmem_limit_bytes=VLIMIT),
    )(live, low, w, cos, sin)


def back_kernel(
    live_ref, low, w_out, q, k, v, out, lse, cos, sin, joined_o, dk, dv, dq_t, mg, delta
):
    live = live_ref[pl.program_id(0)]
    rows = low.shape[1]
    grad = nn(low[0], w_out[...]).astype(BF)
    mg[...] = grad
    weighted = grad.astype(F32).T * out[0]
    delta[0:1, :] = jnp.sum(weighted[:HEAD_DIM], axis=0, keepdims=True)
    delta[1:2, :] = jnp.sum(weighted[HEAD_DIM:], axis=0, keepdims=True)
    k_t = k[0].astype(F32).T.astype(BF)
    dk[...] = jnp.zeros_like(dk)
    dv[...] = jnp.zeros_like(dv)
    head_lane = lax.broadcasted_iota(jnp.int32, (QB, 128), 1) < HEAD_DIM
    alive = lax.broadcasted_iota(jnp.int32, (rows, QB), 0) < live

    def block(b, carry):
        at = pl.ds(pl.multiple_of(b * QB, QB), QB)
        qb = q[0, at, :]
        gb = mg[at, :]
        for h in range(2):
            keep = head_lane if h == 0 else ~head_lane
            qh = jnp.where(keep, qb, BF(0.0))
            gh = jnp.where(keep, gb, BF(0.0))
            s = nt(k[0], qh)
            p = jnp.where(alive, jnp.exp(s - lse[0, h : h + 1, at]), 0.0)
            dp = nt(v[0], gh)
            ds = (p * (dp - delta[h : h + 1, at])).astype(BF)
            dv[...] += nn(p.astype(BF), gh)
            dk[...] += nn(ds, qh)
            dq_t[h * HEAD_DIM : (h + 1) * HEAD_DIM, at] = nn(
                k_t[h * HEAD_DIM : (h + 1) * HEAD_DIM], ds
            )
        return carry

    lax.fori_loop(0, rows // QB, block, 0)
    lane = lax.broadcasted_iota(jnp.int32, (rows, 128), 1)
    dq = dq_t[...].T * 0.125
    joined_o[0, :, 0:128] = rotate(dq, cos[...], sin[...], lane, -1.0).astype(BF)
    joined_o[0, :, 128:256] = rotate(dk[...], cos[...], sin[...], lane, -1.0).astype(BF)
    joined_o[0, :, 256:384] = dv[...].astype(BF)


def attend_back(live, low, w_out, q, k, v, out, lse, cos, sin):
    m, rows, _ = low.shape
    one = lambda *shape: pl.BlockSpec((1,) + shape, lambda i, live: (i, 0, 0))
    whole = lambda *shape: pl.BlockSpec(shape, lambda i, live: (0, 0))
    return pl.pallas_call(
        back_kernel,
        out_shape=shaped((m, rows, 384), BF),
        grid_spec=pltpu.PrefetchScalarGridSpec(
            num_scalar_prefetch=1,
            grid=(m,),
            in_specs=[one(rows, D), whole(D, 128), one(rows, 128), one(rows, 128), one(rows, 128),
                      one(128, rows), one(8, rows), whole(rows, 128), whole(rows, 128)],
            out_specs=one(rows, 384),
            scratch_shapes=[
                pltpu.VMEM((rows, 128), F32),
                pltpu.VMEM((rows, 128), F32),
                pltpu.VMEM((128, rows), F32),
                pltpu.VMEM((rows, 128), BF),
                pltpu.VMEM((8, rows), F32),
            ],
        ),
        compiler_params=pltpu.CompilerParams(vmem_limit_bytes=VLIMIT),
    )(live, low, w_out, q, k, v, out, lse, cos, sin)


def rope_tables(rows):
    lane = jnp.arange(128, dtype=jnp.int32)
    exponent = (2 * (lane % (HEAD_DIM // 2))).astype(F32)
    inverse = rope_base ** (-exponent / HEAD_DIM)
    angles = jnp.arange(rows, dtype=jnp.int32).astype(F32)[:, None] * inverse[None, :]
    sign = jnp.where(lane % HEAD_DIM < HEAD_DIM // 2, -1.0, 1.0)
    return jnp.cos(angles), jnp.sin(angles) * sign[None, :]


def per_device(n_f, n_c, n_t, tokens, cotangent, lengths, owners,
               norm_attn, norm_mlp, w_qkv, w_out, w_in, w_down):
    f, c, t = here()
    micro, seqs, _, piece, _ = tokens.shape
    assert n_c == 4 and n_t == 2 and micro == 2 and seqs == n_f
    span = piece * n_f
    half = span // 2
    rows = span * n_c
    total = micro * rows
    wr = w_qkv.shape[0]
    hid = w_in.shape[2] // n_c
    hp = -(-hid // 128) * 128
    heads = w_qkv.shape[2] // n_c

    inverse_order = jnp.argsort(owners, axis=1).astype(jnp.int32)
    my_order = lax.dynamic_index_in_dim(inverse_order, t, axis=0, keepdims=False)
    sent_tok = lax.dynamic_index_in_dim(tokens, t, 0, keepdims=False)[:, 0][my_order]
    sent_cot = lax.dynamic_index_in_dim(cotangent, t, 0, keepdims=False)[:, 0][my_order]
    live = lax.dynamic_index_in_dim(lengths, f, axis=1, keepdims=False)

    place = (f * n_c + c) * wr
    gains_own = jnp.stack([norm_attn, norm_mlp]).astype(F32)
    gains_row = lax.dynamic_update_slice(jnp.zeros((8, D), F32), gains_own, (0, place))

    def quarters(a):
        return a.transpose(2, 0, 1, 3).reshape(n_c, wr, -1)

    pad = [(0, 0)] * 3 + [(0, hp - hid)]
    p_qkv = quarters(w_qkv.reshape(wr, 3, n_c, heads))
    p_out = w_out.reshape(n_c, heads, wr).transpose(0, 2, 1)
    p1 = jnp.concatenate([p_qkv, p_out], axis=2)
    p2 = quarters(jnp.pad(w_in.reshape(wr, 2, n_c, hid), pad))
    p3 = jnp.pad(w_down.reshape(n_c, hid, wr).transpose(0, 2, 1), pad[1:])
    n1, n2, n3 = p1.shape[2], p2.shape[2], p3.shape[2]

    full_shape = (micro, n_c, 2, half, D)
    tok, cot, gains, q1, q2, q3, first_low = comm_call(
        functools.partial(start_kernel, n_f),
        [
            shaped((n_f, piece, D), BF), shaped((n_f, piece, D), BF), shaped((8, D), F32),
            shaped((n_c, wr, n1), BF), shaped((n_c, wr, n2), BF), shaped((n_c, wr, n3), BF),
            shaped(full_shape, BF),
        ],
        [pltpu.VMEM((n_f, 8, D), F32), pltpu.VMEM((n_c, 8, D), F32)],
        3 * (n_f - 1) + 12 + GATHER_SEMS, 0, 6,
    )(sent_tok, sent_cot, gains_row, p1, p2, p3)
    W1, W2, W3 = (
        lax.all_gather(q, "fsdp", axis=0, tiled=True).reshape(D, -1) for q in (q1, q2, q3)
    )
    wq, wo = W1[:, : 3 * heads], W1[:, 3 * heads :]
    cos, sin = rope_tables(rows)

    low3 = first_low.reshape(micro, rows, D)
    q, k, v, mixed, out_t, lse = attend(live, low3, wq, cos, sin)
    hidden, second_low = comm_call(
        mid1_kernel,
        [shaped((span, D), F32), shaped(full_shape, BF)],
        reduce_scratch(half), REDUCE_SEMS + GATHER_SEMS, 1, 4,
    )(mixed.reshape(micro, n_c, span, 128), wo, tok, gains)

    cot_full = lax.all_gather(
        lax.all_gather(cot.reshape(span, D), "ctx", axis=0, tiled=True), "tp", axis=0, tiled=True
    )
    flat = second_low.reshape(total, D)
    gate_up = nn(flat, W2)
    u, g = gate_up[:, :hp], gate_up[:, hp:]
    gelu, gelu_back = jax.vjp(lambda a: jax.nn.gelu(a, approximate=False), u)
    activated = (gelu * g).astype(BF)
    act_grad = nn(cot_full, W3)
    gate_grad = jnp.concatenate(
        [gelu_back(act_grad * g)[0], act_grad * gelu], axis=1
    ).astype(BF)
    hg, gain2, attn_low = comm_call(
        mid2_kernel,
        [shaped((span, D), F32), shaped((8, D), F32), shaped(full_shape, BF)],
        reduce_scratch(half), REDUCE_SEMS + GATHER_SEMS, 2, 5,
    )(gate_grad.reshape(micro, n_c, span, 2 * hp), W2, hidden, cot, gains)
    g_down = tn(cot_full, activated)
    g_in = tn(flat, gate_grad)
    early = jnp.concatenate([g_in, g_down], axis=1).astype(BF)
    early = lax.psum_scatter(early, "fsdp", scatter_dimension=0, tiled=True)

    out_rows = comm_call(
        mlp_kernel, shaped((n_f, piece, D), BF), reduce_scratch(half), REDUCE_SEMS, 3, 3
    )(activated.reshape(micro, n_c, span, hp), W3, hidden)

    attn_flat = attn_low.reshape(total, D)
    joined = attend_back(
        live, attn_low.reshape(micro, rows, D), wo, q, k, v, out_t, lse, cos, sin
    )
    g_out = tn(attn_flat, mixed.reshape(total, 128))
    g_qkv = tn(low3.reshape(total, D), joined.reshape(total, 384))
    late = jnp.concatenate([g_qkv, g_out], axis=1).astype(BF)
    late = lax.psum_scatter(late, "fsdp", scatter_dimension=0, tiled=True)

    outs, grads, gain_grads = comm_call(
        functools.partial(end_kernel, n_f),
        [shaped((n_f, piece, D), BF), shaped((n_f, piece, D), BF), shaped((8, D), F32)],
        [pltpu.VMEM((n_f, piece, D), BF)]
        + reduce_scratch(half)
        + [pltpu.VMEM((n_f, 8, D), F32), pltpu.VMEM((n_c, 8, D), F32), pltpu.VMEM((2, 8, D), F32)],
        3 * (n_f - 1) + REDUCE_SEMS + 4, 4, 7,
    )(joined.reshape(micro, n_c, span, 384), wq, tok, hg, gains, gain2, out_rows)

    shares = jnp.concatenate([late, early], axis=1).reshape(n_c, wr, -1)
    shares = comm_call(swap_kernel, shaped(shares.shape, BF), [], 3, 5, 1)(shares).astype(F32)
    grad_qkv = shares[:, :, : 3 * heads].reshape(n_c, wr, 3, heads).transpose(1, 2, 0, 3)
    grad_qkv = grad_qkv.reshape(wr, 3, n_c * heads)
    grad_out = shares[:, :, 3 * heads : n1].transpose(0, 2, 1).reshape(n_c * heads, wr)
    grad_in = shares[:, :, n1 : n1 + n2].reshape(n_c, wr, 2, hp)[..., :hid]
    grad_in = grad_in.transpose(1, 2, 0, 3).reshape(wr, 2, n_c * hid)
    grad_down = shares[:, :, n1 + n2 : n1 + n2 + hid].transpose(0, 2, 1).reshape(n_c * hid, wr)

    both_o = lax.all_gather(outs, "tp", axis=0, tiled=False)
    both_g = lax.all_gather(grads, "tp", axis=0, tiled=False)
    index = jnp.arange(micro, dtype=jnp.int32)[:, None]
    output = both_o[index, owners][:, :, None]
    grad_tokens = both_g[index, owners][:, :, None]
    mine = lax.dynamic_slice(gain_grads, (0, place), (2, wr))
    return (output, grad_tokens, mine[0], mine[1], grad_qkv, grad_out, grad_in, grad_down)


def solution(mesh):
    rows = P(None, None, "ctx", "fsdp", None)
    gain = P(("fsdp", "ctx"))
    tall = P(("fsdp", "ctx"), None, "tp")
    wide = P("tp", ("fsdp", "ctx"))
    return jax.shard_map(
        functools.partial(per_device, mesh.shape["fsdp"], mesh.shape["ctx"], mesh.shape["tp"]),
        mesh=mesh,
        in_specs=(rows, rows, P(), P(), gain, gain, tall, wide, tall, wide),
        out_specs=(rows, rows, gain, gain, tall, wide, tall, wide),
        check_vma=False,
    )
```

time: 1450 us -> 516 us (0.36)
  waiting for transfers between devices: 991 us -> 121 us
  Pallas kernels: 0 us -> 266 us
  matrix products: 131 us -> 26.3 us
  blocking collectives: 123 us -> 29.6 us
  local copies, waits for them, and re-layouts: 103 us -> 33.6 us
  other arithmetic: 59.4 us -> 19.4 us
  starting transfers between devices: 20.2 us -> 0.57 us
    reduce_scatter x7 -> x2, waiting for transfers between devices: 418 us -> 75.1 us  [the longest x1 49.2 us: per_device(): early = lax.psum_scatter(early, 'fsdp', scatter_dimension=0, tiled=True)]
    pallas_call x0 -> x8, Pallas kernels: none -> 266 us  [the longest x1 50.9 us: per_device(): comm_call(mid2_kernel, [shaped((span, D), F32), shaped((8, D), F32), shap...]
    unnamed x20 -> x8, waiting for transfers between devices: 224 us -> 1.98 us
    all_gather x8 -> x6, waiting for transfers between devices: 256 us -> 43.9 us  [the longest x1 38.1 us: per_device(): lax.all_gather(cot.reshape(span, D), 'ctx', axis=0, tiled=True)]
    unnamed x2 -> x0, blocking collectives: 123 us -> none
    dot_general x52 -> x6, matrix products: 131 us -> 26.3 us  [the longest x2 13.6 us: nn(): lax.dot_general(a, b, (((1,), (0,)), ((), ())), preferred_element_type=F32)]
    all_to_all x4 -> x0, waiting for transfers between devices: 74.6 us -> none  [the longest x1 50.2 us: per_device(): lax.all_to_all(stacked, 'fsdp', split_axis=3, concat_axis=1, tiled=True)]
    all_gather x0 -> x1, blocking collectives: none -> 29.6 us  [per_device(): lax.all_gather(q, 'fsdp', axis=0, tiled=True).reshape(D, -1)]
  transfers between devices with their start and end apart: 23 -> 8, of which waited for: 18 -> 4; matrix products, arithmetic and copies ran while one was open for 13% -> 9% of each run, Pallas kernels for 0% -> 18%
where the time goes in v1:
time: 516 us; the launch traced here: 511 us
  Pallas kernels  266 us (52%)
  waiting for transfers between devices  121 us (23%)
  local copies, waits for them, and re-layouts  33.6 us (7%)
  blocking collectives  29.6 us (6%)
  matrix products  26.3 us (5%)
  other arithmetic  19.4 us (4%)
  between operations  15.1 us (3%)
    pallas_call x1, Pallas kernels, per_device(): comm_call(mid2_kernel, [shaped((span, D), F32), shaped((8, D), F32), shap...  50.9 us
    reduce_scatter x1, waiting for transfers between devices, per_device(): early = lax.psum_scatter(early, 'fsdp', scatter_dimension=0, tiled=True)  49.2 us
    pallas_call x1, Pallas kernels, per_device(): comm_call(mid1_kernel, [shaped((span, D), F32), shaped(full_shape, BF)],...  47.8 us
    pallas_call x1, Pallas kernels, per_device(): comm_call(functools.partial(end_kernel, n_f), [shaped((n_f, piece, D), BF...  43.7 us
    pallas_call x1, Pallas kernels, per_device(): comm_call(functools.partial(start_kernel, n_f), [shaped((n_f, piece, D),...  43.2 us
    all_gather x1, waiting for transfers between devices, per_device(): lax.all_gather(cot.reshape(span, D), 'ctx', axis=0, tiled=True)  38.1 us
    all_gather x1, blocking collectives, per_device(): lax.all_gather(q, 'fsdp', axis=0, tiled=True).reshape(D, -1)  29.6 us
    pallas_call x1, Pallas kernels, per_device(): comm_call(mlp_kernel, shaped((n_f, piece, D), BF), reduce_scratch(half),...  26.4 us
  transfers between devices with their start and end apart: 8, of which 4 were waited for; matrix products, arithmetic and copies ran while one was open for 9% of the time, Pallas kernels for 18%

profile of v1, /device:TPU:0, one launch (start us, length us, event | category | flops | bytes accessed | tf_op | source)
XLA Modules:
  0.0 511.3 jit_solution(10761024274117349145)
XLA Ops:
  7.2 0.8 copy.42
  8.9 1.3 dynamic-slice_bitcast_fusion
  10.3 1.4 gather_fusion.1
  11.7 1.4 gather_fusion
  14.3 1.0 reshape.164.w2
  16.1 0.7 pad_maximum_fusion.4.w1
  16.8 0.7 pad.9.w3
  18.4 43.2 %shard_map.161 = (bf16[4,64,1024]{2,1,0:T(8,128)(2,1)}, bf16[4,64,1024]{2,1,0:T(8,128)(2,1)}, f32[8,1024]{1,0:T(8,128)}, bf16[4,64,512]{2,1,0:T(8,128)(2,1)}, bf...) custom-call(bf16[4,64,1024]{2,1,0:T(8,128)(2,1)} %gather_fusion, ...), custom_call_target="tpu_custom_call" | custom-call | tf_op jit(solution)/shard_map/pallas_call | solution.py:528
  61.7 0.7 all-gather.9.cloned.1.call-update
  63.2 38.1 %all-gather.13.cloned.1.call-done = bf16[1024,1024]{1,0:T(8,128)(2,1)} async-done(((bf16[256,1024]{1,0:T(8,128)(2,1)}), bf16[1024,1024]{1,0:T(8,128)(2,1)}) %all-gather.13.cloned.1.call-update) | async-done | bytes 2097168 | tf_op jit(solution)/shard_map/all_gather | solution.py:553
  101.4 0.7 fusion.15.live_ref
  102.1 3.1 fusion.14
  105.2 29.6 %all_gather.31 = bf16[16,64,384]{2,1,0:T(8,128)(2,1)} all-gather(bf16[4,64,384]{2,1,0:T(8,128)(2,1)S(1)} %copy-done.13), channel_id=1, replica_groups=mesh['fsdp'=4,'ctx'=4,'tp'=2] {'fsdp'}, dimensions={0}, use_global_device_ids=true | all-gather | bytes 983040 | tf_op jit(solution)/shard_map/all_gather | solution.py:539
  134.8 5.7 %all-gather.9.cloned.1.call-done = bf16[16,64,512]{2,1,0:T(8,128)(2,1)} async-done(((bf16[4,64,512]{2,1,0:T(8,128)(2,1)}), bf16[16,64,512]{2,1,0:T(8,128)(2,1)}) %all-gather.9.cloned.1.call-update) | async-done | bytes 1048592 | tf_op jit(solution)/shard_map/all_gather | solution.py:539
  140.5 2.1 slice.52.w.w_qkv
  142.6 1.7 slice.53.w_out
  144.3 20.1 %shard_map.162 = (bf16[2,1024,128]{2,1,0:T(8,128)(2,1)}, bf16[2,1024,128]{2,1,0:T(8,128)(2,1)}, bf16[2,1024,128]{2,1,0:T(8,128)(2,1)}, bf16[2,1024,128]{2,1,0:T(...) custom-call(s32[2]{0:T(128)} %fusion.15.live_ref, bf16[2,1024,1024]{2,1,0:T(8,128)(2,1)} %bitcast.91, ...), custom_call_target="tpu_custom_call" | custom-call | tf_op jit(solution)/shard_map/pallas_call | solution.py:401
  164.4 47.8 %shard_map.163 = (f32[256,1024]{1,0:T(8,128)}, bf16[2,4,2,128,1024]{4,3,2,1,0:T(8,128)(2,1)}) custom-call(bf16[2,4,256,128]{3,2,1,0:T(8,128)(2,1)} %bitcast.110, bf16[1024,128]{1,0:T(8,128)(2,1)} %slice.53.w_out, bf16[4,64,1024]{2,1,0:T(8,128)(2,1)} %get-tuple-element.34.tok, f32[8,1024]{1,0:T(8,128)} %get-tuple-element.35.gains), custom_call_target="tpu_custom_call" | custom-call | tf_op jit(solution)/shard_map/pallas_call | solution.py:546
  212.2 5.7 %fusion.28 = f32[2048,768]{1,0:T(8,128)S(1)} fusion(bf16[2048,1024]{1,0:T(8,128)(2,1)} %bitcast.114, bf16[1024,768]{1,0:T(8,128)(2,1)} %bitcast.98), kind=kOutput, calls=%fused_computation.75 | convolution fusion | flops 3221225472 | bytes 12058624 | tf_op jit(solution)/shard_map/dot_general | solution.py:22
  217.9 7.9 %multiply_convert_fusion = (bf16[2048,384]{1,0:T(8,128)(2,1)}, f32[2048,384]{1,0:T(8,128)S(1)}) fusion(f32[2048,768]{1,0:T(8,128)S(1)} %fusion.28), kind=kLoop, calls=%fused_computation.11 | loop fusion | flops 51904512 | bytes 11010048 | tf_op jit(solution)/shard_map/convert_element_type | solution.py:559
  225.7 26.4 %shard_map.166.out_rows = bf16[4,64,1024]{2,1,0:T(8,128)(2,1)} custom-call(bf16[2,4,256,384]{3,2,1,0:T(8,128)(2,1)} %bitcast.88, bf16[1024,384]{1,0:T(8,128)(2,1)} %bitcast.94, f32[256,1024]{1,0:T(8,128)} %get-tuple-element.40.hidden), custom_call_target="tpu_custom_call" | custom-call | tf_op jit(solution)/shard_map/pallas_call | solution.py:574
  252.2 7.9 %add_convert_fusion = (bf16[2048,384]{1,0:T(8,128)(2,1)S(1)}, bf16[2048,384]{1,0:T(8,128)(2,1)S(1)}) fusion(f32[2048,384]{1,0:T(8,128)S(1)} %get-tuple-element.53, f32[2048,768]{1,0:T(8,128)} %copy-done.3, bf16[2048,1024]{1,0:T(8,128)(2,1)} %all-gather.15.cloned.1.call-done, bf16[1024,384]{1,0:T(8,128)(2,1)} %bitcast.95), kind=kOutput, calls=%fused_computation.13 | convolution fusion | flops 1624768512 | bytes 17563648 | tf_op jit(solution)/shard_map/dot_general | solution.py:22
  260.1 1.2 copy-done.6
  261.8 2.0 pad_maximum_fusion.gate_grad
  263.8 50.9 %shard_map.164 = (f32[256,1024]{1,0:T(8,128)}, f32[8,1024]{1,0:T(8,128)}, bf16[2,4,2,128,1024]{4,3,2,1,0:T(8,128)(2,1)}) custom-call(bf16[2,4,256,768]{3,2,1,0:T(8,128)(2,1)} %pad_maximum_fusion.gate_grad, bf16[1024,768]{1,0:T(8,128)(2,1)} %bitcast.99, f32[256,1024]{1,0:T(8,128)} %get-tuple-element.40.hidden, bf16[4,64,1024]{2,1,0:T(8,128)(2,1)} %get-tuple-element.38.cot, ...), custom_call_target="tpu_custom_call" | custom-call | tf_op jit(solution)/shard_map/pallas_call | solution.py:564
  314.7 19.2 %shard_map.165 = bf16[2,1024,384]{2,1,0:T(8,128)(2,1)} custom-call(s32[2]{0:T(128)} %fusion.15.live_ref, bf16[2,1024,1024]{2,1,0:T(8,128)(2,1)} %bitcast.89, bf16[1024,128]{1,0:T(8,128)(2,1)} %slice.53.w_out, bf16[2,1024,128]{2,1,0:T(8,128)(2,1)} %get-tuple-element.42.q, bf16[2,1024,128]{2,1,0:T(8,128)(2,1)} %get-tuple-element.43.k, ...), custom_call_target="tpu_custom_call" | custom-call | tf_op jit(solution)/shard_map/pallas_call | solution.py:462
  333.9 43.7 %shard_map.167 = (bf16[4,64,1024]{2,1,0:T(8,128)(2,1)}, bf16[4,64,1024]{2,1,0:T(8,128)(2,1)}, f32[8,1024]{1,0:T(8,128)}) custom-call(bf16[2,4,256,384]{3,2,1,0:T(8,128)(2,1)} %bitcast.86, bf16[1024,384]{1,0:T(8,128)(2,1)} %slice.52.w.w_qkv, bf16[4,64,1024]{2,1,0:T(8,128)(2,1)} %get-tuple-element.34.tok, f32[256,1024]{1,0:T(8,128)} %get-tuple-element.47.hg, ...), custom_call_target="tpu_custom_call" | custom-call | tf_op jit(solution)/shard_map/pallas_call | solution.py:587
  378.3 3.1 convolution_convert_fusion.2
  381.4 0.7 copy-done.5
  382.2 1.9 convolution_convert_fusion.1
  384.0 1.1 pad_maximum_fusion.2
  385.8 4.2 convolution_convert_fusion
  390.1 3.6 fusion.11
  393.7 1.6 pad_maximum_fusion.1
  395.4 0.8 constant_dynamic-slice_fusion
  396.7 2.8 gather_fusion.2
  399.5 2.8 gather_fusion.3
  402.3 25.9 %reduce-scatter.3.cloned.1.call-done = bf16[256,512]{0,1:T(8,128)(2,1)} async-done(((bf16[1024,512]{0,1:T(8,128)(2,1)}), bf16[256,512]{0,1:T(8,128)(2,1)}) %reduce-scatter.3.cloned.1.call-update) | async-done | bytes 262160 | tf_op jit(solution)/shard_map/reduce_scatter | solution.py:585
  428.2 49.2 %reduce-scatter.5.cloned.1.call-done = bf16[256,1152]{0,1:T(8,128)(2,1)} async-done(((bf16[1024,1152]{0,1:T(8,128)(2,1)}), bf16[256,1152]{0,1:T(8,128)(2,1)}) %reduce-scatter.5.cloned.1.call-update) | async-done | bytes 589840 | tf_op jit(solution)/shard_map/reduce_scatter | solution.py:572
  477.4 1.2 pad_maximum_fusion.3
  478.6 1.4 copy.47
  479.9 14.4 %shard_map.168 = bf16[4,64,1664]{2,1,0:T(8,128)(2,1)} custom-call(bf16[4,64,1664]{2,1,0:T(8,128)(2,1)} %bitcast.93), custom_call_target="tpu_custom_call" | custom-call | tf_op jit(solution)/shard_map/pallas_call | solution.py:597
  494.4 1.1 slice.58
  495.4 1.3 convert_element_type.47
  497.4 1.0 slice.56
  499.6 1.9 reshape.184
  501.7 1.0 reshape.185
  503.1 0.9 reshape.181
  (89 shorter events, 9.7 us)
Async XLA Ops:
  7.2 8.6 %copy-start = (bf16[512,64]{0,1:T(8,128)(2,1)S(1)}, bf16[512,64]{0,1:T(8,128)(2,1)}, u32[]{:S(2)}) copy-start(bf16[512,64]{0,1:T(8,128)(2,1)} %param.17) | copy-start | bytes 196612
  7.2 5.8 %copy-start.11 = (bf16[64,2,1312]{2,1,0:T(2,128)(2,1)S(1)}, bf16[64,2,1312]{2,1,0:T(2,128)(2,1)}, u32[]{:S(2)}) copy-start(bf16[64,2,1312]{2,1,0:T(2,128)(2,1)} %param.18) | copy-start | bytes 1007620
  7.2 94.2 %all-gather.13.cloned.1.call-start = ((), (), s32[]{:S(2)}) async-start(), calls=%async_computation.4 | async-start | bytes 2621440 | tf_op jit(solution)/shard_map/all_gather | solution.py:553
  8.9 6.4 %copy-start.12 = (bf16[64,3,512]{2,0,1:T(8,128)(2,1)S(1)}, bf16[64,3,512]{2,0,1:T(8,128)(2,1)}, u32[]{:S(2)}) copy-start(bf16[64,3,512]{2,0,1:T(8,128)(2,1)} %param.16) | copy-start | bytes 589828
  10.3 5.5 %copy-start.14 = (bf16[1312,64]{0,1:T(8,128)(2,1)S(1)}, bf16[1312,64]{0,1:T(8,128)(2,1)}, u32[]{:S(2)}) copy-start(bf16[1312,64]{0,1:T(8,128)(2,1)} %param.19) | copy-start | bytes 503812
  11.7 4.4 copy-start.18
  11.7 4.4 copy-start.19
  16.1 85.4 %copy-start.17 = (s32[2,4]{1,0:T(2,128)S(1)}, s32[2,4]{1,0:T(2,128)}, u32[]{:S(2)}) copy-start(s32[2,4]{1,0:T(2,128)} %param.12) | copy-start | bytes 100
  17.8 0.6 copy-start.15
  61.7 43.6 %copy-start.13 = (bf16[4,64,384]{2,1,0:T(8,128)(2,1)S(1)}, bf16[4,64,384]{2,1,0:T(8,128)(2,1)}, u32[]{:S(2)}) copy-start(bf16[4,64,384]{2,1,0:T(8,128)(2,1)} %get-tuple-element.39) | copy-start | bytes 589828
  61.7 78.8 %all-gather.9.cloned.1.call-start = ((), (), s32[]{:S(2)}) async-start(), calls=%async_computation.2 | async-start | bytes 1310720 | tf_op jit(solution)/shard_map/all_gather | solution.py:539
  62.4 149.7 %all-gather.11.cloned.1.call-start = ((), (), s32[]{:S(2)}) async-start(), calls=%async_computation.3 | async-start | bytes 1966080 | tf_op jit(solution)/shard_map/all_gather | solution.py:539
  63.2 189.0 %all-gather.15.cloned.1.call-start = ((), (), s32[]{:S(2)}) async-start(), calls=%async_computation.5 | async-start | bytes 6291456 | tf_op jit(solution)/shard_map/all_gather | solution.py:552
  101.4 295.3 %all-gather.17.cloned.1.call-start = ((), (), s32[]{:S(2)}) async-start(), calls=%async_computation.8 | async-start | bytes 1572864 | tf_op jit(solution)/shard_map/all_gather | solution.py:605
  217.8 7.9 %copy-start.3 = (f32[2048,768]{1,0:T(8,128)}, f32[2048,768]{1,0:T(8,128)S(1)}, u32[]{:S(2)}) copy-start(f32[2048,768]{1,0:T(8,128)S(1)} %fusion.28) | copy-start | bytes 18874372
  260.1 1.2 copy-start.6
  260.1 1.7 copy-start.8
  333.9 44.4 %copy-start.10 = (bf16[2,1024,128]{2,1,0:T(8,128)(2,1)S(1)}, bf16[2,1024,128]{2,1,0:T(8,128)(2,1)}, u32[]{:S(2)}) copy-start(bf16[2,1024,128]{2,1,0:T(8,128)(2,1)} %get-tuple-element.33) | copy-start | bytes 1572868
  377.6 21.9 %all-gather.19.cloned.1.call-start = ((), (), s32[]{:S(2)}) async-start(), calls=%async_computation.9 | async-start | bytes 1572864 | tf_op jit(solution)/shard_map/all_gather | solution.py:606
  378.2 3.2 copy-start.2
  378.2 50.0 %reduce-scatter.3.cloned.1.call-start = ((), (), s32[]{:S(2)}) async-start(), calls=%async_computation.6 | async-start | bytes 1310720 | tf_op jit(solution)/shard_map/reduce_scatter | solution.py:585
  378.3 3.9 copy-start.5
  384.0 1.8 copy-start.4
  385.1 4.9 copy-start.7
  385.1 92.2 %reduce-scatter.5.cloned.1.call-start = ((), (), s32[]{:S(2)}) async-start(), calls=%async_computation.7 | async-start | bytes 2949120 | tf_op jit(solution)/shard_map/reduce_scatter | solution.py:572
  385.8 4.2 copy-start.9
  385.8 4.2 copy-start.20
  393.7 1.7 copy-start.16
  499.1 4.9 copy-start.1
Sparse Core Ops, SparseCore 0:
  61.8 39.5 all-gather.12
  102.9 37.5 all-gather.8
  142.1 35.6 all-gather.10
  179.2 13.1 all-gather.14
  377.8 8.1 all-gather.16
  387.4 10.1 all-gather.18
  399.9 28.2 reduce-scatter.2
  430.6 46.7 reduce-scatter.4

commit v2 on v0

v2 whole, which is shorter than its diff:
```python
import functools

import jax
import jax.numpy as jnp
from jax import lax
from jax.experimental import pallas as pl
from jax.experimental.pallas import tpu as pltpu
from jax.sharding import PartitionSpec as P

D = 1024
HEAD_DIM = 64
norm_eps = 1e-05
rope_base = 160000.0
masked_score = -1e30
MESH = pl.DeviceIdType.MESH
BF = jnp.bfloat16
F32 = jnp.float32
VLIMIT = 56 << 20


def nn(a, b):
    return lax.dot_general(a, b, (((1,), (0,)), ((), ())), preferred_element_type=F32)


def nt(a, b):
    return lax.dot_general(a, b, (((1,), (1,)), ((), ())), preferred_element_type=F32)


def tn(a, b):
    return lax.dot_general(a, b, (((0,), (0,)), ((), ())), preferred_element_type=F32)


def norm_stats(values):
    center = values - jnp.mean(values, axis=-1, keepdims=True)
    spread = jnp.mean(center * center, axis=-1, keepdims=True)
    inverse_std = lax.rsqrt(spread + norm_eps)
    return center * inverse_std, inverse_std


def norm_back(upstream, normed, inverse_std, gain):
    scaled = upstream * gain
    adjusted = (
        scaled
        - jnp.mean(scaled, axis=-1, keepdims=True)
        - normed * jnp.mean(scaled * normed, axis=-1, keepdims=True)
    )
    return adjusted * inverse_std


def here():
    return lax.axis_index("fsdp"), lax.axis_index("ctx"), lax.axis_index("tp")


def remote(src, dst, sems, i, where, j=None):
    return pltpu.make_async_remote_copy(
        src_ref=src,
        dst_ref=dst,
        send_sem=sems.at[0, i],
        recv_sem=sems.at[1, i if j is None else j],
        device_id=where,
        device_id_type=MESH,
    )


def greet(peers):
    bar = pltpu.get_barrier_semaphore()
    for p in peers:
        pl.semaphore_signal(bar, inc=1, device_id=p, device_id_type=MESH)
    pl.semaphore_wait(bar, len(peers))


class Ids:
    def __init__(self):
        self.next = 0

    def take(self, count):
        self.next += count
        return self.next - count


def each(copies, what):
    for copy in copies:
        getattr(copy, what)()


class Gather:
    def __init__(self, full, m, sems, ids):
        f, c, t = here()
        px, py, po = (f, c ^ 1, t), (f, c ^ 2, t), (f, c, 1 - t)
        cx, cy, cd = c ^ 1, c ^ 2, c ^ 3
        base = ids.take(10)

        def cp(i, view, where):
            return remote(view, view, sems, base + i, where)

        self.bx = cp(0, full.at[m, c, t, 1], px)
        self.ay = cp(1, full.at[m, c, t, 0], py)
        self.ax = cp(2, full.at[m, c, t, 0], px)
        self.by = cp(3, full.at[m, c, t, 1], py)
        self.oo = cp(4, full.at[m, c, t], po)
        self.fy = cp(5, full.at[m, cx, t, 1], py)
        self.fx = cp(6, full.at[m, cy, t, 0], px)
        self.ox = cp(7, full.at[m, cx, t], po)
        self.oy = cp(8, full.at[m, cy, t], po)
        self.od = cp(9, full.at[m, cd, t], po)

    def s0(self):
        each([self.bx, self.ay, self.ax, self.by, self.oo], "start")

    def s1(self):
        self.bx.wait_recv()
        self.fy.start()
        self.ay.wait_recv()
        self.fx.start()

    def s2(self):
        self.ax.wait_recv()
        self.ox.start()
        self.by.wait_recv()
        self.oy.start()

    def s3(self):
        self.fy.wait_recv()
        self.fx.wait_recv()
        self.od.start()

    def s4(self):
        each([self.oo, self.ox, self.oy, self.od], "wait_recv")

    def rest(self):
        self.s2()
        self.s3()
        self.s4()

    def end(self):
        each(
            [self.bx, self.ay, self.ax, self.by, self.oo, self.fy, self.fx, self.ox, self.oy,
             self.od],
            "wait_send",
        )


class Reduce:
    def __init__(self, part, r0, rx, ry, sems, ids):
        f, c, t = here()
        px, py, self.po = (f, c ^ 1, t), (f, c ^ 2, t), (f, c, 1 - t)
        cx, cy, cd = c ^ 1, c ^ 2, c ^ 3
        self.base = ids.take(10)
        self.part, self.r0, self.rx, self.ry, self.sems = part, r0, rx, ry, sems
        self.own, self.t, self.cx, self.cy, self.cd = c, t, cx, cy, cd

        def cp(i, src, dst, where):
            return remote(src, dst, sems, self.base + i, where)

        self.cross = [self.crossing(i) for i in range(4)]
        self.a0 = cp(4, part.at[cd, t, 0], rx.at[0], px)
        self.b0 = cp(5, part.at[cd, t, 1], ry.at[0], py)
        self.a1 = cp(6, part.at[cx, t, 0], rx.at[1], px)
        self.b1 = cp(7, part.at[cy, t, 1], ry.at[1], py)
        self.b2 = cp(8, part.at[cy, t, 0], ry.at[2], py)
        self.a2 = cp(9, part.at[cx, t, 1], rx.at[2], px)

    def span(self, i):
        return self.own ^ (3 - i - jnp.where(jnp.int32(i) == 1, 1, 0) + jnp.where(jnp.int32(i) == 2, 1, 0))

    def crossing(self, i):
        return remote(
            self.part.at[self.span(i), 1 - self.t], self.r0.at[i], self.sems, self.base + i, self.po
        )

    def add(self, i, span):
        self.cross[i].wait_recv()
        part, t = self.part, self.t
        part[span, t] = (part[span, t].astype(F32) + self.r0[i].astype(F32)).astype(BF)

    def s1(self):
        self.add(0, self.cd)
        self.a0.start()
        self.b0.start()

    def s2(self):
        self.add(1, self.cx)
        self.a1.start()
        self.add(2, self.cy)
        self.b1.start()

    def s3(self):
        part, t = self.part, self.t
        self.a0.wait_recv()
        part[self.cy, t, 0] = (part[self.cy, t, 0].astype(F32) + self.rx[0].astype(F32)).astype(BF)
        self.b2.start()
        self.b0.wait_recv()
        part[self.cx, t, 1] = (part[self.cx, t, 1].astype(F32) + self.ry[0].astype(F32)).astype(BF)
        self.a2.start()

    def s4(self):
        self.cross[3].wait_recv()
        own = self.part[self.own, self.t].astype(F32) + self.r0[3].astype(F32)
        each([self.a1, self.b1, self.b2, self.a2], "wait_recv")
        top = own[0] + self.rx[1].astype(F32) + self.ry[2].astype(F32)
        bottom = own[1] + self.ry[1].astype(F32) + self.rx[2].astype(F32)
        return jnp.concatenate([top, bottom], axis=0)

    def end(self):
        each(self.cross + [self.a0, self.b0, self.a1, self.b1, self.b2, self.a2], "wait_send")


def reduce_scratch(half):
    return [
        pltpu.VMEM((2, 4, 2, 2, half, D), BF),
        pltpu.VMEM((2, 4, 2, half, D), BF),
        pltpu.VMEM((2, 3, half, D), BF),
        pltpu.VMEM((2, 3, half, D), BF),
    ]


class Spread:
    def __init__(self, ref, n_f, sems, ids):
        f, c, t = here()
        self.f, self.n_f, self.ref = f, n_f, ref
        if n_f == 4:
            base = ids.take(5)
            self.steps = (-1, -2, 1, 2)
            self.copies = [
                remote(ref.at[f], ref.at[f], sems, base + i, (lax.rem(f - d + n_f, n_f), c, t))
                for i, d in enumerate(self.steps)
            ]
            self.far = remote(
                ref.at[jnp.where(f == 2, 0, 3)], ref.at[jnp.where(f == 2, 0, 3)], sems, base + 4,
                (jnp.where(f == 2, 3, 0), c, t),
            )
        else:
            base = ids.take(1)
            self.copies = [
                remote(ref.at[f], ref.at[f], sems, base, (lax.rem(f + k, n_f), c, t))
                for k in range(1, n_f)
            ]
            most = ref.at[pl.ds(0, n_f - 1)]
            self.all = remote(most, most, sems, base, (f, c, 1 - t))

    def start(self):
        if self.n_f != 4:
            return each(self.copies, "start")
        for d, cp in zip(self.steps, self.copies):
            pl.when((self.f - d >= 0) & (self.f - d < 4))(cp.start)

    def relay(self):
        if self.n_f != 4:
            return

        @pl.when(self.f == 2)
        def _():
            self.copies[1].wait_recv()
            self.far.start()

        @pl.when(self.f == 1)
        def _():
            self.copies[3].wait_recv()
            self.far.start()

    def wait(self):
        if self.n_f != 4:
            return self.all.wait_recv()
        f = self.f
        pl.when(f >= 1)(self.copies[0].wait_recv)
        pl.when(f == 3)(self.copies[1].wait_recv)
        pl.when(f <= 2)(self.copies[2].wait_recv)
        pl.when(f == 0)(self.copies[3].wait_recv)
        pl.when((f == 0) | (f == 3))(self.far.wait_recv)

    def end(self):
        if self.n_f != 4:
            return self.all.wait_send()
        for d, cp in zip(self.steps, self.copies):
            pl.when((self.f - d >= 0) & (self.f - d < 4))(cp.wait_send)
        pl.when((self.f == 1) | (self.f == 2))(self.far.wait_send)


class Collect:
    def __init__(self, ref, got, n_f, sems, ids):
        f, c, t = here()
        self.f, self.n_f, self.ref, self.got = f, n_f, ref, got
        if n_f == 4:
            base = ids.take(5)
            self.steps = (-1, -2, 1, 2)
            self.copies = []
            for i, d in enumerate(self.steps):
                j = lax.rem(f - d + n_f, n_f)
                self.copies.append(remote(ref.at[j], got.at[i], sems, base + i, (j, c, t)))
            away = jnp.where(f == 0, 3, 0)
            self.far = remote(
                ref.at[away], got.at[4], sems, base + 4, (jnp.where(f == 0, 1, 2), c, t)
            )
        else:
            base = ids.take(1)
            self.copies = []
            for k in range(1, n_f):
                j = lax.rem(f + k, n_f)
                self.copies.append(remote(ref.at[j], got.at[k - 1], sems, base, (j, c, t)))
            most = ref.at[pl.ds(0, n_f - 1)]
            self.all = remote(most, got, sems, base, (f, c, 1 - t))

    def there(self, d):
        return (self.f - d >= 0) & (self.f - d < 4)

    def late(self, d):
        if d == 2:
            return self.f == 2
        if d == -2:
            return self.f == 1
        return self.f < 0

    def start(self):
        if self.n_f != 4:
            return each(self.copies, "start")
        pl.when((self.f == 0) | (self.f == 3))(self.far.start)
        for d, cp in zip(self.steps, self.copies):
            pl.when(self.there(d) & ~self.late(d))(cp.start)

    def relay(self):
        if self.n_f != 4:
            return
        for d, cp, j in ((2, self.copies[3], 0), (-2, self.copies[1], 3)):

            @pl.when(self.late(d))
            def _():
                self.far.wait_recv()
                self.ref[j] = (self.ref[j].astype(F32) + self.got[4].astype(F32)).astype(BF)
                cp.start()

    def total(self, acc):
        acc[...] = self.ref[self.f].astype(F32)
        if self.n_f != 4:
            self.all.wait_recv()
            for k in range(self.n_f - 1):
                acc[...] += self.got[k].astype(F32)
            return
        for i, d in enumerate(self.steps):

            @pl.when((self.f + d >= 0) & (self.f + d < 4))
            def _():
                self.copies[i].wait_recv()
                acc[...] += self.got[i].astype(F32)

    def end(self):
        if self.n_f != 4:
            return self.all.wait_send()
        for d, cp in zip(self.steps, self.copies):
            pl.when(self.there(d))(cp.wait_send)
        pl.when((self.f == 0) | (self.f == 3))(self.far.wait_send)


def collect_slots(n_f):
    return 5 if n_f == 4 else n_f - 1


class Deal:
    def __init__(self, stage, own, n_f, sems, ids):
        f, c, t = here()
        n_h = n_f // 2
        self.base = ids.take(2 * n_f)
        self.f, self.t, self.n_h, self.own, self.sems = f, t, n_h, own, sems
        side, at = f // n_h, lax.rem(f, n_h)
        recv = self.base + t * n_h + at
        self.away = [
            remote(stage.at[lax.rem(f + k, n_f)], own.at[t, at], sems, self.base + k,
                   (lax.rem(f + k, n_f), c, side), recv)
            for k in range(1, n_f)
        ]
        self.over = remote(stage.at[f], own.at[t, at], sems, self.base, (f, c, 1 - t), recv)
        self.keep = pltpu.make_async_copy(stage.at[f], own.at[t, at], sems.at[1, recv])
        self.mine = side == t

    def start(self):
        each(self.away, "start")
        pl.when(self.mine)(self.keep.start)
        pl.when(~self.mine)(self.over.start)

    def wait(self, m):
        for j in range(self.n_h):
            i = self.base + m * self.n_h + j
            view = self.own.at[m, j]
            local = (self.t == m) & (self.f == self.t * self.n_h + j)
            f, c, t = here()
            pl.when(local)(pltpu.make_async_copy(view, view, self.sems.at[1, i]).wait)
            pl.when(~local)(remote(view, view, self.sems, i, (f, c, 1 - t)).wait_recv)

    def end(self):
        each(self.away, "wait_send")
        pl.when(~self.mine)(self.over.wait_send)


class Return:
    def __init__(self, own, back, other, n_f, sems, ids):
        f, c, t = here()
        n_h = n_f // 2
        self.base = ids.take(2 * n_f + 1)
        self.f, self.t, self.n_f, self.back, self.sems = f, t, n_f, back, sems
        self.moves = []
        for m in range(2):
            for j in range(n_h):
                to = t * n_h + j
                i = self.base + m * n_h + j
                far = remote(own.at[m, j], back.at[f], sems, i, (to, c, m), self.base + f)
                keep = pltpu.make_async_copy(own.at[m, j], back.at[f], sems.at[1, self.base + f])
                self.moves.append((m, (to == f) & (t == m), far, keep))
        self.swap = remote(back, other, sems, self.base + 2 * n_f, (f, c, 1 - t))

    def start(self, m):
        for which, local, far, keep in self.moves:
            if which == m:
                pl.when(local)(keep.start)
                pl.when(~local)(far.start)

    def wait(self):
        n_h = self.n_f // 2
        f, c, t = here()
        for s in range(self.n_f):
            local = (f == s) & (f // n_h == t)
            view = self.back.at[s]
            i = self.base + s
            pl.when(local)(pltpu.make_async_copy(view, view, self.sems.at[1, i]).wait)
            pl.when(~local)(remote(view, view, self.sems, i, (f, c, 1 - t)).wait_recv)
        self.swap.start()

    def end(self):
        self.swap.wait_recv()
        for _, local, far, _ in self.moves:
            pl.when(~local)(far.wait_send)
        self.swap.wait_send()


class Swap:
    def __init__(self, src, dst, sems, ids):
        f, c, t = here()
        base = ids.take(3)
        self.src, self.dst, self.c = src, dst, c
        self.copies = [
            remote(src.at[c ^ k], dst.at[c], sems, base + k - 1, (f, c ^ k, t)) for k in (1, 2, 3)
        ]

    def start(self):
        each(self.copies, "start")

    def keep(self):
        self.dst[self.c] = self.src[self.c]

    def wait(self):
        each(self.copies, "wait_recv")

    def end(self):
        each(self.copies, "wait_send")


def everyone(n_f):
    f, c, t = here()
    peers = [(f, c ^ 1, t), (f, c ^ 2, t), (f, c ^ 3, t), (f, c, 1 - t)]
    for k in range(1, n_f):
        for core in range(2):
            peers.append((lax.rem(f + k, n_f), c, core))
    return peers


def vm():
    return pl.BlockSpec(memory_space=pltpu.VMEM)


def sm():
    return pl.BlockSpec(memory_space=pltpu.SMEM)


def hb():
    return pl.BlockSpec(memory_space=pl.ANY)


def shaped(shape, dtype):
    return jax.ShapeDtypeStruct(shape, dtype)


def comm_call(kernel, outs, ins, scratch, n_sems, n_local, cid, flops):
    return pl.pallas_call(
        kernel,
        out_shape=[s for s, _ in outs],
        in_specs=ins,
        out_specs=[b for _, b in outs],
        scratch_shapes=scratch
        + [pltpu.SemaphoreType.DMA((2, n_sems)), pltpu.SemaphoreType.DMA((n_local,))],
        compiler_params=pltpu.CompilerParams(
            collective_id=cid, has_side_effects=True, vmem_limit_bytes=VLIMIT
        ),
        cost_estimate=pl.CostEstimate(flops=flops, bytes_accessed=1 << 20, transcendentals=0),
    )


def rotate(u, cos, sin, sign):
    lane = lax.broadcasted_iota(jnp.int32, u.shape, 1)
    partner = jnp.where(lane % HEAD_DIM < HEAD_DIM // 2, pltpu.roll(u, 96, 1), pltpu.roll(u, 32, 1))
    return u * cos + partner * (sin * sign)


def first_kernel(
    n_f, order, live, tok, cot, gains, pq, po, p2, p3, cos, sin,
    tok_o, cot_o, gains_o, wq, wo, w2, q3, first_h, cot_h, q_o, k_o, v_o, mixed_o, out_o, lse_o,
    hidden_o, second_o,
    stok, scot, gz, gp, first, cotf, part, r0, rx, ry, v_t, sems, lsem,
):
    f, c, t = here()
    ids = Ids()
    plane = [(f, c ^ k, t) for k in (1, 2, 3)]
    zs = [(lax.rem(f + k, n_f), c, t) for k in range(1, n_f)]
    half = first.shape[4]
    rows = 4 * 2 * 2 * half

    deal_tok = Deal(stok, tok_o, n_f, sems, ids)
    deal_cot = Deal(scot, cot_o, n_f, sems, ids)
    base = ids.take(n_f - 1)
    gs = [remote(gains, gz.at[f], sems, base + k, zs[k]) for k in range(n_f - 1)]
    base = ids.take(3)
    gps = [remote(gp.at[c], gp.at[c], sems, base + k, plane[k]) for k in range(3)]
    swaps = [Swap(src, dst, sems, ids)
             for src, dst in ((pq, wq.at[f]), (po, wo.at[f]), (p2, w2.at[f]), (p3, q3))]
    spreads = [Spread(w, n_f, sems, ids) for w in (wq, wo, w2)]
    g1 = [Gather(first, m, sems, ids) for m in range(2)]
    gc = [Gather(cotf, m, sems, ids) for m in range(2)]
    red = [Reduce(part.at[m], r0.at[m], rx.at[m], ry.at[m], sems, ids) for m in range(2)]
    local = [pltpu.make_async_copy(first, first_h, lsem.at[0]),
             pltpu.make_async_copy(cotf, cot_h, lsem.at[1])]

    for j in range(n_f):
        stok[j] = tok[t, order[t, j]]
    greet(everyone(n_f))
    each(gs, "start")
    deal_tok.start()
    each(swaps, "start")
    each(swaps, "keep")
    for j in range(n_f):
        scot[j] = cot[t, order[t, j]]
    gz[f] = gains[...]
    each(gs, "wait_recv")
    gp[c] = jnp.sum(gz[...], axis=0)
    each(gps, "start")
    swaps[0].wait()
    spreads[0].start()
    each(gps, "wait_recv")
    gains_o[...] = jnp.sum(gp[...], axis=0)

    def norm1(m):
        deal_tok.wait(m)
        hat, _ = norm_stats(tok_o[m].reshape(-1, D).astype(F32))
        first[m, c, t] = (hat * gains_o[0:1, :]).astype(BF).reshape(2, half, D)

    norm1(0)
    g1[0].s0()
    norm1(1)
    spreads[0].relay()
    g1[0].s1()
    g1[1].s0()
    swaps[1].wait()
    spreads[1].start()
    deal_cot.start()
    g1[0].s2()
    g1[0].s3()
    swaps[2].wait()
    spreads[2].start()
    g1[0].s4()
    spreads[0].wait()

    def attend(m, hooks):
        joined = nn(first[m].reshape(rows, D), wq[...].reshape(D, -1))
        q_o[m] = rotate(joined[:, 0:128], cos[...], sin[...], 1.0).astype(BF) * BF(0.125)
        k_o[m] = rotate(joined[:, 128:256], cos[...], sin[...], 1.0).astype(BF)
        v = joined[:, 256:384]
        v_o[m] = v.astype(BF)
        v_t[...] = v.T.astype(BF)
        lane = lax.broadcasted_iota(jnp.int32, (rows, 128), 1)
        alive = lax.broadcasted_iota(jnp.int32, (rows, rows), 0) < live[m]

        def head(h, carry):
            at = pl.ds(pl.multiple_of(h * HEAD_DIM, HEAD_DIM), HEAD_DIM)
            qh = jnp.where(lane // HEAD_DIM == h, q_o[m], BF(0.0))
            s = jnp.where(alive, nt(k_o[m], qh), masked_score)
            top = jnp.max(s, axis=0, keepdims=True)
            p = jnp.exp(s - top)
            total = jnp.sum(p, axis=0, keepdims=True)
            out_o[m, at, :] = nn(v_t[at, :], p.astype(BF)) / total
            lse_o[m, pl.ds(h, 1), :] = top + jnp.log(total)
            for i, hook in enumerate(hooks):
                pl.when(h == i)(hook)
            return carry

        lax.fori_loop(0, 2, head, 0)
        mixed_o[m] = out_o[m].T.astype(BF)

    def product(m):
        def step(i, carry):
            span = red[m].span(i)
            block = mixed_o[m, pl.ds(pl.multiple_of(span * 4 * half, 4 * half), 4 * half), :]
            part[m, span] = nt(block, wo[...].reshape(D, -1)).astype(BF).reshape(2, 2, half, D)
            red[m].crossing(i).start()
            return carry

        lax.fori_loop(0, 4, step, 0)

    def norm2(m):
        hidden = tok_o[m].reshape(-1, D).astype(F32) + red[m].s4()
        hidden_o[m] = hidden
        hat, _ = norm_stats(hidden)
        second_o[m] = (hat * gains_o[1:2, :]).astype(BF).reshape(2, half, D)

    g1[1].s1()

    def hook0():
        g1[1].s2()
        spreads[1].relay()

    attend(0, (hook0, g1[1].s3))
    g1[1].s4()
    local[0].start()
    spreads[1].wait()
    product(0)
    red[0].s1()
    deal_cot.wait(0)
    deal_cot.wait(1)
    for m in range(2):
        cotf[m, c, t] = cot_o[m].reshape(2, half, D)
    red[0].s2()

    def hook1():
        red[0].s3()
        gc[0].s0()

    def hook2():
        spreads[2].relay()

    attend(1, (hook1, hook2))
    product(1)
    red[1].s1()
    red[1].s2()
    norm2(0)
    red[1].s3()
    gc[0].s1()
    gc[1].s0()
    gc[0].s2()
    gc[0].s3()
    norm2(1)
    gc[1].s1()
    gc[1].rest()
    gc[0].s4()
    local[1].start()
    swaps[3].wait()
    spreads[2].wait()
    each(gs + gps, "wait_send")
    for x in [deal_tok, deal_cot] + swaps + spreads + g1 + gc + red:
        x.end()
    each(local, "wait")


def second_kernel(
    n_f, second, w2, q3, cot_h, cot_own, hidden, gains,
    hg_o, attn_o, act_o, gain_o, w3, gi_o, gd_o,
    full, cotf, gg, gd, got, acc, part, r0, rx, ry, sems, lsem,
):
    f, c, t = here()
    ids = Ids()
    half = full.shape[4]
    hp = w3.shape[3]
    rows = 16 * half
    g2 = [Gather(full, m, sems, ids) for m in range(2)]
    red = [Reduce(part.at[m], r0.at[m], rx.at[m], ry.at[m], sems, ids) for m in range(2)]
    spread = Spread(w3, n_f, sems, ids)
    collect = Collect(gd, got, n_f, sems, ids)
    load = pltpu.make_async_copy(cot_h, cotf, lsem.at[0])
    load.start()
    w3[f] = q3[...]
    for m in range(2):
        full[m, c, t] = second[m]
    greet(everyone(n_f))
    g2[0].s0()
    spread.start()
    g2[0].s1()
    g2[1].s0()
    spread.relay()
    g2[0].rest()
    load.wait()
    spread.wait()
    g2[1].s1()

    def mlp(m, hooks):
        def step(i, carry):
            span = red[m].span(i)
            low = full[m, span].reshape(4 * half, D)
            win = w2[...].reshape(D, 2 * hp)
            u = nn(low, win[:, :hp])
            g = nn(low, win[:, hp:])
            a = nn(cotf[m, span].reshape(4 * half, D), w3[...].reshape(D, hp))
            phi = 0.5 * (1.0 + lax.erf(u * 0.7071067811865476))
            gelu = u * phi
            slope = phi + u * (jnp.exp(-0.5 * u * u) * 0.3989422804014327)
            act_o[m, span] = (gelu * g).astype(BF)
            gg[m, span, :, 0:hp] = (a * g * slope).astype(BF)
            gg[m, span, :, hp:] = (a * gelu).astype(BF)
            part[m, span] = nt(gg[m, span], win).astype(BF).reshape(2, 2, half, D)
            red[m].crossing(i).start()
            for j, hook in enumerate(hooks):
                pl.when(i == j)(hook)
            return carry

        lax.fori_loop(0, 4, step, 0)

    mlp(0, (g2[1].s2, g2[1].s3))
    red[0].s1()
    g2[1].s4()
    mlp(1, (red[0].s2, red[0].s3))
    red[1].s1()
    flat_act = act_o[...].reshape(2 * rows, hp)
    flat_gg = gg[...].reshape(2 * rows, 2 * hp)
    n_d = 256

    def down(b, carry):
        x = cotf[:, :, :, :, :, pl.ds(pl.multiple_of(b * n_d, n_d), n_d)].reshape(2 * rows, n_d)
        blk = n_d // gd.shape[1] if gd.shape[1] < n_d else 1
        gd_view = tn(x, flat_act).astype(BF)
        if gd.shape[1] == n_d:
            gd[b] = gd_view
        else:
            gd[pl.ds(b * blk, blk)] = gd_view.reshape(blk, gd.shape[1], hp)
        return carry

    lax.fori_loop(0, D // n_d, down, 0)
    collect.start()
    red[1].s2()

    def norm3(m):
        grad = red[m].s4()
        hat, inv = norm_stats(hidden[m])
        hg = cot_own[m].reshape(-1, D).astype(F32) + norm_back(grad, hat, inv, gains[1:2, :])
        hg_o[m] = hg
        attn_o[m] = hg.astype(BF).reshape(2, half, D)
        return jnp.sum(grad * hat, axis=0, keepdims=True)

    gain = norm3(0)
    red[1].s3()

    def inner(b, carry):
        x = full[:, :, :, :, :, pl.ds(pl.multiple_of(b * n_d, n_d), n_d)].reshape(2 * rows, n_d)
        gi_o[pl.ds(pl.multiple_of(b * n_d, n_d), n_d), :] = tn(x, flat_gg).astype(BF)
        return carry

    lax.fori_loop(0, D // n_d, inner, 0)
    collect.relay()
    gain = gain + norm3(1)
    gain_o[...] = jnp.broadcast_to(gain, gain_o.shape)
    collect.total(acc)
    gd_o[...] = acc[...].astype(BF)
    for x in g2 + red + [spread, collect]:
        x.end()


def third_kernel(
    n_f, owners, live, attn, wo, wq, w3, act, q, k, v, mixed, out, lse, first_h, hg, hidden, tok,
    gains, gain2, gi, gd, cos, sin,
    out_o, grad_o, gain_o, share_o,
    full, first, dk, dv, dq_t, mg, delta, k_t, joined, part, r0, rx, ry, r0b, rxb, ryb,
    gl, gotl, gotg, accl, accg, ssend, orow, grow, oback, gback, oother, gother, gz, gp, gt,
    sems, lsem,
):
    f, c, t = here()
    ids = Ids()
    half = full.shape[4]
    rows = 16 * half
    hp = w3.shape[3]
    nl, ng = accl.shape[1], accg.shape[1]
    plane = [(f, c ^ k_, t) for k_ in (1, 2, 3)]
    zs = [(lax.rem(f + k_, n_f), c, t) for k_ in range(1, n_f)]
    po = (f, c, 1 - t)
    g3 = [Gather(full, m, sems, ids) for m in range(2)]
    red4 = [Reduce(part.at[m], r0.at[m], rx.at[m], ry.at[m], sems, ids) for m in range(2)]
    red3 = [Reduce(part.at[m], r0b.at[m], rxb.at[m], ryb.at[m], sems, ids) for m in range(2)]
    collect_g = Collect(gi, gotg, n_f, sems, ids)
    collect_l = Collect(gl, gotl, n_f, sems, ids)
    ret_o = Return(orow, oback, oother, n_f, sems, ids)
    ret_g = Return(grow, gback, gother, n_f, sems, ids)
    swap = Swap(ssend, share_o, sems, ids)
    base = ids.take(1 + 3 + n_f - 1)
    s0 = remote(gt.at[0], gt.at[1], sems, base, po)
    gps = [remote(gp.at[c], gp.at[c], sems, base + 1 + j, plane[j]) for j in range(3)]
    gzs = [remote(gz.at[f], gz.at[f], sems, base + 4 + j, zs[j]) for j in range(n_f - 1)]
    load = pltpu.make_async_copy(first_h, first, lsem.at[0])
    load.start()
    for m in range(2):
        full[m, c, t] = attn[m]
    greet(everyone(n_f))
    g3[0].s0()
    collect_g.start()

    def product(red, m, source, weight):
        def step(i, carry):
            span = red[m].span(i)
            part[m, span] = nt(source(m, span), weight()).astype(BF).reshape(2, 2, half, D)
            red[m].crossing(i).start()
            return carry

        lax.fori_loop(0, 4, step, 0)

    def act_rows(m, span):
        return act[m, span]

    def joined_rows(m, span):
        return joined[m, pl.ds(pl.multiple_of(span * 4 * half, 4 * half), 4 * half), :]

    g3[0].s1()
    g3[1].s0()
    product(red4, 0, act_rows, lambda: w3[...].reshape(D, hp))
    product(red4, 1, act_rows, lambda: w3[...].reshape(D, hp))
    g3[0].rest()
    collect_g.relay()
    QB = 512

    def attend_back(m, hooks):
        grad = nn(full[m].reshape(rows, D), wo[...].reshape(D, -1)).astype(BF)
        mg[...] = grad
        weighted = grad.astype(F32).T * out[m]
        delta[0:1, :] = jnp.sum(weighted[:HEAD_DIM], axis=0, keepdims=True)
        delta[1:2, :] = jnp.sum(weighted[HEAD_DIM:], axis=0, keepdims=True)
        k_t[...] = k[m].astype(F32).T.astype(BF)
        dk[...] = jnp.zeros_like(dk)
        dv[...] = jnp.zeros_like(dv)
        lane = lax.broadcasted_iota(jnp.int32, (QB, 128), 1)
        alive = lax.broadcasted_iota(jnp.int32, (rows, QB), 0) < live[m]
        n_b = rows // QB

        def block(i, carry):
            h = i // n_b
            at = pl.ds(pl.multiple_of(lax.rem(i, n_b) * QB, QB), QB)
            hs = pl.ds(pl.multiple_of(h * HEAD_DIM, HEAD_DIM), HEAD_DIM)
            keep = lane // HEAD_DIM == h
            qh = jnp.where(keep, q[m, at, :], BF(0.0))
            gh = jnp.where(keep, mg[at, :], BF(0.0))
            s = nt(k[m], qh)
            p = jnp.where(alive, jnp.exp(s - lse[m, pl.ds(h, 1), at]), 0.0)
            dp = nt(v[m], gh)
            ds = (p * (dp - delta[pl.ds(h, 1), at])).astype(BF)
            dv[...] += nn(p.astype(BF), gh)
            dk[...] += nn(ds, qh)
            dq_t[hs, at] = nn(k_t[hs, :], ds)
            for j, hook in enumerate(hooks):
                pl.when(i == j)(hook)
            return carry

        lax.fori_loop(0, 2 * n_b, block, 0)
        dq = dq_t[...].T * 0.125
        joined[m, :, 0:128] = rotate(dq, cos[...], sin[...], -1.0).astype(BF)
        joined[m, :, 128:256] = rotate(dk[...], cos[...], sin[...], -1.0).astype(BF)
        joined[m, :, 256:384] = dv[...].astype(BF)

    def nothing():
        pass

    def h0():
        g3[1].s1()
        red4[0].s1()

    def h1():
        g3[1].s2()
        red4[0].s2()

    def h2():
        g3[1].s3()
        red4[0].s3()

    def h3():
        red4[1].s1()

    attend_back(0, (h0, h1, h2, h3))
    g3[1].s4()

    def finish_out(m):
        rows_out = hidden[m] + red4[m].s4()
        orow[m] = rows_out.astype(BF).reshape(orow.shape[1:])
        ret_o.start(m)
        red4[m].end()

    finish_out(0)
    product(red3, 0, joined_rows, lambda: wq[...].reshape(D, -1))

    def k0():
        red4[1].s2()
        red3[0].s1()

    def k1():
        red4[1].s3()
        red3[0].s2()

    def k2():
        red3[0].s3()

    attend_back(1, (k0, k1, k2))
    finish_out(1)
    product(red3, 1, joined_rows, lambda: wq[...].reshape(D, -1))
    red3[1].s1()
    load.wait()
    flat_j = joined[...].reshape(2 * rows, -1)
    flat_m = mixed[...].reshape(2 * rows, -1)
    n_d = 256

    def late(b, carry):
        at = pl.ds(pl.multiple_of(b * n_d, n_d), n_d)
        x = first[:, :, :, :, :, at].reshape(2 * rows, n_d)
        y = full[:, :, :, :, :, at].reshape(2 * rows, n_d)
        gq = tn(x, flat_j).astype(BF)
        go = tn(y, flat_m).astype(BF)
        if gl.shape[1] == n_d:
            gl[b, :, 0:384] = gq
            gl[b, :, 384:512] = go
        else:
            blk = n_d // gl.shape[1]
            gl[pl.ds(b * blk, blk), :, 0:384] = gq.reshape(blk, gl.shape[1], 384)
            gl[pl.ds(b * blk, blk), :, 384:512] = go.reshape(blk, gl.shape[1], 128)
        return carry

    lax.fori_loop(0, D // n_d, late, 0)
    collect_l.start()
    red3[1].s2()

    def norm4(m):
        grad = red3[m].s4()
        hat, inv = norm_stats(tok[m].reshape(-1, D).astype(F32))
        new = hg[m] + norm_back(grad, hat, inv, gains[0:1, :])
        grow[m] = new.astype(BF).reshape(grow.shape[1:])
        ret_g.start(m)
        return jnp.sum(grad * hat, axis=0, keepdims=True)

    gain1 = norm4(0)
    red3[1].s3()
    collect_g.total(accg)
    collect_l.relay()
    gain1 = gain1 + norm4(1)
    row = lax.broadcasted_iota(jnp.int32, gain2.shape, 0)
    gt[0] = jnp.where(row == 0, gain1, jnp.where(row == 1, gain2[...], 0.0))
    s0.start()
    ret_o.wait()
    s0.wait_recv()
    gp[c] = gt[0] + gt[1]
    each(gps, "start")
    collect_l.total(accl)
    ssend[:, :, 0:nl] = accl[...].astype(BF).reshape(4, -1, nl)
    ssend[:, :, nl : nl + ng] = accg[...].astype(BF).reshape(4, -1, ng)
    ssend[:, :, nl + ng :] = gd[...].reshape(4, -1, hp)
    swap.start()
    each(gps, "wait_recv")
    gz[f] = jnp.sum(gp[...], axis=0)
    each(gzs, "start")
    swap.keep()
    ret_g.wait()
    ret_o.end()

    def unpack(dst, back, other):
        for s in range(n_f):
            dst[t, s] = back[owners[t, s]]
            dst[1 - t, s] = other[owners[1 - t, s]]

    unpack(out_o, oback, oother)
    each(gzs, "wait_recv")
    gain_o[...] = jnp.sum(gz[...], axis=0)
    ret_g.end()
    unpack(grad_o, gback, gother)
    swap.wait()
    each([s0] + gps + gzs, "wait_send")
    for x in g3 + red3 + [collect_g, collect_l, swap]:
        x.end()


def rope_tables(rows):
    lane = jnp.arange(128, dtype=jnp.int32)
    exponent = (2 * (lane % (HEAD_DIM // 2))).astype(F32)
    inverse = rope_base ** (-exponent / HEAD_DIM)
    angles = jnp.arange(rows, dtype=jnp.int32).astype(F32)[:, None] * inverse[None, :]
    sign = jnp.where(lane % HEAD_DIM < HEAD_DIM // 2, -1.0, 1.0)
    return jnp.cos(angles), jnp.sin(angles) * sign[None, :]


def per_device(n_f, n_c, n_t, tokens, cotangent, lengths, owners,
               norm_attn, norm_mlp, w_qkv, w_out, w_in, w_down):
    f, c, t = here()
    micro, seqs, _, piece, _ = tokens.shape
    assert n_c == 4 and n_t == 2 and micro == 2 and seqs == n_f
    span = piece * n_f
    half = span // 4
    rows = span * n_c
    n_h = n_f // 2
    wr = w_qkv.shape[0]
    hid = w_in.shape[2]
    hp = -(-hid // (n_c * 128)) * 128
    heads = w_qkv.shape[2] // n_c
    wb = n_c * wr

    order = jnp.argsort(owners, axis=1).astype(jnp.int32)
    live = lax.dynamic_index_in_dim(lengths, f, axis=1, keepdims=False)
    place = (f * n_c + c) * wr
    gains_own = jnp.stack([norm_attn, norm_mlp]).astype(F32)
    gains_row = lax.dynamic_update_slice(jnp.zeros((8, D), F32), gains_own, (0, place))

    def quarters(a):
        return a.transpose(2, 0, 1, 3).reshape(n_c, wr, -1)

    more = n_c * hp - hid
    p_qkv = quarters(w_qkv.reshape(wr, 3, n_c, heads))
    p_out = w_out.reshape(n_c, heads, wr).transpose(0, 2, 1)
    p_in = quarters(jnp.pad(w_in, [(0, 0), (0, 0), (0, more)]).reshape(wr, 2, n_c, hp))
    p_down = jnp.pad(w_down, [(0, more), (0, 0)]).reshape(n_c, hp, wr).transpose(0, 2, 1)
    n_q = 3 * heads
    cos, sin = rope_tables(rows)

    full_shape = (micro, n_c, 2, 2, half, D)
    own_shape = (micro, n_h, piece, D)
    row_shape = (micro, 2 * half, D)
    head_shape = (micro, rows, 128)
    V = pltpu.VMEM
    (tok, cot, gains, wq, wo, w2, q3, first_h, cot_h, q, k, v, mixed, out_t, lse, hidden,
     second) = comm_call(
        functools.partial(first_kernel, n_f),
        [
            (shaped(own_shape, BF), vm()), (shaped(own_shape, BF), vm()),
            (shaped((8, D), F32), vm()),
            (shaped((n_f, n_c, wr, n_q), BF), vm()), (shaped((n_f, n_c, wr, heads), BF), vm()),
            (shaped((n_f, n_c, wr, 2 * hp), BF), vm()), (shaped((n_c, wr, hp), BF), vm()),
            (shaped(full_shape, BF), hb()), (shaped(full_shape, BF), hb()),
        ]
        + [(shaped(head_shape, BF), vm())] * 4
        + [
            (shaped((micro, 128, rows), F32), vm()), (shaped((micro, 8, rows), F32), vm()),
            (shaped(row_shape, F32), vm()), (shaped((micro, 2, half, D), BF), vm()),
        ],
        [sm(), sm()] + [vm()] * 9,
        [
            V((n_f, piece, D), BF), V((n_f, piece, D), BF), V((n_f, 8, D), F32),
            V((n_c, 8, D), F32), V(full_shape, BF), V(full_shape, BF),
        ]
        + reduce_scratch(half)
        + [V((128, rows), BF)],
        5 * n_f + 120, 2, 0, 10**10,
    )(order, live, tokens[:, :, 0], cotangent[:, :, 0], gains_row, p_qkv, p_out, p_in, p_down,
      cos, sin)

    hg, attn, act, gain2, w3, g_in, g_down = comm_call(
        functools.partial(second_kernel, n_f),
        [
            (shaped(row_shape, F32), vm()), (shaped((micro, 2, half, D), BF), vm()),
            (shaped((micro, n_c, span, hp), BF), vm()), (shaped((8, D), F32), vm()),
            (shaped((n_f, n_c, wr, hp), BF), vm()),
            (shaped((D, 2 * hp), BF), vm()), (shaped((wb, hp), BF), vm()),
        ],
        [vm(), vm(), vm(), hb()] + [vm()] * 3,
        [
            V(full_shape, BF), V(full_shape, BF), V((micro, n_c, span, 2 * hp), BF),
            V((n_f, wb, hp), BF), V((collect_slots(n_f), wb, hp), BF), V((wb, hp), F32),
        ]
        + reduce_scratch(half),
        n_f + 60, 1, 1, 10**10,
    )(second, w2, q3, cot_h, cot, hidden, gains)

    outs, grads, gain_grads, shares = comm_call(
        functools.partial(third_kernel, n_f),
        [
            (shaped((micro, n_f, piece, D), BF), vm()), (shaped((micro, n_f, piece, D), BF), vm()),
            (shaped((8, D), F32), vm()), (shaped((n_c, wr, n_q + heads + 3 * hp), BF), vm()),
        ],
        [sm(), sm()] + [vm()] * 11 + [hb()] + [vm()] * 9,
        [
            V(full_shape, BF), V(full_shape, BF), V((rows, 128), F32), V((rows, 128), F32),
            V((128, rows), F32), V((rows, 128), BF), V((8, rows), F32), V((128, rows), BF),
            V((micro, rows, 384), BF),
        ]
        + reduce_scratch(half)
        + reduce_scratch(half)[1:]
        + [
            V((n_f, wb, n_q + heads), BF),
            V((collect_slots(n_f), wb, n_q + heads), BF), V((collect_slots(n_f), wb, 2 * hp), BF),
            V((wb, n_q + heads), F32), V((wb, 2 * hp), F32),
            V((n_c, wr, n_q + heads + 3 * hp), BF),
            V(own_shape, BF), V(own_shape, BF),
            V((n_f, piece, D), BF), V((n_f, piece, D), BF),
            V((n_f, piece, D), BF), V((n_f, piece, D), BF),
            V((n_f, 8, D), F32), V((n_c, 8, D), F32), V((2, 8, D), F32),
        ],
        6 * n_f + 100, 1, 2, 10**10,
    )(owners, live, attn, wo, wq, w3, act, q, k, v, mixed, out_t, lse, first_h, hg, hidden, tok,
      gains, gain2, g_in.reshape(n_f, wb, 2 * hp), g_down, cos, sin)

    shares = shares.astype(F32)
    n1, n2 = n_q + heads, n_q + heads + 2 * hp
    grad_qkv = shares[:, :, :n_q].reshape(n_c, wr, 3, heads).transpose(1, 2, 0, 3)
    grad_qkv = grad_qkv.reshape(wr, 3, n_c * heads)
    grad_out = shares[:, :, n_q:n1].transpose(0, 2, 1).reshape(n_c * heads, wr)
    grad_in = shares[:, :, n1:n2].reshape(n_c, wr, 2, hp)
    grad_in = grad_in.transpose(1, 2, 0, 3).reshape(wr, 2, n_c * hp)[..., :hid]
    grad_down = shares[:, :, n2:].transpose(0, 2, 1).reshape(n_c * hp, wr)[:hid]
    mine = lax.dynamic_slice(gain_grads, (0, place), (2, wr))
    return (outs[:, :, None], grads[:, :, None], mine[0], mine[1],
            grad_qkv, grad_out, grad_in, grad_down)


def solution(mesh):
    rows = P(None, None, "ctx", "fsdp", None)
    gain = P(("fsdp", "ctx"))
    tall = P(("fsdp", "ctx"), None, "tp")
    wide = P("tp", ("fsdp", "ctx"))
    return jax.shard_map(
        functools.partial(per_device, mesh.shape["fsdp"], mesh.shape["ctx"], mesh.shape["tp"]),
        mesh=mesh,
        in_specs=(rows, rows, P(), P(), gain, gain, tall, wide, tall, wide),
        out_specs=(rows, rows, gain, gain, tall, wide, tall, wide),
        check_vma=False,
    )
```

time: 1450 us -> 286 us (0.20)
  waiting for transfers between devices: 991 us -> 0 us
  Pallas kernels: 0 us -> 262 us
  matrix products: 131 us -> 0 us
  blocking collectives: 123 us -> 0 us
  local copies, waits for them, and re-layouts: 103 us -> 17.8 us
  other arithmetic: 59.4 us -> 4.47 us
  starting transfers between devices: 20.2 us -> 0 us
  between operations: 16.8 us -> 0.83 us
    reduce_scatter x7 -> x0, waiting for transfers between devices: 418 us -> none  [the longest x1 140 us: per_device(): lax.psum_scatter(grad_totals[2], ('fsdp', 'ctx'), scatter_dimension=0, ti...]
    pallas_call x0 -> x3, Pallas kernels: none -> 262 us  [the longest x1 105 us: per_device(): comm_call(functools.partial(first_kernel, n_f), [(shaped(own_shape, BF),...]
    all_gather x8 -> x0, waiting for transfers between devices: 256 us -> none  [the longest x1 75.1 us: per_device(): lax.all_gather(w_in, ('fsdp', 'ctx'), axis=0, tiled=True)]
    unnamed x20 -> x0, waiting for transfers between devices: 224 us -> none
    dot_general x52 -> x0, matrix products: 131 us -> none  [the longest x8 14.9 us: one_block(): jnp.einsum('qhd,khd->hqk', queries, key_block, preferred_element_type=jnp...]
    unnamed x2 -> x0, blocking collectives: 123 us -> none
    all_to_all x4 -> x0, waiting for transfers between devices: 74.6 us -> none  [the longest x1 50.2 us: per_device(): lax.all_to_all(stacked, 'fsdp', split_axis=3, concat_axis=1, tiled=True)]
    reduce_sum x13 -> x0, other arithmetic: 24.7 us -> none  [the longest x4 13.6 us: one_block(): row_total = row_total * rescale + jnp.sum(attn_probs, axis=-1)]
  transfers between devices with their start and end apart: 23 -> 0, of which waited for: 18 -> 0; matrix products, arithmetic and copies ran while one was open for 13% -> 0% of each run, Pallas kernels for 0% -> 0%
where the time goes in v2:
time: 286 us; the launch traced here: 285 us
  Pallas kernels  262 us (92%)
  local copies, waits for them, and re-layouts  17.8 us (6%)
  other arithmetic  4.47 us (2%)
    pallas_call x1, Pallas kernels, per_device(): comm_call(functools.partial(first_kernel, n_f), [(shaped(own_shape, BF),...  105 us
    pallas_call x1, Pallas kernels, per_device(): comm_call(functools.partial(third_kernel, n_f), [(shaped((micro, n_f, pie...  96.6 us
    pallas_call x1, Pallas kernels, per_device(): comm_call(functools.partial(second_kernel, n_f), [(shaped(row_shape, F32)...  61.1 us

profile of v2, /device:TPU:0, one launch (start us, length us, event | category | flops | bytes accessed | tf_op | source)
XLA Modules:
  0.0 285.4 jit_solution(10046874208719132920)
XLA Ops:
  0.6 0.0 copy-start
  0.6 0.0 copy-start.4
  0.7 1.4 dynamic-slice_reduce_fusion.live
  2.1 0.7 maximum_convert_fusion
  2.8 0.8 copy.35
  3.6 0.6 sort.17
  4.2 0.7 copy.40.order
  4.9 0.3 dynamic_update_slice.3.gains
  5.2 0.0 copy-done
  5.2 0.0 copy-start.5
  5.2 0.6 bitcast_bitcast_fusion.2.po
  5.8 1.0 reshape.84
  6.8 0.2 copy.59
  7.0 0.8 reshape.85.pq
  7.8 0.9 pad.9
  8.8 0.7 copy.60
  9.5 0.0 copy-done.4
  9.5 0.3 pad.8
  9.8 0.3 copy.58
  10.1 0.0 copy-done.5
  10.1 1.0 reshape.88.p2
  11.1 3.0 %fusion = (f32[1024,128]{1,0:T(8,128)}, f32[1024,128]{1,0:T(8,128)}) fusion(f32[128]{0:T(128)S(1)} %get-tuple-element.94, f32[128]{0:T(128)S(1)} %get-tuple-element.95, f32[1024]{0:T(1024)S(1)} %iota_convert_fusion), kind=kLoop, calls=%fused_computation.2 | loop fusion | flops 262144 | bytes 1053696 | tf_op jit(solution)/shard_map/mul | solution.py:979
  14.1 104.6 %shard_map.161 = (bf16[2,2,64,1024]{3,2,1,0:T(8,128)(2,1)}, bf16[2,2,64,1024]{3,2,1,0:T(8,128)(2,1)}, f32[8,1024]{1,0:T(8,128)}, bf16[4,4,64,384]{3,2,1,0:T(8,12...) custom-call(s32[2,4]{1,0:T(2,128)} %copy.40.order, ...), custom_call_target="tpu_custom_call" | custom-call | flops 10000000000 | bytes 1048576 | tf_op jit(solution)/shard_map/pallas_call | solution.py:1020
  118.7 61.1 %shard_map.162 = (f32[2,128,1024]{2,1,0:T(8,128)}, bf16[2,2,64,1024]{3,2,1,0:T(8,128)(2,1)}, bf16[2,4,256,384]{3,2,1,0:T(8,128)(2,1)}, f32[8,1024]{1,0:T(8,128)}...) custom-call(bf16[2,2,64,1024]{3,2,1,0:T(8,128)(2,1)} %get-tuple-element.38.second, ...), custom_call_target="tpu_custom_call" | custom-call | flops 10000000000 | bytes 1048576 | tf_op jit(solution)/shard_map/pallas_call | solution.py:1045
  179.8 96.6 %shard_map.163 = (bf16[2,4,64,1024]{3,2,1,0:T(8,128)(2,1)}, bf16[2,4,64,1024]{3,2,1,0:T(8,128)(2,1)}, f32[8,1024]{1,0:T(8,128)}, bf16[4,64,1664]{2,1,0:T(8,128)(2,1)}) custom-call(s32[2,4]{1,0:T(2,128)} %owners.1, s32[2]{0:T(128)} %dynamic-slice_reduce_fusion.live, bf16[2,2,64,1024]{3,2,1,0:T(8,128)(2,1)} %get-tuple-element.45.attn, ...), custom_call_target="tpu_custom_call" | custom-call | flops 10000000000 | bytes 1048576 | tf_op jit(solution)/shard_map/pallas_call | solution.py:1062
  276.4 0.8 constant_dynamic-slice_fusion
  277.2 0.5 slice_bitcast_fusion.2
  277.7 0.0 copy-start.1
  277.7 1.0 slice.32
  278.7 0.2 reshape.91
  278.9 0.3 copy.41
  279.2 0.9 reshape.92
  280.1 0.0 copy-done.1
  280.1 0.1 slice.34
  280.1 0.4 reshape.94
  280.6 0.3 copy.51
  280.8 0.9 slice.35
  281.8 0.1 convert_element_type.39
  281.9 0.0 copy-start.3
  281.9 0.7 copy_bitcast_fusion.1
  282.6 0.0 copy-start.2
  282.6 0.8 slice.37
  283.4 0.0 copy-done.3
  283.4 1.0 copy.64
  284.4 0.0 copy-done.2
  284.4 1.0 copy.65
  (6 shorter events, 0.1 us)
Async XLA Ops:
  0.6 4.5 %copy-start = (bf16[512,64]{0,1:T(8,128)(2,1)S(1)}, bf16[512,64]{0,1:T(8,128)(2,1)}, u32[]{:S(2)}) copy-start(bf16[512,64]{0,1:T(8,128)(2,1)} %param.17) | copy-start | bytes 196612
  0.6 8.8 %copy-start.4 = (bf16[64,2,1312]{2,1,0:T(2,128)(2,1)S(1)}, bf16[64,2,1312]{2,1,0:T(2,128)(2,1)}, u32[]{:S(2)}) copy-start(bf16[64,2,1312]{2,1,0:T(2,128)(2,1)} %param.18) | copy-start | bytes 1007620
  5.2 4.9 %copy-start.5 = (f32[8,1024]{1,0:T(8,128)}, f32[8,1024]{1,0:T(8,128)S(1)}, u32[]{:S(2)}) copy-start(f32[8,1024]{1,0:T(8,128)S(1)} %dynamic_update_slice.3.gains) | copy-start | bytes 98308
  277.7 2.4 copy-start.1
  281.9 1.5 copy-start.3
  282.6 1.8 copy-start.2

commit v3 on v2

--- a/solution.py
+++ b/solution.py
@@ -277,8 +277,9 @@
 
 
 class Collect:
-    def __init__(self, ref, got, n_f, sems, ids):
+    def __init__(self, ref, got, n_f, sems, ids, passed=True):
         f, c, t = here()
+        n_f = n_f if passed or n_f != 4 else -n_f
         self.f, self.n_f, self.ref, self.got = f, n_f, ref, got
         if n_f == 4:
             base = ids.take(5)
@@ -294,11 +295,12 @@
         else:
             base = ids.take(1)
             self.copies = []
+            n_f = abs(n_f)
             for k in range(1, n_f):
                 j = lax.rem(f + k, n_f)
                 self.copies.append(remote(ref.at[j], got.at[k - 1], sems, base, (j, c, t)))
             most = ref.at[pl.ds(0, n_f - 1)]
-            self.all = remote(most, got, sems, base, (f, c, 1 - t))
+            self.all = remote(most, got.at[pl.ds(0, n_f - 1)], sems, base, (f, c, 1 - t))
 
     def there(self, d):
         return (self.f - d >= 0) & (self.f - d < 4)
@@ -332,7 +334,7 @@
         acc[...] = self.ref[self.f].astype(F32)
         if self.n_f != 4:
             self.all.wait_recv()
-            for k in range(self.n_f - 1):
+            for k in range(abs(self.n_f) - 1):
                 acc[...] += self.got[k].astype(F32)
             return
         for i, d in enumerate(self.steps):
@@ -359,35 +361,47 @@
         f, c, t = here()
         n_h = n_f // 2
         self.base = ids.take(2 * n_f)
-        self.f, self.t, self.n_h, self.own, self.sems = f, t, n_h, own, sems
-        side, at = f // n_h, lax.rem(f, n_h)
-        recv = self.base + t * n_h + at
-        self.away = [
-            remote(stage.at[lax.rem(f + k, n_f)], own.at[t, at], sems, self.base + k,
-                   (lax.rem(f + k, n_f), c, side), recv)
-            for k in range(1, n_f)
-        ]
-        self.over = remote(stage.at[f], own.at[t, at], sems, self.base, (f, c, 1 - t), recv)
-        self.keep = pltpu.make_async_copy(stage.at[f], own.at[t, at], sems.at[1, recv])
-        self.mine = side == t
-
-    def start(self):
-        each(self.away, "start")
-        pl.when(self.mine)(self.keep.start)
-        pl.when(~self.mine)(self.over.start)
+        self.f, self.t, self.n_f, self.n_h, self.own, self.sems = f, t, n_f, n_h, own, sems
+        self.side, at = f // n_h, lax.rem(f, n_h)
+        self.mine = self.side == t
+        self.moves = []
+        for m in range(2):
+            dst = self.piece(m, at, t)
+            recv = self.base + (m * n_h + at) * 2 + t
+            sent = self.base + m * n_f
+            away = [
+                remote(stage.at[m, lax.rem(f + k, n_f)], dst, sems, sent + k,
+                       (lax.rem(f + k, n_f), c, self.side), recv)
+                for k in range(1, n_f)
+            ]
+            over = remote(stage.at[m, f], dst, sems, sent, (f, c, 1 - t), recv)
+            keep = pltpu.make_async_copy(stage.at[m, f], dst, sems.at[1, recv])
+            self.moves.append((away, over, keep))
+
+    def piece(self, m, j, core):
+        wide = D // 2
+        return self.own.at[m, j, :, pl.ds(pl.multiple_of(core * wide, wide), wide)]
+
+    def start(self, m):
+        away, over, keep = self.moves[m]
+        each(away, "start")
+        pl.when(self.mine)(keep.start)
+        pl.when(~self.mine)(over.start)
 
     def wait(self, m):
+        f, c, t = here()
         for j in range(self.n_h):
-            i = self.base + m * self.n_h + j
-            view = self.own.at[m, j]
-            local = (self.t == m) & (self.f == self.t * self.n_h + j)
-            f, c, t = here()
-            pl.when(local)(pltpu.make_async_copy(view, view, self.sems.at[1, i]).wait)
-            pl.when(~local)(remote(view, view, self.sems, i, (f, c, 1 - t)).wait_recv)
+            for core in range(2):
+                i = self.base + (m * self.n_h + j) * 2 + core
+                view = self.piece(m, j, core)
+                local = (t == core) & (f == t * self.n_h + j)
+                pl.when(local)(pltpu.make_async_copy(view, view, self.sems.at[1, i]).wait)
+                pl.when(~local)(remote(view, view, self.sems, i, (f, c, 1 - t)).wait_recv)
 
     def end(self):
-        each(self.away, "wait_send")
-        pl.when(~self.mine)(self.over.wait_send)
+        for away, over, _ in self.moves:
+            each(away, "wait_send")
+            pl.when(~self.mine)(over.wait_send)
 
 
 class Return:
@@ -498,82 +512,117 @@
     return u * cos + partner * (sin * sign)
 
 
-def first_kernel(
-    n_f, order, live, tok, cot, gains, pq, po, p2, p3, cos, sin,
-    tok_o, cot_o, gains_o, wq, wo, w2, q3, first_h, cot_h, q_o, k_o, v_o, mixed_o, out_o, lse_o,
-    hidden_o, second_o,
-    stok, scot, gz, gp, first, cotf, part, r0, rx, ry, v_t, sems, lsem,
+class Keep:
+    def __init__(self, sems):
+        self.sems, self.copies = sems, []
+
+    def move(self, src, dst):
+        copy = pltpu.make_async_copy(src, dst, self.sems.at[len(self.copies)])
+        copy.start()
+        self.copies.append(copy)
+        return copy
+
+
+def table(small, dst):
+    fine_cos, fine_sin = small[2], small[3]
+    steps = fine_cos.shape[0]
+    for i in range(dst.shape[1] // steps):
+        coarse_cos, coarse_sin = small[0, i : i + 1, :], small[1, i : i + 1, :]
+        at = pl.ds(i * steps, steps)
+        dst[0, at, :] = coarse_cos * fine_cos - coarse_sin * fine_sin
+        dst[1, at, :] = (coarse_sin * fine_cos + coarse_cos * fine_sin) * small[4]
+
+
+def front_kernel(
+    n_f, order, lengths, tok, cot, gains, pq, po, p2, p3, small,
+    gains_o, tok_h, hidden_h, wq_h, wo_h, w3_h, q_h, k_h, v_h, mixed_h, out_h, lse_h, first_h,
+    act_h, hg_o, attn_o, gain_o, gi_o, gd_o,
+    tok_o, cot_o, hidden_o, wq, wo, w2, w3, q_o, k_o, v_o, mixed_o, out_o, lse_o, act_o,
+    stage, scot, gz, gp, first, cotf, full, gg, gd, got, acc, part, r0, rx, ry, v_t, turn,
+    sems, lsem,
 ):
     f, c, t = here()
     ids = Ids()
     plane = [(f, c ^ k, t) for k in (1, 2, 3)]
     zs = [(lax.rem(f + k, n_f), c, t) for k in range(1, n_f)]
     half = first.shape[4]
-    rows = 4 * 2 * 2 * half
-
-    deal_tok = Deal(stok, tok_o, n_f, sems, ids)
+    rows = 16 * half
+    hp = w3.shape[3]
+    wide = D // 2
+
+    deal_tok = Deal(stage, tok_o, n_f, sems, ids)
     deal_cot = Deal(scot, cot_o, n_f, sems, ids)
     base = ids.take(n_f - 1)
     gs = [remote(gains, gz.at[f], sems, base + k, zs[k]) for k in range(n_f - 1)]
     base = ids.take(3)
     gps = [remote(gp.at[c], gp.at[c], sems, base + k, plane[k]) for k in range(3)]
-    swaps = [Swap(src, dst, sems, ids)
-             for src, dst in ((pq, wq.at[f]), (po, wo.at[f]), (p2, w2.at[f]), (p3, q3))]
-    spreads = [Spread(w, n_f, sems, ids) for w in (wq, wo, w2)]
-    g1 = [Gather(first, m, sems, ids) for m in range(2)]
-    gc = [Gather(cotf, m, sems, ids) for m in range(2)]
-    red = [Reduce(part.at[m], r0.at[m], rx.at[m], ry.at[m], sems, ids) for m in range(2)]
-    local = [pltpu.make_async_copy(first, first_h, lsem.at[0]),
-             pltpu.make_async_copy(cotf, cot_h, lsem.at[1])]
-
-    for j in range(n_f):
-        stok[j] = tok[t, order[t, j]]
+    swaps = [Swap(src, w.at[f], sems, ids)
+             for src, w in ((pq, wq), (po, wo), (p2, w2), (p3, w3))]
+    spreads = [Spread(w, n_f, sems, ids) for w in (wq, wo, w2, w3)]
+    g1, gc, g2 = ([Gather(x, m, sems, ids) for m in range(2)] for x in (first, cotf, full))
+    red1, red2 = (
+        [Reduce(part.at[m], r0.at[m], rx.at[m], ry.at[m], sems, ids) for m in range(2)]
+        for _ in range(2)
+    )
+    collect = Collect(gd, got, n_f, sems, ids, passed=False)
+    keep = Keep(lsem)
+    mine = pl.ds(pl.multiple_of(t * wide, wide), wide)
+
+    def stage_rows(src, dst, m):
+        for j in range(n_f):
+            dst[m, j] = src[m, order[m, j], :, mine]
+
+    stage_rows(tok, stage, 0)
     greet(everyone(n_f))
+    deal_tok.start(0)
     each(gs, "start")
-    deal_tok.start()
-    each(swaps, "start")
+    each(swaps[:2], "start")
+    stage_rows(tok, stage, 1)
+    deal_tok.start(1)
+    each(swaps[2:], "start")
     each(swaps, "keep")
-    for j in range(n_f):
-        scot[j] = cot[t, order[t, j]]
     gz[f] = gains[...]
+    stage_rows(cot, scot, 0)
+    stage_rows(cot, scot, 1)
+    table(small, turn)
     each(gs, "wait_recv")
     gp[c] = jnp.sum(gz[...], axis=0)
     each(gps, "start")
-    swaps[0].wait()
-    spreads[0].start()
-    each(gps, "wait_recv")
-    gains_o[...] = jnp.sum(gp[...], axis=0)
 
     def norm1(m):
         deal_tok.wait(m)
         hat, _ = norm_stats(tok_o[m].reshape(-1, D).astype(F32))
         first[m, c, t] = (hat * gains_o[0:1, :]).astype(BF).reshape(2, half, D)
 
+    each(gps, "wait_recv")
+    gains_o[...] = jnp.sum(gp[...], axis=0)
     norm1(0)
     g1[0].s0()
+    swaps[0].wait()
     norm1(1)
-    spreads[0].relay()
+    spreads[0].start()
     g1[0].s1()
     g1[1].s0()
     swaps[1].wait()
+    g1[0].s2()
     spreads[1].start()
-    deal_cot.start()
-    g1[0].s2()
     g1[0].s3()
-    swaps[2].wait()
-    spreads[2].start()
+    spreads[0].relay()
+    deal_cot.start(0)
+    deal_cot.start(1)
     g1[0].s4()
     spreads[0].wait()
+    g1[1].s1()
 
     def attend(m, hooks):
         joined = nn(first[m].reshape(rows, D), wq[...].reshape(D, -1))
-        q_o[m] = rotate(joined[:, 0:128], cos[...], sin[...], 1.0).astype(BF) * BF(0.125)
-        k_o[m] = rotate(joined[:, 128:256], cos[...], sin[...], 1.0).astype(BF)
+        q_o[m] = rotate(joined[:, 0:128], turn[0], turn[1], 1.0).astype(BF) * BF(0.125)
+        k_o[m] = rotate(joined[:, 128:256], turn[0], turn[1], 1.0).astype(BF)
         v = joined[:, 256:384]
         v_o[m] = v.astype(BF)
         v_t[...] = v.T.astype(BF)
         lane = lax.broadcasted_iota(jnp.int32, (rows, 128), 1)
-        alive = lax.broadcasted_iota(jnp.int32, (rows, rows), 0) < live[m]
+        alive = lax.broadcasted_iota(jnp.int32, (rows, rows), 0) < lengths[m, f]
 
         def head(h, carry):
             at = pl.ds(pl.multiple_of(h * HEAD_DIM, HEAD_DIM), HEAD_DIM)
@@ -593,101 +642,80 @@
 
     def product(m):
         def step(i, carry):
-            span = red[m].span(i)
+            span = red1[m].span(i)
             block = mixed_o[m, pl.ds(pl.multiple_of(span * 4 * half, 4 * half), 4 * half), :]
             part[m, span] = nt(block, wo[...].reshape(D, -1)).astype(BF).reshape(2, 2, half, D)
-            red[m].crossing(i).start()
+            red1[m].crossing(i).start()
             return carry
 
         lax.fori_loop(0, 4, step, 0)
 
     def norm2(m):
-        hidden = tok_o[m].reshape(-1, D).astype(F32) + red[m].s4()
+        hidden = tok_o[m].reshape(-1, D).astype(F32) + red1[m].s4()
         hidden_o[m] = hidden
         hat, _ = norm_stats(hidden)
-        second_o[m] = (hat * gains_o[1:2, :]).astype(BF).reshape(2, half, D)
-
-    g1[1].s1()
+        full[m, c, t] = (hat * gains_o[1:2, :]).astype(BF).reshape(2, half, D)
+        g2[m].s0()
 
     def hook0():
         g1[1].s2()
         spreads[1].relay()
 
     attend(0, (hook0, g1[1].s3))
-    g1[1].s4()
-    local[0].start()
     spreads[1].wait()
     product(0)
-    red[0].s1()
-    deal_cot.wait(0)
-    deal_cot.wait(1)
-    for m in range(2):
-        cotf[m, c, t] = cot_o[m].reshape(2, half, D)
-    red[0].s2()
+    g1[1].s4()
+    swaps[2].wait()
+    swaps[3].wait()
+    spreads[2].start()
+    for src, dst in ((first, first_h), (tok_o, tok_h), (wq, wq_h), (wo, wo_h)):
+        keep.move(src, dst)
+    red1[0].s1()
 
     def hook1():
-        red[0].s3()
-        gc[0].s0()
+        red1[0].s2()
 
     def hook2():
-        spreads[2].relay()
+        red1[0].s3()
+        deal_cot.wait(0)
+        cotf[0, c, t] = cot_o[0].reshape(2, half, D)
 
     attend(1, (hook1, hook2))
     product(1)
-    red[1].s1()
-    red[1].s2()
+    gc[0].s0()
+    red1[1].s1()
+    deal_cot.wait(1)
+    cotf[1, c, t] = cot_o[1].reshape(2, half, D)
     norm2(0)
-    red[1].s3()
+    red1[1].s2()
+    spreads[2].relay()
+    spreads[3].start()
+    red1[1].s3()
     gc[0].s1()
     gc[1].s0()
+    g2[0].s1()
+    norm2(1)
     gc[0].s2()
+    g2[0].s2()
     gc[0].s3()
-    norm2(1)
+    g2[0].s3()
+    g2[1].s1()
     gc[1].s1()
-    gc[1].rest()
+    for m in range(2):
+        red1[m].end()
+    for src, dst in ((q_o, q_h), (k_o, k_h), (v_o, v_h), (mixed_o, mixed_h), (out_o, out_h),
+                     (lse_o, lse_h), (hidden_o, hidden_h)):
+        keep.move(src, dst)
+    spreads[3].relay()
     gc[0].s4()
-    local[1].start()
-    swaps[3].wait()
+    g2[0].s4()
     spreads[2].wait()
-    each(gs + gps, "wait_send")
-    for x in [deal_tok, deal_cot] + swaps + spreads + g1 + gc + red:
-        x.end()
-    each(local, "wait")
-
-
-def second_kernel(
-    n_f, second, w2, q3, cot_h, cot_own, hidden, gains,
-    hg_o, attn_o, act_o, gain_o, w3, gi_o, gd_o,
-    full, cotf, gg, gd, got, acc, part, r0, rx, ry, sems, lsem,
-):
-    f, c, t = here()
-    ids = Ids()
-    half = full.shape[4]
-    hp = w3.shape[3]
-    rows = 16 * half
-    g2 = [Gather(full, m, sems, ids) for m in range(2)]
-    red = [Reduce(part.at[m], r0.at[m], rx.at[m], ry.at[m], sems, ids) for m in range(2)]
-    spread = Spread(w3, n_f, sems, ids)
-    collect = Collect(gd, got, n_f, sems, ids)
-    load = pltpu.make_async_copy(cot_h, cotf, lsem.at[0])
-    load.start()
-    w3[f] = q3[...]
-    for m in range(2):
-        full[m, c, t] = second[m]
-    greet(everyone(n_f))
-    g2[0].s0()
-    spread.start()
-    g2[0].s1()
-    g2[1].s0()
-    spread.relay()
-    g2[0].rest()
-    load.wait()
-    spread.wait()
-    g2[1].s1()
+    spreads[3].wait()
+    keep.move(w3, w3_h)
 
     def mlp(m, hooks):
         def step(i, carry):
-            span = red[m].span(i)
+            span = red2[m].span(i)
             low = full[m, span].reshape(4 * half, D)
             win = w2[...].reshape(D, 2 * hp)
             u = nn(low, win[:, :hp])
@@ -700,46 +728,56 @@
             gg[m, span, :, 0:hp] = (a * g * slope).astype(BF)
             gg[m, span, :, hp:] = (a * gelu).astype(BF)
             part[m, span] = nt(gg[m, span], win).astype(BF).reshape(2, 2, half, D)
-            red[m].crossing(i).start()
+            red2[m].crossing(i).start()
             for j, hook in enumerate(hooks):
                 pl.when(i == j)(hook)
             return carry
 
         lax.fori_loop(0, 4, step, 0)
 
-    mlp(0, (g2[1].s2, g2[1].s3))
-    red[0].s1()
+    def rest2():
+        gc[1].s2()
+        g2[1].s2()
+
+    def rest3():
+        gc[1].s3()
+        g2[1].s3()
+
+    mlp(0, (rest2, rest3))
+    red2[0].s1()
+    gc[1].s4()
     g2[1].s4()
-    mlp(1, (red[0].s2, red[0].s3))
-    red[1].s1()
+    mlp(1, (red2[0].s2, red2[0].s3))
+    red2[1].s1()
+    keep.move(act_o, act_h)
     flat_act = act_o[...].reshape(2 * rows, hp)
     flat_gg = gg[...].reshape(2 * rows, 2 * hp)
-    n_d = 256
+    n_d = max(256, gd.shape[1])
 
     def down(b, carry):
         x = cotf[:, :, :, :, :, pl.ds(pl.multiple_of(b * n_d, n_d), n_d)].reshape(2 * rows, n_d)
-        blk = n_d // gd.shape[1] if gd.shape[1] < n_d else 1
-        gd_view = tn(x, flat_act).astype(BF)
+        sums = tn(x, flat_act).astype(BF)
         if gd.shape[1] == n_d:
-            gd[b] = gd_view
+            gd[b] = sums
         else:
-            gd[pl.ds(b * blk, blk)] = gd_view.reshape(blk, gd.shape[1], hp)
+            blk = n_d // gd.shape[1]
+            gd[pl.ds(b * blk, blk)] = sums.reshape(blk, gd.shape[1], hp)
         return carry
 
     lax.fori_loop(0, D // n_d, down, 0)
     collect.start()
-    red[1].s2()
+    red2[1].s2()
 
     def norm3(m):
-        grad = red[m].s4()
-        hat, inv = norm_stats(hidden[m])
-        hg = cot_own[m].reshape(-1, D).astype(F32) + norm_back(grad, hat, inv, gains[1:2, :])
+        grad = red2[m].s4()
+        hat, inv = norm_stats(hidden_o[m])
+        hg = cot_o[m].reshape(-1, D).astype(F32) + norm_back(grad, hat, inv, gains_o[1:2, :])
         hg_o[m] = hg
         attn_o[m] = hg.astype(BF).reshape(2, half, D)
         return jnp.sum(grad * hat, axis=0, keepdims=True)
 
     gain = norm3(0)
-    red[1].s3()
+    red2[1].s3()
 
     def inner(b, carry):
         x = full[:, :, :, :, :, pl.ds(pl.multiple_of(b * n_d, n_d), n_d)].reshape(2 * rows, n_d)
@@ -747,21 +785,23 @@
         return carry
 
     lax.fori_loop(0, D // n_d, inner, 0)
-    collect.relay()
     gain = gain + norm3(1)
     gain_o[...] = jnp.broadcast_to(gain, gain_o.shape)
     collect.total(acc)
     gd_o[...] = acc[...].astype(BF)
-    for x in g2 + red + [spread, collect]:
+    each(gs + gps, "wait_send")
+    for x in [deal_tok, deal_cot, collect] + swaps + spreads + g1 + gc + g2 + red2:
         x.end()
+    each(keep.copies, "wait")
 
 
 def third_kernel(
-    n_f, owners, live, attn, wo, wq, w3, act, q, k, v, mixed, out, lse, first_h, hg, hidden, tok,
-    gains, gain2, gi, gd, cos, sin,
-    out_o, grad_o, gain_o, share_o,
+    n_f, owners, lengths, attn, wo_h, wq_h, w3_h, act_h, q_h, k_h, v_h, mixed_h, out_h, lse_h,
+    first_h, hg_h, hidden_h, tok_h, gains, gain2, gi, gd_h, small,
+    out_o, grad_o, gain_o, early_o, late_o,
+    wo, wq, w3, act, q, k, v, mixed, out, lse, hg, hidden, tok, gd, turn,
     full, first, dk, dv, dq_t, mg, delta, k_t, joined, part, r0, rx, ry, r0b, rxb, ryb,
-    gl, gotl, gotg, accl, accg, ssend, orow, grow, oback, gback, oother, gother, gz, gp, gt,
+    gl, gotl, gotg, accl, accg, ssend, slate, orow, grow, oback, gback, oother, gother, gz, gp, gt,
     sems, lsem,
 ):
     f, c, t = here()
@@ -780,13 +820,19 @@
     collect_l = Collect(gl, gotl, n_f, sems, ids)
     ret_o = Return(orow, oback, oother, n_f, sems, ids)
     ret_g = Return(grow, gback, gother, n_f, sems, ids)
-    swap = Swap(ssend, share_o, sems, ids)
+    swap = Swap(ssend, early_o, sems, ids)
+    swap_late = Swap(slate, late_o, sems, ids)
     base = ids.take(1 + 3 + n_f - 1)
     s0 = remote(gt.at[0], gt.at[1], sems, base, po)
     gps = [remote(gp.at[c], gp.at[c], sems, base + 1 + j, plane[j]) for j in range(3)]
     gzs = [remote(gz.at[f], gz.at[f], sems, base + 4 + j, zs[j]) for j in range(n_f - 1)]
-    load = pltpu.make_async_copy(first_h, first, lsem.at[0])
-    load.start()
+    keep = Keep(lsem)
+    l_act, l_w3, l_wo, l_out, l_q, l_k, l_v, l_lse, l_hidden, l_wq, l_mixed, l_first, l_tok, l_hg, l_gd = [
+        keep.move(src, dst)
+        for src, dst in ((act_h, act), (w3_h, w3), (wo_h, wo), (out_h, out), (q_h, q), (k_h, k),
+                         (v_h, v), (lse_h, lse), (hidden_h, hidden), (wq_h, wq),
+                         (mixed_h, mixed), (first_h, first), (tok_h, tok), (hg_h, hg), (gd_h, gd))
+    ]
     for m in range(2):
         full[m, c, t] = attn[m]
     greet(everyone(n_f))
@@ -808,12 +854,16 @@
     def joined_rows(m, span):
         return joined[m, pl.ds(pl.multiple_of(span * 4 * half, 4 * half), 4 * half), :]
 
+    table(small, turn)
+    l_act.wait()
+    l_w3.wait()
     g3[0].s1()
     g3[1].s0()
     product(red4, 0, act_rows, lambda: w3[...].reshape(D, hp))
     product(red4, 1, act_rows, lambda: w3[...].reshape(D, hp))
     g3[0].rest()
     collect_g.relay()
+    each([l_wo, l_out, l_q, l_k, l_v, l_lse], "wait")
     QB = 512
 
     def attend_back(m, hooks):
@@ -826,7 +876,7 @@
         dk[...] = jnp.zeros_like(dk)
         dv[...] = jnp.zeros_like(dv)
         lane = lax.broadcasted_iota(jnp.int32, (QB, 128), 1)
-        alive = lax.broadcasted_iota(jnp.int32, (rows, QB), 0) < live[m]
+        alive = lax.broadcasted_iota(jnp.int32, (rows, QB), 0) < lengths[m, f]
         n_b = rows // QB
 
         def block(i, carry):
@@ -849,8 +899,8 @@
 
         lax.fori_loop(0, 2 * n_b, block, 0)
         dq = dq_t[...].T * 0.125
-        joined[m, :, 0:128] = rotate(dq, cos[...], sin[...], -1.0).astype(BF)
-        joined[m, :, 128:256] = rotate(dk[...], cos[...], sin[...], -1.0).astype(BF)
+        joined[m, :, 0:128] = rotate(dq, turn[0], turn[1], -1.0).astype(BF)
+        joined[m, :, 128:256] = rotate(dk[...], turn[0], turn[1], -1.0).astype(BF)
         joined[m, :, 256:384] = dv[...].astype(BF)
 
     def nothing():
@@ -873,6 +923,8 @@
 
     attend_back(0, (h0, h1, h2, h3))
     g3[1].s4()
+    l_hidden.wait()
+    l_wq.wait()
 
     def finish_out(m):
         rows_out = hidden[m] + red4[m].s4()
@@ -898,10 +950,10 @@
     finish_out(1)
     product(red3, 1, joined_rows, lambda: wq[...].reshape(D, -1))
     red3[1].s1()
-    load.wait()
+    each([l_mixed, l_first, l_tok, l_hg, l_gd], "wait")
     flat_j = joined[...].reshape(2 * rows, -1)
     flat_m = mixed[...].reshape(2 * rows, -1)
-    n_d = 256
+    n_d = max(256, gl.shape[1])
 
     def late(b, carry):
         at = pl.ds(pl.multiple_of(b * n_d, n_d), n_d)
@@ -933,6 +985,9 @@
     gain1 = norm4(0)
     red3[1].s3()
     collect_g.total(accg)
+    ssend[:, :, 0:ng] = accg[...].astype(BF).reshape(4, -1, ng)
+    ssend[:, :, ng:] = gd[...].reshape(4, -1, hp)
+    swap.start()
     collect_l.relay()
     gain1 = gain1 + norm4(1)
     row = lax.broadcasted_iota(jnp.int32, gain2.shape, 0)
@@ -943,14 +998,13 @@
     gp[c] = gt[0] + gt[1]
     each(gps, "start")
     collect_l.total(accl)
-    ssend[:, :, 0:nl] = accl[...].astype(BF).reshape(4, -1, nl)
-    ssend[:, :, nl : nl + ng] = accg[...].astype(BF).reshape(4, -1, ng)
-    ssend[:, :, nl + ng :] = gd[...].reshape(4, -1, hp)
-    swap.start()
+    slate[...] = accl[...].astype(BF).reshape(4, -1, nl)
+    swap_late.start()
     each(gps, "wait_recv")
     gz[f] = jnp.sum(gp[...], axis=0)
     each(gzs, "start")
     swap.keep()
+    swap_late.keep()
     ret_g.wait()
     ret_o.end()
 
@@ -965,8 +1019,9 @@
     ret_g.end()
     unpack(grad_o, gback, gother)
     swap.wait()
+    swap_late.wait()
     each([s0] + gps + gzs, "wait_send")
-    for x in g3 + red3 + [collect_g, collect_l, swap]:
+    for x in g3 + red3 + [collect_g, collect_l, swap, swap_late]:
         x.end()
 
 
@@ -974,19 +1029,22 @@
     lane = jnp.arange(128, dtype=jnp.int32)
     exponent = (2 * (lane % (HEAD_DIM // 2))).astype(F32)
     inverse = rope_base ** (-exponent / HEAD_DIM)
-    angles = jnp.arange(rows, dtype=jnp.int32).astype(F32)[:, None] * inverse[None, :]
     sign = jnp.where(lane % HEAD_DIM < HEAD_DIM // 2, -1.0, 1.0)
-    return jnp.cos(angles), jnp.sin(angles) * sign[None, :]
+    fine = jnp.arange(32, dtype=jnp.int32)
+    coarse = fine * (rows // 32)
+    both = jnp.stack([coarse, fine]).astype(F32)[:, :, None] * inverse[None, None, :]
+    cos, sin = jnp.cos(both), jnp.sin(both)
+    return jnp.stack([cos[0], sin[0], cos[1], sin[1], jnp.broadcast_to(sign, cos[0].shape)])
 
 
 def per_device(n_f, n_c, n_t, tokens, cotangent, lengths, owners,
                norm_attn, norm_mlp, w_qkv, w_out, w_in, w_down):
     f, c, t = here()
     micro, seqs, _, piece, _ = tokens.shape
-    assert n_c == 4 and n_t == 2 and micro == 2 and seqs == n_f
     span = piece * n_f
     half = span // 4
     rows = span * n_c
+    assert n_c == 4 and n_t == 2 and micro == 2 and seqs == n_f and rows == 1024
     n_h = n_f // 2
     wr = w_qkv.shape[0]
     hid = w_in.shape[2]
@@ -994,8 +1052,9 @@
     heads = w_qkv.shape[2] // n_c
     wb = n_c * wr
 
-    order = jnp.argsort(owners, axis=1).astype(jnp.int32)
-    live = lax.dynamic_index_in_dim(lengths, f, axis=1, keepdims=False)
+    slots = jnp.arange(n_f, dtype=jnp.int32)
+    same = owners[:, :, None] == slots[None, None, :]
+    order = jnp.sum(jnp.where(same, slots[None, :, None], 0), axis=1, dtype=jnp.int32)
     place = (f * n_c + c) * wr
     gains_own = jnp.stack([norm_attn, norm_mlp]).astype(F32)
     gains_row = lax.dynamic_update_slice(jnp.zeros((8, D), F32), gains_own, (0, place))
@@ -1009,64 +1068,65 @@
     p_in = quarters(jnp.pad(w_in, [(0, 0), (0, 0), (0, more)]).reshape(wr, 2, n_c, hp))
     p_down = jnp.pad(w_down, [(0, more), (0, 0)]).reshape(n_c, hp, wr).transpose(0, 2, 1)
     n_q = 3 * heads
-    cos, sin = rope_tables(rows)
+    small = rope_tables(rows)
 
     full_shape = (micro, n_c, 2, 2, half, D)
     own_shape = (micro, n_h, piece, D)
     row_shape = (micro, 2 * half, D)
     head_shape = (micro, rows, 128)
+    act_shape = (micro, n_c, span, hp)
+    stat_shape, wide_shape = (micro, 8, rows), (micro, 128, rows)
     V = pltpu.VMEM
-    (tok, cot, gains, wq, wo, w2, q3, first_h, cot_h, q, k, v, mixed, out_t, lse, hidden,
-     second) = comm_call(
-        functools.partial(first_kernel, n_f),
-        [
-            (shaped(own_shape, BF), vm()), (shaped(own_shape, BF), vm()),
-            (shaped((8, D), F32), vm()),
-            (shaped((n_f, n_c, wr, n_q), BF), vm()), (shaped((n_f, n_c, wr, heads), BF), vm()),
-            (shaped((n_f, n_c, wr, 2 * hp), BF), vm()), (shaped((n_c, wr, hp), BF), vm()),
-            (shaped(full_shape, BF), hb()), (shaped(full_shape, BF), hb()),
+    w_shapes = [(n_f, n_c, wr, n) for n in (n_q, heads, 2 * hp, hp)]
+    send = (micro, n_f, piece, D // 2)
+    (gains, tok, hidden, wq, wo, w3, q, k, v, mixed, out_t, lse, first, act, hg, attn, gain2, g_in,
+     g_down) = comm_call(
+        functools.partial(front_kernel, n_f),
+        [(shaped((8, D), F32), vm())]
+        + [
+            (shaped(a, d), hb())
+            for a, d in (
+                (own_shape, BF), (row_shape, F32), (w_shapes[0], BF), (w_shapes[1], BF),
+                (w_shapes[3], BF), (head_shape, BF), (head_shape, BF), (head_shape, BF),
+                (head_shape, BF), (wide_shape, F32), (stat_shape, F32), (full_shape, BF),
+                (act_shape, BF),
+            )
         ]
-        + [(shaped(head_shape, BF), vm())] * 4
         + [
-            (shaped((micro, 128, rows), F32), vm()), (shaped((micro, 8, rows), F32), vm()),
             (shaped(row_shape, F32), vm()), (shaped((micro, 2, half, D), BF), vm()),
+            (shaped((8, D), F32), vm()), (shaped((D, 2 * hp), BF), vm()),
+            (shaped((wb, hp), BF), vm()),
         ],
-        [sm(), sm()] + [vm()] * 9,
-        [
-            V((n_f, piece, D), BF), V((n_f, piece, D), BF), V((n_f, 8, D), F32),
-            V((n_c, 8, D), F32), V(full_shape, BF), V(full_shape, BF),
+        [sm(), sm()] + [vm()] * 8,
+        [V(own_shape, BF), V(own_shape, BF), V(row_shape, F32)]
+        + [V(a, BF) for a in w_shapes]
+        + [V(head_shape, BF)] * 4
+        + [V(wide_shape, F32), V(stat_shape, F32), V(act_shape, BF)]
+        + [
+            V(send, BF), V(send, BF), V((n_f, 8, D), F32), V((n_c, 8, D), F32),
+            V(full_shape, BF), V(full_shape, BF), V(full_shape, BF),
+            V((micro, n_c, span, 2 * hp), BF), V((n_f, wb, hp), BF),
+            V((collect_slots(n_f), wb, hp), BF), V((wb, hp), F32),
         ]
         + reduce_scratch(half)
-        + [V((128, rows), BF)],
-        5 * n_f + 120, 2, 0, 10**10,
-    )(order, live, tokens[:, :, 0], cotangent[:, :, 0], gains_row, p_qkv, p_out, p_in, p_down,
-      cos, sin)
-
-    hg, attn, act, gain2, w3, g_in, g_down = comm_call(
-        functools.partial(second_kernel, n_f),
-        [
-            (shaped(row_shape, F32), vm()), (shaped((micro, 2, half, D), BF), vm()),
-            (shaped((micro, n_c, span, hp), BF), vm()), (shaped((8, D), F32), vm()),
-            (shaped((n_f, n_c, wr, hp), BF), vm()),
-            (shaped((D, 2 * hp), BF), vm()), (shaped((wb, hp), BF), vm()),
-        ],
-        [vm(), vm(), vm(), hb()] + [vm()] * 3,
-        [
-            V(full_shape, BF), V(full_shape, BF), V((micro, n_c, span, 2 * hp), BF),
-            V((n_f, wb, hp), BF), V((collect_slots(n_f), wb, hp), BF), V((wb, hp), F32),
-        ]
-        + reduce_scratch(half),
-        n_f + 60, 1, 1, 10**10,
-    )(second, w2, q3, cot_h, cot, hidden, gains)
-
-    outs, grads, gain_grads, shares = comm_call(
+        + [V((128, rows), BF), V((2, rows, 128), F32)],
+        6 * n_f + 160, 16, 0, 10**10,
+    )(order, lengths, tokens[:, :, 0], cotangent[:, :, 0], gains_row, p_qkv, p_out, p_in, p_down,
+      small)
+
+    outs, grads, gain_grads, early, late = comm_call(
         functools.partial(third_kernel, n_f),
         [
             (shaped((micro, n_f, piece, D), BF), vm()), (shaped((micro, n_f, piece, D), BF), vm()),
-            (shaped((8, D), F32), vm()), (shaped((n_c, wr, n_q + heads + 3 * hp), BF), vm()),
+            (shaped((8, D), F32), vm()), (shaped((n_c, wr, 3 * hp), BF), vm()),
+            (shaped((n_c, wr, n_q + heads), BF), vm()),
         ],
-        [sm(), sm()] + [vm()] * 11 + [hb()] + [vm()] * 9,
-        [
+        [sm(), sm(), vm()] + [hb()] * 14 + [vm()] * 3 + [hb(), vm()],
+        [V(w_shapes[1], BF), V(w_shapes[0], BF), V(w_shapes[3], BF), V(act_shape, BF)]
+        + [V(head_shape, BF)] * 4
+        + [V(wide_shape, F32), V(stat_shape, F32), V(row_shape, F32), V(row_shape, F32),
+           V(own_shape, BF), V((wb, hp), BF), V((2, rows, 128), F32)]
+        + [
             V(full_shape, BF), V(full_shape, BF), V((rows, 128), F32), V((rows, 128), F32),
             V((128, rows), F32), V((rows, 128), BF), V((8, rows), F32), V((128, rows), BF),
             V((micro, rows, 384), BF),
@@ -1077,24 +1137,22 @@
             V((n_f, wb, n_q + heads), BF),
             V((collect_slots(n_f), wb, n_q + heads), BF), V((collect_slots(n_f), wb, 2 * hp), BF),
             V((wb, n_q + heads), F32), V((wb, 2 * hp), F32),
-            V((n_c, wr, n_q + heads + 3 * hp), BF),
+            V((n_c, wr, 3 * hp), BF), V((n_c, wr, n_q + heads), BF),
             V(own_shape, BF), V(own_shape, BF),
             V((n_f, piece, D), BF), V((n_f, piece, D), BF),
             V((n_f, piece, D), BF), V((n_f, piece, D), BF),
             V((n_f, 8, D), F32), V((n_c, 8, D), F32), V((2, 8, D), F32),
         ],
-        6 * n_f + 100, 1, 2, 10**10,
-    )(owners, live, attn, wo, wq, w3, act, q, k, v, mixed, out_t, lse, first_h, hg, hidden, tok,
-      gains, gain2, g_in.reshape(n_f, wb, 2 * hp), g_down, cos, sin)
-
-    shares = shares.astype(F32)
-    n1, n2 = n_q + heads, n_q + heads + 2 * hp
-    grad_qkv = shares[:, :, :n_q].reshape(n_c, wr, 3, heads).transpose(1, 2, 0, 3)
+        6 * n_f + 100, 16, 1, 10**10,
+    )(owners, lengths, attn, wo, wq, w3, act, q, k, v, mixed, out_t, lse, first, hg, hidden, tok,
+      gains, gain2, g_in.reshape(n_f, wb, 2 * hp), g_down, small)
+
+    grad_qkv = late[:, :, :n_q].astype(F32).reshape(n_c, wr, 3, heads).transpose(1, 2, 0, 3)
     grad_qkv = grad_qkv.reshape(wr, 3, n_c * heads)
-    grad_out = shares[:, :, n_q:n1].transpose(0, 2, 1).reshape(n_c * heads, wr)
-    grad_in = shares[:, :, n1:n2].reshape(n_c, wr, 2, hp)
+    grad_out = late[:, :, n_q:].astype(F32).transpose(0, 2, 1).reshape(n_c * heads, wr)
+    grad_in = early[:, :, : 2 * hp].astype(F32).reshape(n_c, wr, 2, hp)
     grad_in = grad_in.transpose(1, 2, 0, 3).reshape(wr, 2, n_c * hp)[..., :hid]
-    grad_down = shares[:, :, n2:].transpose(0, 2, 1).reshape(n_c * hp, wr)[:hid]
+    grad_down = early[:, :, 2 * hp :].astype(F32).transpose(0, 2, 1).reshape(n_c * hp, wr)[:hid]
     mine = lax.dynamic_slice(gain_grads, (0, place), (2, wr))
     return (outs[:, :, None], grads[:, :, None], mine[0], mine[1],
             grad_qkv, grad_out, grad_in, grad_down)

time: 286 us -> 252 us (0.88)
  Pallas kernels: 262 us -> 234 us
  local copies, waits for them, and re-layouts: 17.8 us -> 10.2 us
    pallas_call x2 -> x1, Pallas kernels: 166 us -> 141 us  [per_device(): comm_call(functools.partial(front_kernel, n_f), [(shaped((8, D), F32), vm...]
    pallas_call x1, Pallas kernels: 96.6 us -> 93.4 us  [per_device(): comm_call(functools.partial(third_kernel, n_f), [(shaped((micro, n_f, pie...]
    mul x1, other arithmetic: 3.04 us -> 0.01 us  [rope_tables(): coarse = fine * (rows // 32)]
where the time goes in v3:
time: 252 us
  Pallas kernels  234 us (93%)
  local copies, waits for them, and re-layouts  10.2 us (4%)
  other arithmetic  6.72 us (3%)
    pallas_call x1, Pallas kernels, per_device(): comm_call(functools.partial(front_kernel, n_f), [(shaped((8, D), F32), vm...  141 us
    pallas_call x1, Pallas kernels, per_device(): comm_call(functools.partial(third_kernel, n_f), [(shaped((micro, n_f, pie...  93.4 us

profile of v3, /device:TPU:0, one launch (start us, length us, event | category | flops | bytes accessed | tf_op | source)
XLA Modules:
  0.0 251.8 jit_solution(8337902868534160861)
XLA Ops:
  0.6 0.0 copy-start
  0.6 0.0 copy-start.5
  0.7 0.0 copy-start.4
  0.7 0.8 maximum_convert_fusion
  1.5 1.3 select_reduce_fusion.order
  2.9 0.2 dynamic_update_slice.3.gains
  3.1 0.0 copy-start.6
  3.1 0.2 multiply_sine_fusion
  3.3 0.0 copy-done
  3.3 0.6 bitcast_bitcast_fusion.2.po
  4.0 0.0 copy-start.7
  4.0 1.0 reshape.98
  5.0 0.2 copy.65
  5.2 0.8 reshape.99.pq
  6.0 0.0 copy-done.5
  6.1 0.7 copy.66
  6.8 0.0 copy-done.4
  6.8 0.3 pad.8
  7.1 0.0 copy-done.6
  7.1 0.3 copy.64
  7.4 0.0 copy-done.7
  7.4 1.0 reshape.102.p2
  8.4 140.6 %shard_map.161 = (f32[8,1024]{1,0:T(8,128)}, bf16[2,2,64,1024]{3,2,1,0:T(8,128)(2,1)}, f32[2,128,1024]{2,1,0:T(8,128)}, bf16[4,4,64,384]{3,2,1,0:T(8,128)(2,1)},...) custom-call(s32[2,4]{1,0:T(2,128)} %select_reduce_fusion.order, ...), custom_call_target="tpu_custom_call" | custom-call | flops 10000000000 | bytes 1048576 | tf_op jit(solution)/shard_map/pallas_call | solution.py:1083
  148.9 93.4 %shard_map.162 = (bf16[2,4,64,1024]{3,2,1,0:T(8,128)(2,1)}, bf16[2,4,64,1024]{3,2,1,0:T(8,128)(2,1)}, f32[8,1024]{1,0:T(8,128)}, bf16[4,64,1152]{2,1,0:T(8,128)(2,1)}, bf16[4,64,512]{2,1,0:T(8,128)(2,1)}) custom-call(s32[2,4]{1,0:T(2,128)} %owners.1, s32[2,4]{1,0:T(2,128)} %lengths.3, bf16[2,2,64,1024]{3,2,1,0:T(8,128)(2,1)} %get-tuple-element.32.attn, ...), custom_call_target="tpu_custom_call" | custom-call | flops 10000000000 | bytes 1048576 | tf_op jit(solution)/shard_map/pallas_call | solution.py:1117
  242.3 0.8 constant_dynamic-slice_fusion
  243.1 0.5 slice_bitcast_fusion.1
  243.6 1.5 copy_bitcast_fusion.1
  245.1 0.0 copy-start.3
  245.1 1.0 slice_convert_fusion.1
  246.1 0.2 reshape.120
  246.3 0.3 copy.47
  246.6 0.9 reshape.114
  247.5 0.0 copy-done.3
  247.5 0.1 reshape.110
  247.6 0.0 copy-start.2
  247.6 0.3 copy.57
  247.9 0.8 slice_convert_fusion.2
  248.7 0.0 copy-start.1
  248.7 1.1 slice_convert_fusion
  249.8 0.0 copy-done.2
  249.8 1.0 copy.74
  250.8 0.0 copy-done.1
  250.8 1.0 copy.75
  (15 shorter events, 0.1 us)
Async XLA Ops:
  0.6 2.7 %copy-start = (bf16[512,64]{0,1:T(8,128)(2,1)S(1)}, bf16[512,64]{0,1:T(8,128)(2,1)}, u32[]{:S(2)}) copy-start(bf16[512,64]{0,1:T(8,128)(2,1)} %param.17) | copy-start | bytes 196612
  0.6 5.4 %copy-start.5 = (bf16[1312,64]{0,1:T(8,128)(2,1)S(1)}, bf16[1312,64]{0,1:T(8,128)(2,1)}, u32[]{:S(2)}) copy-start(bf16[1312,64]{0,1:T(8,128)(2,1)} %param.19) | copy-start | bytes 503812
  0.7 6.1 %copy-start.4 = (bf16[64,2,1312]{2,1,0:T(2,128)(2,1)S(1)}, bf16[64,2,1312]{2,1,0:T(2,128)(2,1)}, u32[]{:S(2)}) copy-start(bf16[64,2,1312]{2,1,0:T(2,128)(2,1)} %param.18) | copy-start | bytes 1007620
  3.1 4.0 %copy-start.6 = (f32[8,1024]{1,0:T(8,128)}, f32[8,1024]{1,0:T(8,128)S(1)}, u32[]{:S(2)}) copy-start(f32[8,1024]{1,0:T(8,128)S(1)} %dynamic_update_slice.3.gains) | copy-start | bytes 98308
  4.0 3.4 %copy-start.7 = (f32[5,32,128]{2,1,0:T(8,128)}, f32[5,32,128]{2,1,0:T(8,128)S(1)}, u32[]{:S(2)}) copy-start(f32[5,32,128]{2,1,0:T(8,128)S(1)} %constant_dynamic-update-slice_fusion.small) | copy-start | bytes 245764
  245.1 2.4 copy-start.3
  247.6 2.2 copy-start.2
  248.7 2.1 copy-start.1

commit v4 on v3

--- a/solution.py
+++ b/solution.py
@@ -217,18 +217,15 @@
 class Spread:
     def __init__(self, ref, n_f, sems, ids):
         f, c, t = here()
-        self.f, self.n_f, self.ref = f, n_f, ref
+        self.f, self.n_f = f, n_f
         if n_f == 4:
-            base = ids.take(5)
-            self.steps = (-1, -2, 1, 2)
-            self.copies = [
-                remote(ref.at[f], ref.at[f], sems, base + i, (lax.rem(f - d + n_f, n_f), c, t))
-                for i, d in enumerate(self.steps)
-            ]
-            self.far = remote(
-                ref.at[jnp.where(f == 2, 0, 3)], ref.at[jnp.where(f == 2, 0, 3)], sems, base + 4,
-                (jnp.where(f == 2, 3, 0), c, t),
-            )
+            base = ids.take(6)
+            up, down = (lax.rem(f + 1, n_f), c, t), (lax.rem(f + n_f - 1, n_f), c, t)
+            self.up, self.down = [], []
+            for k in range(3):
+                low, high = ref.at[lax.rem(f - k + n_f, n_f)], ref.at[lax.rem(f + k, n_f)]
+                self.up.append(remote(low, low, sems, base + k, up))
+                self.down.append(remote(high, high, sems, base + 3 + k, down))
         else:
             base = ids.take(1)
             self.copies = [
@@ -238,42 +235,40 @@
             most = ref.at[pl.ds(0, n_f - 1)]
             self.all = remote(most, most, sems, base, (f, c, 1 - t))
 
+    def sends_up(self, k):
+        return (self.f >= k) & (self.f <= 2)
+
+    def sends_down(self, k):
+        return (self.f <= 3 - k) & (self.f >= 1)
+
     def start(self):
         if self.n_f != 4:
             return each(self.copies, "start")
-        for d, cp in zip(self.steps, self.copies):
-            pl.when((self.f - d >= 0) & (self.f - d < 4))(cp.start)
-
-    def relay(self):
+        pl.when(self.sends_up(0))(self.up[0].start)
+        pl.when(self.sends_down(0))(self.down[0].start)
+
+    def arrive(self, k):
+        pl.when(self.f >= k + 1)(self.up[k].wait_recv)
+        pl.when(self.f <= 2 - k)(self.down[k].wait_recv)
+
+    def step(self, k):
         if self.n_f != 4:
             return
-
-        @pl.when(self.f == 2)
-        def _():
-            self.copies[1].wait_recv()
-            self.far.start()
-
-        @pl.when(self.f == 1)
-        def _():
-            self.copies[3].wait_recv()
-            self.far.start()
+        self.arrive(k - 1)
+        pl.when(self.sends_up(k))(self.up[k].start)
+        pl.when(self.sends_down(k))(self.down[k].start)
 
     def wait(self):
         if self.n_f != 4:
             return self.all.wait_recv()
-        f = self.f
-        pl.when(f >= 1)(self.copies[0].wait_recv)
-        pl.when(f == 3)(self.copies[1].wait_recv)
-        pl.when(f <= 2)(self.copies[2].wait_recv)
-        pl.when(f == 0)(self.copies[3].wait_recv)
-        pl.when((f == 0) | (f == 3))(self.far.wait_recv)
+        self.arrive(2)
 
     def end(self):
         if self.n_f != 4:
             return self.all.wait_send()
-        for d, cp in zip(self.steps, self.copies):
-            pl.when((self.f - d >= 0) & (self.f - d < 4))(cp.wait_send)
-        pl.when((self.f == 1) | (self.f == 2))(self.far.wait_send)
+        for k in range(3):
+            pl.when(self.sends_up(k))(self.up[k].wait_send)
+            pl.when(self.sends_down(k))(self.down[k].wait_send)
 
 
 class Collect:
@@ -536,9 +531,9 @@
 def front_kernel(
     n_f, order, lengths, tok, cot, gains, pq, po, p2, p3, small,
     gains_o, tok_h, hidden_h, wq_h, wo_h, w3_h, q_h, k_h, v_h, mixed_h, out_h, lse_h, first_h,
-    act_h, hg_o, attn_o, gain_o, gi_o, gd_o,
+    act_h, hg_o, attn_o, gain_o, gi_o,
     tok_o, cot_o, hidden_o, wq, wo, w2, w3, q_o, k_o, v_o, mixed_o, out_o, lse_o, act_o,
-    stage, scot, gz, gp, first, cotf, full, gg, gd, got, acc, part, r0, rx, ry, v_t, turn,
+    stage, scot, gz, gp, first, cotf, full, gg, part, r0, rx, ry, v_t, turn,
     sems, lsem,
 ):
     f, c, t = here()
@@ -564,7 +559,6 @@
         [Reduce(part.at[m], r0.at[m], rx.at[m], ry.at[m], sems, ids) for m in range(2)]
         for _ in range(2)
     )
-    collect = Collect(gd, got, n_f, sems, ids, passed=False)
     keep = Keep(lsem)
     mine = pl.ds(pl.multiple_of(t * wide, wide), wide)
 
@@ -603,14 +597,16 @@
     spreads[0].start()
     g1[0].s1()
     g1[1].s0()
+    spreads[0].step(1)
     swaps[1].wait()
+    spreads[1].start()
     g1[0].s2()
-    spreads[1].start()
     g1[0].s3()
-    spreads[0].relay()
+    spreads[0].step(2)
     deal_cot.start(0)
     deal_cot.start(1)
     g1[0].s4()
+    spreads[1].step(1)
     spreads[0].wait()
     g1[1].s1()
 
@@ -659,7 +655,7 @@
 
     def hook0():
         g1[1].s2()
-        spreads[1].relay()
+        spreads[1].step(2)
 
     attend(0, (hook0, g1[1].s3))
     spreads[1].wait()
@@ -668,6 +664,7 @@
     swaps[2].wait()
     swaps[3].wait()
     spreads[2].start()
+    spreads[3].start()
     for src, dst in ((first, first_h), (tok_o, tok_h), (wq, wq_h), (wo, wo_h)):
         keep.move(src, dst)
     red1[0].s1()
@@ -688,13 +685,15 @@
     cotf[1, c, t] = cot_o[1].reshape(2, half, D)
     norm2(0)
     red1[1].s2()
-    spreads[2].relay()
-    spreads[3].start()
+    spreads[2].step(1)
+    spreads[3].step(1)
     red1[1].s3()
     gc[0].s1()
     gc[1].s0()
     g2[0].s1()
     norm2(1)
+    spreads[2].step(2)
+    spreads[3].step(2)
     gc[0].s2()
     g2[0].s2()
     gc[0].s3()
@@ -706,7 +705,6 @@
     for src, dst in ((q_o, q_h), (k_o, k_h), (v_o, v_h), (mixed_o, mixed_h), (out_o, out_h),
                      (lse_o, lse_h), (hidden_o, hidden_h)):
         keep.move(src, dst)
-    spreads[3].relay()
     gc[0].s4()
     g2[0].s4()
     spreads[2].wait()
@@ -752,20 +750,18 @@
     keep.move(act_o, act_h)
     flat_act = act_o[...].reshape(2 * rows, hp)
     flat_gg = gg[...].reshape(2 * rows, 2 * hp)
-    n_d = max(256, gd.shape[1])
-
-    def down(b, carry):
-        x = cotf[:, :, :, :, :, pl.ds(pl.multiple_of(b * n_d, n_d), n_d)].reshape(2 * rows, n_d)
-        sums = tn(x, flat_act).astype(BF)
-        if gd.shape[1] == n_d:
-            gd[b] = sums
-        else:
-            blk = n_d // gd.shape[1]
-            gd[pl.ds(b * blk, blk)] = sums.reshape(blk, gd.shape[1], hp)
-        return carry
-
-    lax.fori_loop(0, D // n_d, down, 0)
-    collect.start()
+    n_d = 256
+
+    def sums(source, weight, first_column, columns):
+        def step(b, carry):
+            at = pl.ds(pl.multiple_of(b * n_d, n_d), n_d)
+            x = source[:, :, :, :, :, at].reshape(2 * rows, n_d)
+            gi_o[at, first_column : first_column + columns] = tn(x, weight).astype(BF)
+            return carry
+
+        lax.fori_loop(0, D // n_d, step, 0)
+
+    sums(cotf, flat_act, 2 * hp, hp)
     red2[1].s2()
 
     def norm3(m):
@@ -779,27 +775,20 @@
     gain = norm3(0)
     red2[1].s3()
 
-    def inner(b, carry):
-        x = full[:, :, :, :, :, pl.ds(pl.multiple_of(b * n_d, n_d), n_d)].reshape(2 * rows, n_d)
-        gi_o[pl.ds(pl.multiple_of(b * n_d, n_d), n_d), :] = tn(x, flat_gg).astype(BF)
-        return carry
-
-    lax.fori_loop(0, D // n_d, inner, 0)
+    sums(full, flat_gg, 0, 2 * hp)
     gain = gain + norm3(1)
     gain_o[...] = jnp.broadcast_to(gain, gain_o.shape)
-    collect.total(acc)
-    gd_o[...] = acc[...].astype(BF)
     each(gs + gps, "wait_send")
-    for x in [deal_tok, deal_cot, collect] + swaps + spreads + g1 + gc + g2 + red2:
+    for x in [deal_tok, deal_cot] + swaps + spreads + g1 + gc + g2 + red2:
         x.end()
     each(keep.copies, "wait")
 
 
 def third_kernel(
     n_f, owners, lengths, attn, wo_h, wq_h, w3_h, act_h, q_h, k_h, v_h, mixed_h, out_h, lse_h,
-    first_h, hg_h, hidden_h, tok_h, gains, gain2, gi, gd_h, small,
+    first_h, hg_h, hidden_h, tok_h, gains, gain2, gi, small,
     out_o, grad_o, gain_o, early_o, late_o,
-    wo, wq, w3, act, q, k, v, mixed, out, lse, hg, hidden, tok, gd, turn,
+    wo, wq, w3, act, q, k, v, mixed, out, lse, hg, hidden, tok, turn,
     full, first, dk, dv, dq_t, mg, delta, k_t, joined, part, r0, rx, ry, r0b, rxb, ryb,
     gl, gotl, gotg, accl, accg, ssend, slate, orow, grow, oback, gback, oother, gother, gz, gp, gt,
     sems, lsem,
@@ -827,11 +816,11 @@
     gps = [remote(gp.at[c], gp.at[c], sems, base + 1 + j, plane[j]) for j in range(3)]
     gzs = [remote(gz.at[f], gz.at[f], sems, base + 4 + j, zs[j]) for j in range(n_f - 1)]
     keep = Keep(lsem)
-    l_act, l_w3, l_wo, l_out, l_q, l_k, l_v, l_lse, l_hidden, l_wq, l_mixed, l_first, l_tok, l_hg, l_gd = [
+    l_act, l_w3, l_wo, l_out, l_q, l_k, l_v, l_lse, l_hidden, l_wq, l_mixed, l_first, l_tok, l_hg = [
         keep.move(src, dst)
         for src, dst in ((act_h, act), (w3_h, w3), (wo_h, wo), (out_h, out), (q_h, q), (k_h, k),
                          (v_h, v), (lse_h, lse), (hidden_h, hidden), (wq_h, wq),
-                         (mixed_h, mixed), (first_h, first), (tok_h, tok), (hg_h, hg), (gd_h, gd))
+                         (mixed_h, mixed), (first_h, first), (tok_h, tok), (hg_h, hg))
     ]
     for m in range(2):
         full[m, c, t] = attn[m]
@@ -950,7 +939,7 @@
     finish_out(1)
     product(red3, 1, joined_rows, lambda: wq[...].reshape(D, -1))
     red3[1].s1()
-    each([l_mixed, l_first, l_tok, l_hg, l_gd], "wait")
+    each([l_mixed, l_first, l_tok, l_hg], "wait")
     flat_j = joined[...].reshape(2 * rows, -1)
     flat_m = mixed[...].reshape(2 * rows, -1)
     n_d = max(256, gl.shape[1])
@@ -985,8 +974,7 @@
     gain1 = norm4(0)
     red3[1].s3()
     collect_g.total(accg)
-    ssend[:, :, 0:ng] = accg[...].astype(BF).reshape(4, -1, ng)
-    ssend[:, :, ng:] = gd[...].reshape(4, -1, hp)
+    ssend[...] = accg[...].astype(BF).reshape(4, -1, ng)
     swap.start()
     collect_l.relay()
     gain1 = gain1 + norm4(1)
@@ -1079,8 +1067,8 @@
     V = pltpu.VMEM
     w_shapes = [(n_f, n_c, wr, n) for n in (n_q, heads, 2 * hp, hp)]
     send = (micro, n_f, piece, D // 2)
-    (gains, tok, hidden, wq, wo, w3, q, k, v, mixed, out_t, lse, first, act, hg, attn, gain2, g_in,
-     g_down) = comm_call(
+    (gains, tok, hidden, wq, wo, w3, q, k, v, mixed, out_t, lse, first, act, hg, attn, gain2,
+     g_in) = comm_call(
         functools.partial(front_kernel, n_f),
         [(shaped((8, D), F32), vm())]
         + [
@@ -1094,8 +1082,7 @@
         ]
         + [
             (shaped(row_shape, F32), vm()), (shaped((micro, 2, half, D), BF), vm()),
-            (shaped((8, D), F32), vm()), (shaped((D, 2 * hp), BF), vm()),
-            (shaped((wb, hp), BF), vm()),
+            (shaped((8, D), F32), vm()), (shaped((D, 3 * hp), BF), vm()),
         ],
         [sm(), sm()] + [vm()] * 8,
         [V(own_shape, BF), V(own_shape, BF), V(row_shape, F32)]
@@ -1105,8 +1092,7 @@
         + [
             V(send, BF), V(send, BF), V((n_f, 8, D), F32), V((n_c, 8, D), F32),
             V(full_shape, BF), V(full_shape, BF), V(full_shape, BF),
-            V((micro, n_c, span, 2 * hp), BF), V((n_f, wb, hp), BF),
-            V((collect_slots(n_f), wb, hp), BF), V((wb, hp), F32),
+            V((micro, n_c, span, 2 * hp), BF),
         ]
         + reduce_scratch(half)
         + [V((128, rows), BF), V((2, rows, 128), F32)],
@@ -1121,11 +1107,11 @@
             (shaped((8, D), F32), vm()), (shaped((n_c, wr, 3 * hp), BF), vm()),
             (shaped((n_c, wr, n_q + heads), BF), vm()),
         ],
-        [sm(), sm(), vm()] + [hb()] * 14 + [vm()] * 3 + [hb(), vm()],
+        [sm(), sm(), vm()] + [hb()] * 14 + [vm()] * 4,
         [V(w_shapes[1], BF), V(w_shapes[0], BF), V(w_shapes[3], BF), V(act_shape, BF)]
         + [V(head_shape, BF)] * 4
         + [V(wide_shape, F32), V(stat_shape, F32), V(row_shape, F32), V(row_shape, F32),
-           V(own_shape, BF), V((wb, hp), BF), V((2, rows, 128), F32)]
+           V(own_shape, BF), V((2, rows, 128), F32)]
         + [
             V(full_shape, BF), V(full_shape, BF), V((rows, 128), F32), V((rows, 128), F32),
             V((128, rows), F32), V((rows, 128), BF), V((8, rows), F32), V((128, rows), BF),
@@ -1135,8 +1121,8 @@
         + reduce_scratch(half)[1:]
         + [
             V((n_f, wb, n_q + heads), BF),
-            V((collect_slots(n_f), wb, n_q + heads), BF), V((collect_slots(n_f), wb, 2 * hp), BF),
-            V((wb, n_q + heads), F32), V((wb, 2 * hp), F32),
+            V((collect_slots(n_f), wb, n_q + heads), BF), V((collect_slots(n_f), wb, 3 * hp), BF),
+            V((wb, n_q + heads), F32), V((wb, 3 * hp), F32),
             V((n_c, wr, 3 * hp), BF), V((n_c, wr, n_q + heads), BF),
             V(own_shape, BF), V(own_shape, BF),
             V((n_f, piece, D), BF), V((n_f, piece, D), BF),
@@ -1145,7 +1131,7 @@
         ],
         6 * n_f + 100, 16, 1, 10**10,
     )(owners, lengths, attn, wo, wq, w3, act, q, k, v, mixed, out_t, lse, first, hg, hidden, tok,
-      gains, gain2, g_in.reshape(n_f, wb, 2 * hp), g_down, small)
+      gains, gain2, g_in.reshape(n_f, wb, 3 * hp), small)
 
     grad_qkv = late[:, :, :n_q].astype(F32).reshape(n_c, wr, 3, heads).transpose(1, 2, 0, 3)
     grad_qkv = grad_qkv.reshape(wr, 3, n_c * heads)

time: 252 us -> 250 us (level)
  Pallas kernels: 234 us -> 231 us
    pallas_call x1, Pallas kernels: 141 us -> 137 us  [per_device(): comm_call(functools.partial(front_kernel, n_f), [(shaped((8, D), F32), vm...]
where the time goes in v4:
time: 250 us
  Pallas kernels  231 us (92%)
  local copies, waits for them, and re-layouts  11.2 us (4%)
  other arithmetic  6.61 us (3%)
    pallas_call x1, Pallas kernels, per_device(): comm_call(functools.partial(front_kernel, n_f), [(shaped((8, D), F32), vm...  137 us
    pallas_call x1, Pallas kernels, per_device(): comm_call(functools.partial(third_kernel, n_f), [(shaped((micro, n_f, pie...  93.9 us

profile of v4, /device:TPU:0, one launch (start us, length us, event | category | flops | bytes accessed | tf_op | source)
XLA Modules:
  0.0 249.6 jit_solution(12119026383453248298)
XLA Ops:
  0.6 0.0 copy-start
  0.6 0.0 copy-start.4
  0.7 0.7 maximum_convert_fusion
  1.5 1.3 select_reduce_fusion.order
  2.8 0.2 dynamic_update_slice.3.gains
  3.0 0.0 copy-start.5
  3.1 0.2 multiply_sine_fusion
  3.3 0.0 copy-done
  3.3 0.6 bitcast_bitcast_fusion.2.po
  3.9 0.0 copy-start.6
  3.9 1.0 reshape.98
  5.0 0.2 copy.65
  5.1 0.8 reshape.99.pq
  6.0 0.9 pad.9
  6.9 0.7 copy.66
  7.6 0.0 copy-done.4
  7.6 0.3 pad.8
  7.9 0.3 copy.64
  8.2 1.0 reshape.102.p2
  9.2 0.0 copy-done.5
  9.2 0.0 copy-done.6
  9.2 137.1 %shard_map.161 = (f32[8,1024]{1,0:T(8,128)}, bf16[2,2,64,1024]{3,2,1,0:T(8,128)(2,1)}, f32[2,128,1024]{2,1,0:T(8,128)}, bf16[4,4,64,384]{3,2,1,0:T(8,128)(2,1)},...) custom-call(s32[2,4]{1,0:T(2,128)} %select_reduce_fusion.order, ...), custom_call_target="tpu_custom_call" | custom-call | flops 10000000000 | bytes 1048576 | tf_op jit(solution)/shard_map/pallas_call | solution.py:1071
  146.3 93.9 %shard_map.162 = (bf16[2,4,64,1024]{3,2,1,0:T(8,128)(2,1)}, bf16[2,4,64,1024]{3,2,1,0:T(8,128)(2,1)}, f32[8,1024]{1,0:T(8,128)}, bf16[4,64,1152]{2,1,0:T(8,128)(2,1)}, bf16[4,64,512]{2,1,0:T(8,128)(2,1)}) custom-call(s32[2,4]{1,0:T(2,128)} %owners.1, s32[2,4]{1,0:T(2,128)} %lengths.3, bf16[2,2,64,1024]{3,2,1,0:T(8,128)(2,1)} %get-tuple-element.31.attn, ...), custom_call_target="tpu_custom_call" | custom-call | flops 10000000000 | bytes 1048576 | tf_op jit(solution)/shard_map/pallas_call | solution.py:1103
  240.2 0.0 copy-start.3
  240.2 0.8 constant_dynamic-slice_fusion
  241.0 0.5 slice_bitcast_fusion.1
  241.5 1.5 copy_bitcast_fusion.1
  243.0 1.0 slice_convert_fusion.1
  244.0 0.2 reshape.120
  244.2 0.3 copy.47
  244.4 0.9 reshape.114
  245.3 0.0 copy-done.3
  245.3 0.0 copy-start.2
  245.4 0.1 reshape.110
  245.5 0.0 copy-start.1
  245.5 0.3 copy.57
  245.8 0.8 slice_convert_fusion.2
  246.6 1.1 slice_convert_fusion
  247.7 0.0 copy-done.2
  247.7 1.0 copy.74
  248.6 0.0 copy-done.1
  248.6 1.0 copy.75
  (14 shorter events, 0.1 us)
Async XLA Ops:
  0.6 2.6 %copy-start = (bf16[512,64]{0,1:T(8,128)(2,1)S(1)}, bf16[512,64]{0,1:T(8,128)(2,1)}, u32[]{:S(2)}) copy-start(bf16[512,64]{0,1:T(8,128)(2,1)} %param.17) | copy-start | bytes 196612
  0.6 7.0 %copy-start.4 = (bf16[64,2,1312]{2,1,0:T(2,128)(2,1)S(1)}, bf16[64,2,1312]{2,1,0:T(2,128)(2,1)}, u32[]{:S(2)}) copy-start(bf16[64,2,1312]{2,1,0:T(2,128)(2,1)} %param.18) | copy-start | bytes 1007620
  3.0 6.2 %copy-start.5 = (f32[8,1024]{1,0:T(8,128)}, f32[8,1024]{1,0:T(8,128)S(1)}, u32[]{:S(2)}) copy-start(f32[8,1024]{1,0:T(8,128)S(1)} %dynamic_update_slice.3.gains) | copy-start | bytes 98308
  3.9 5.3 %copy-start.6 = (f32[5,32,128]{2,1,0:T(8,128)}, f32[5,32,128]{2,1,0:T(8,128)S(1)}, u32[]{:S(2)}) copy-start(f32[5,32,128]{2,1,0:T(8,128)S(1)} %constant_dynamic-update-slice_fusion.small) | copy-start | bytes 245764
  240.2 5.1 %copy-start.3 = (bf16[4,64,1152]{2,1,0:T(8,128)(2,1)S(1)}, bf16[4,64,1152]{2,1,0:T(8,128)(2,1)}, u32[]{:S(2)}) copy-start(bf16[4,64,1152]{2,1,0:T(8,128)(2,1)} %get-tuple-element.53) | copy-start | bytes 1769476
  245.3 2.3 copy-start.2
  245.5 3.2 %copy-start.1 = (bf16[2,4,64,1024]{3,2,1,0:T(8,128)(2,1)S(1)}, bf16[2,4,64,1024]{3,2,1,0:T(8,128)(2,1)}, u32[]{:S(2)}) copy-start(bf16[2,4,64,1024]{3,2,1,0:T(8,128)(2,1)} %get-tuple-element.50) | copy-start | bytes 3145732

commit v5 on v4

--- a/solution.py
+++ b/solution.py
@@ -529,11 +529,11 @@
 
 
 def front_kernel(
-    n_f, order, lengths, tok, cot, gains, pq, po, p2, p3, small,
+    n_f, order, lengths, tok, cot_h, gains, pq, po, p2, p3, small,
     gains_o, tok_h, hidden_h, wq_h, wo_h, w3_h, q_h, k_h, v_h, mixed_h, out_h, lse_h, first_h,
-    act_h, hg_o, attn_o, gain_o, gi_o,
+    act_h, hg_h, attn_o, gain_o, gi_h,
     tok_o, cot_o, hidden_o, wq, wo, w2, w3, q_o, k_o, v_o, mixed_o, out_o, lse_o, act_o,
-    stage, scot, gz, gp, first, cotf, full, gg, part, r0, rx, ry, v_t, turn,
+    stage, scot, gz, gp, first, cotf, full, gg, hg_o, gi_o, cot, part, r0, rx, ry, v_t, turn,
     sems, lsem,
 ):
     f, c, t = here()
@@ -566,6 +566,7 @@
         for j in range(n_f):
             dst[m, j] = src[m, order[m, j], :, mine]
 
+    load = keep.move(cot_h, cot)
     stage_rows(tok, stage, 0)
     greet(everyone(n_f))
     deal_tok.start(0)
@@ -576,6 +577,7 @@
     each(swaps[2:], "start")
     each(swaps, "keep")
     gz[f] = gains[...]
+    load.wait()
     stage_rows(cot, scot, 0)
     stage_rows(cot, scot, 1)
     table(small, turn)
@@ -761,14 +763,15 @@
 
         lax.fori_loop(0, D // n_d, step, 0)
 
+    red2[1].s2()
     sums(cotf, flat_act, 2 * hp, hp)
-    red2[1].s2()
 
     def norm3(m):
         grad = red2[m].s4()
         hat, inv = norm_stats(hidden_o[m])
         hg = cot_o[m].reshape(-1, D).astype(F32) + norm_back(grad, hat, inv, gains_o[1:2, :])
         hg_o[m] = hg
+        keep.move(hg_o.at[m], hg_h.at[m])
         attn_o[m] = hg.astype(BF).reshape(2, half, D)
         return jnp.sum(grad * hat, axis=0, keepdims=True)
 
@@ -776,19 +779,20 @@
     red2[1].s3()
 
     sums(full, flat_gg, 0, 2 * hp)
+    keep.move(gi_o, gi_h)
     gain = gain + norm3(1)
     gain_o[...] = jnp.broadcast_to(gain, gain_o.shape)
     each(gs + gps, "wait_send")
     for x in [deal_tok, deal_cot] + swaps + spreads + g1 + gc + g2 + red2:
         x.end()
-    each(keep.copies, "wait")
+    each(keep.copies[1:], "wait")
 
 
 def third_kernel(
     n_f, owners, lengths, attn, wo_h, wq_h, w3_h, act_h, q_h, k_h, v_h, mixed_h, out_h, lse_h,
-    first_h, hg_h, hidden_h, tok_h, gains, gain2, gi, small,
+    first_h, hg_h, hidden_h, tok_h, gains, gain2, gi_h, small,
     out_o, grad_o, gain_o, early_o, late_o,
-    wo, wq, w3, act, q, k, v, mixed, out, lse, hg, hidden, tok, turn,
+    wo, wq, w3, act, q, k, v, mixed, out, lse, hg, hidden, tok, turn, gi,
     full, first, dk, dv, dq_t, mg, delta, k_t, joined, part, r0, rx, ry, r0b, rxb, ryb,
     gl, gotl, gotg, accl, accg, ssend, slate, orow, grow, oback, gback, oother, gother, gz, gp, gt,
     sems, lsem,
@@ -816,9 +820,9 @@
     gps = [remote(gp.at[c], gp.at[c], sems, base + 1 + j, plane[j]) for j in range(3)]
     gzs = [remote(gz.at[f], gz.at[f], sems, base + 4 + j, zs[j]) for j in range(n_f - 1)]
     keep = Keep(lsem)
-    l_act, l_w3, l_wo, l_out, l_q, l_k, l_v, l_lse, l_hidden, l_wq, l_mixed, l_first, l_tok, l_hg = [
+    l_gi, l_act, l_w3, l_wo, l_out, l_q, l_k, l_v, l_lse, l_hidden, l_wq, l_mixed, l_first, l_tok, l_hg = [
         keep.move(src, dst)
-        for src, dst in ((act_h, act), (w3_h, w3), (wo_h, wo), (out_h, out), (q_h, q), (k_h, k),
+        for src, dst in ((gi_h, gi), (act_h, act), (w3_h, w3), (wo_h, wo), (out_h, out), (q_h, q), (k_h, k),
                          (v_h, v), (lse_h, lse), (hidden_h, hidden), (wq_h, wq),
                          (mixed_h, mixed), (first_h, first), (tok_h, tok), (hg_h, hg))
     ]
@@ -826,6 +830,7 @@
         full[m, c, t] = attn[m]
     greet(everyone(n_f))
     g3[0].s0()
+    l_gi.wait()
     collect_g.start()
 
     def product(red, m, source, weight):
@@ -1081,10 +1086,10 @@
             )
         ]
         + [
-            (shaped(row_shape, F32), vm()), (shaped((micro, 2, half, D), BF), vm()),
-            (shaped((8, D), F32), vm()), (shaped((D, 3 * hp), BF), vm()),
+            (shaped(row_shape, F32), hb()), (shaped((micro, 2, half, D), BF), vm()),
+            (shaped((8, D), F32), vm()), (shaped((D, 3 * hp), BF), hb()),
         ],
-        [sm(), sm()] + [vm()] * 8,
+        [sm(), sm(), vm(), hb()] + [vm()] * 6,
         [V(own_shape, BF), V(own_shape, BF), V(row_shape, F32)]
         + [V(a, BF) for a in w_shapes]
         + [V(head_shape, BF)] * 4
@@ -1092,11 +1097,12 @@
         + [
             V(send, BF), V(send, BF), V((n_f, 8, D), F32), V((n_c, 8, D), F32),
             V(full_shape, BF), V(full_shape, BF), V(full_shape, BF),
-            V((micro, n_c, span, 2 * hp), BF),
+            V((micro, n_c, span, 2 * hp), BF), V(row_shape, F32), V((D, 3 * hp), BF),
+            V((micro, seqs, piece, D), BF),
         ]
         + reduce_scratch(half)
         + [V((128, rows), BF), V((2, rows, 128), F32)],
-        6 * n_f + 160, 16, 0, 10**10,
+        6 * n_f + 160, 20, 0, 10**10,
     )(order, lengths, tokens[:, :, 0], cotangent[:, :, 0], gains_row, p_qkv, p_out, p_in, p_down,
       small)
 
@@ -1107,11 +1113,11 @@
             (shaped((8, D), F32), vm()), (shaped((n_c, wr, 3 * hp), BF), vm()),
             (shaped((n_c, wr, n_q + heads), BF), vm()),
         ],
-        [sm(), sm(), vm()] + [hb()] * 14 + [vm()] * 4,
+        [sm(), sm(), vm()] + [hb()] * 14 + [vm(), vm(), hb(), vm()],
         [V(w_shapes[1], BF), V(w_shapes[0], BF), V(w_shapes[3], BF), V(act_shape, BF)]
         + [V(head_shape, BF)] * 4
         + [V(wide_shape, F32), V(stat_shape, F32), V(row_shape, F32), V(row_shape, F32),
-           V(own_shape, BF), V((2, rows, 128), F32)]
+           V(own_shape, BF), V((2, rows, 128), F32), V((n_f, wb, 3 * hp), BF)]
         + [
             V(full_shape, BF), V(full_shape, BF), V((rows, 128), F32), V((rows, 128), F32),
             V((128, rows), F32), V((rows, 128), BF), V((8, rows), F32), V((128, rows), BF),

time: 250 us -> 249 us (level)
  no operation moved by 1% of the time
where the time goes in v5:
time: 249 us; the launch traced here: 248 us
  Pallas kernels  229 us (92%)
  local copies, waits for them, and re-layouts  11.2 us (4%)
  other arithmetic  6.61 us (3%)
    pallas_call x1, Pallas kernels, per_device(): comm_call(functools.partial(front_kernel, n_f), [(shaped((8, D), F32), vm...  136 us
    pallas_call x1, Pallas kernels, per_device(): comm_call(functools.partial(third_kernel, n_f), [(shaped((micro, n_f, pie...  93 us

profile of v5, /device:TPU:0, one launch (start us, length us, event | category | flops | bytes accessed | tf_op | source)
XLA Modules:
  0.0 248.0 jit_solution(4924917745755030971)
XLA Ops:
  0.6 0.0 copy-start
  0.6 0.0 copy-start.4
  0.7 0.7 maximum_convert_fusion
  1.5 1.3 select_reduce_fusion.order
  2.8 0.2 dynamic_update_slice.3.gains
  3.0 0.0 copy-start.5
  3.1 0.2 multiply_sine_fusion
  3.3 0.0 copy-done
  3.3 0.6 bitcast_bitcast_fusion.2.po
  3.9 0.0 copy-start.6
  3.9 1.0 reshape.98
  5.0 0.2 copy.65
  5.1 0.8 reshape.99.pq
  6.0 0.9 pad.9
  6.9 0.7 copy.66
  7.6 0.0 copy-done.4
  7.6 0.3 pad.8
  7.9 0.3 copy.64
  8.2 1.0 reshape.102.p2
  9.2 0.0 copy-done.5
  9.2 0.0 copy-done.6
  9.2 136.3 %shard_map.161 = (f32[8,1024]{1,0:T(8,128)}, bf16[2,2,64,1024]{3,2,1,0:T(8,128)(2,1)}, f32[2,128,1024]{2,1,0:T(8,128)}, bf16[4,4,64,384]{3,2,1,0:T(8,128)(2,1)},...) custom-call(s32[2,4]{1,0:T(2,128)} %select_reduce_fusion.order, ...), custom_call_target="tpu_custom_call" | custom-call | flops 10000000000 | bytes 1048576 | tf_op jit(solution)/shard_map/pallas_call | solution.py:1076
  145.6 93.0 %shard_map.162 = (bf16[2,4,64,1024]{3,2,1,0:T(8,128)(2,1)}, bf16[2,4,64,1024]{3,2,1,0:T(8,128)(2,1)}, f32[8,1024]{1,0:T(8,128)}, bf16[4,64,1152]{2,1,0:T(8,128)(2,1)}, bf16[4,64,512]{2,1,0:T(8,128)(2,1)}) custom-call(s32[2,4]{1,0:T(2,128)} %owners.1, s32[2,4]{1,0:T(2,128)} %lengths.3, bf16[2,2,64,1024]{3,2,1,0:T(8,128)(2,1)} %get-tuple-element.31.attn, ...), custom_call_target="tpu_custom_call" | custom-call | flops 10000000000 | bytes 1048576 | tf_op jit(solution)/shard_map/pallas_call | solution.py:1109
  238.6 0.0 copy-start.3
  238.6 0.8 constant_dynamic-slice_fusion
  239.4 0.5 slice_bitcast_fusion.1
  239.9 1.5 copy_bitcast_fusion.1
  241.4 1.0 slice_convert_fusion.1
  242.4 0.2 reshape.120
  242.6 0.3 copy.47
  242.8 0.9 reshape.114
  243.7 0.0 copy-done.3
  243.7 0.0 copy-start.2
  243.8 0.1 reshape.110
  243.9 0.0 copy-start.1
  243.9 0.3 copy.57
  244.2 0.8 slice_convert_fusion.2
  245.0 1.1 slice_convert_fusion
  246.1 0.0 copy-done.2
  246.1 1.0 copy.74
  247.1 0.0 copy-done.1
  247.1 1.0 copy.75
  (14 shorter events, 0.1 us)
Async XLA Ops:
  0.6 2.6 %copy-start = (bf16[512,64]{0,1:T(8,128)(2,1)S(1)}, bf16[512,64]{0,1:T(8,128)(2,1)}, u32[]{:S(2)}) copy-start(bf16[512,64]{0,1:T(8,128)(2,1)} %param.17) | copy-start | bytes 196612
  0.6 7.0 %copy-start.4 = (bf16[64,2,1312]{2,1,0:T(2,128)(2,1)S(1)}, bf16[64,2,1312]{2,1,0:T(2,128)(2,1)}, u32[]{:S(2)}) copy-start(bf16[64,2,1312]{2,1,0:T(2,128)(2,1)} %param.18) | copy-start | bytes 1007620
  3.0 6.2 %copy-start.5 = (f32[8,1024]{1,0:T(8,128)}, f32[8,1024]{1,0:T(8,128)S(1)}, u32[]{:S(2)}) copy-start(f32[8,1024]{1,0:T(8,128)S(1)} %dynamic_update_slice.3.gains) | copy-start | bytes 98308
  3.9 5.3 %copy-start.6 = (f32[5,32,128]{2,1,0:T(8,128)}, f32[5,32,128]{2,1,0:T(8,128)S(1)}, u32[]{:S(2)}) copy-start(f32[5,32,128]{2,1,0:T(8,128)S(1)} %constant_dynamic-update-slice_fusion.small) | copy-start | bytes 245764
  238.6 5.1 %copy-start.3 = (bf16[4,64,1152]{2,1,0:T(8,128)(2,1)S(1)}, bf16[4,64,1152]{2,1,0:T(8,128)(2,1)}, u32[]{:S(2)}) copy-start(bf16[4,64,1152]{2,1,0:T(8,128)(2,1)} %get-tuple-element.53) | copy-start | bytes 1769476
  243.7 2.3 copy-start.2
  243.9 3.2 %copy-start.1 = (bf16[2,4,64,1024]{3,2,1,0:T(8,128)(2,1)S(1)}, bf16[2,4,64,1024]{3,2,1,0:T(8,128)(2,1)}, u32[]{:S(2)}) copy-start(bf16[2,4,64,1024]{3,2,1,0:T(8,128)(2,1)} %get-tuple-element.50) | copy-start | bytes 3145732
